TPU v7x, 32 devices: a whole 2x2x4 slice. The times are simulated.
32 devices in a mesh: fsdp: 4 (over y, x), dp: 8 (over z, core).
Axes of the slice: x: 2, y: 2, z: 4, core: 2. Of those that a mesh axis runs over, the one named last changes fastest.
Arguments:
- tokens: bfloat16 [32, 256, 2048], P(('fsdp', 'dp')), may hold values from -6 to 6
- lengths: int32 [32], P(('fsdp', 'dp')), may hold values from 1 to 256, 5734 in all
- dealing: int32 [32], replicated, may hold values from 0 to 31, as said below
- cotangent: bfloat16 [32, 256, 2048], P(('fsdp', 'dp')), may hold values from -6 to 6
- query_weight: bfloat16 [2048, 2048], P(('fsdp', 'dp')), may hold values from -0.125 to 0.125
- key_weight: bfloat16 [2048, 2048], P(('fsdp', 'dp')), may hold values from -0.125 to 0.125
- value_weight: bfloat16 [2048, 4096], P(('fsdp', 'dp')), may hold values from -0.125 to 0.125
- gate_weight: bfloat16 [2048, 4096], P(('fsdp', 'dp')), may hold values from -0.125 to 0.125
- mixer_gain: bfloat16 [2048], P(('fsdp', 'dp')), may hold values from 0.25 to 1.75
- mixer_bias: bfloat16 [2048], P(('fsdp', 'dp')), may hold values from -1.796875 to 1.796875
- output_weight: bfloat16 [4096, 2048], P(('fsdp', 'dp')), may hold values from -0.1875 to 0.1875
- feed_gate: bfloat16 [2048, 4096], P(('fsdp', 'dp')), may hold values from -0.125 to 0.125
- feed_up: bfloat16 [2048, 4096], P(('fsdp', 'dp')), may hold values from -0.125 to 0.125
- feed_down: bfloat16 [4096, 2048], P(('fsdp', 'dp')), may hold values from -0.1875 to 0.1875
- feed_gain: bfloat16 [2048], P(('fsdp', 'dp')), may hold values from 0.25 to 1.75
- feed_bias: bfloat16 [2048], P(('fsdp', 'dp')), may hold values from -1.796875 to 1.796875
Outputs:
- out_tokens: bfloat16 [32, 256, 2048], P(('fsdp', 'dp'))
- input_grad: bfloat16 [32, 256, 2048], P(('fsdp', 'dp'))
- query_weight_grad: float32 [2048, 2048], P(('fsdp', 'dp'))
- key_weight_grad: float32 [2048, 2048], P(('fsdp', 'dp'))
- value_weight_grad: float32 [2048, 4096], P(('fsdp', 'dp'))
- gate_weight_grad: float32 [2048, 4096], P(('fsdp', 'dp'))
- mixer_gain_grad: float32 [2048], P(('fsdp', 'dp'))
- mixer_bias_grad: float32 [2048], P(('fsdp', 'dp'))
- output_weight_grad: float32 [4096, 2048], P(('fsdp', 'dp'))
- feed_gate_grad: float32 [2048, 4096], P(('fsdp', 'dp'))
- feed_up_grad: float32 [2048, 4096], P(('fsdp', 'dp'))
- feed_down_grad: float32 [4096, 2048], P(('fsdp', 'dp'))
- feed_gain_grad: float32 [2048], P(('fsdp', 'dp'))
- feed_bias_grad: float32 [2048], P(('fsdp', 'dp'))
Inputs may be any that keep to these rules, and one draw needn't show every extreme that they name: dealing is a permutation of the 32 sequences; sequence s and slot dealing[s] lie on devices with the same index of dp.
All inputs are finite; a program needn't handle non-finite values. No bound on the sum of `lengths` on one device may be relied on, other than what follows from the above.
Results may differ from a plain program's by a relative error of at most 0.015.
Values may be sent and summed in bfloat16 or wider, within the bound.
No kernel may reach another device: no remote copies, remote signals or barrier semaphores. Data moves between devices by JAX's collectives and lax.ppermute only.
A program may use at most 448 MiB of HBM per device.

v0:
```python
import math

import jax
import jax.numpy as jnp
from jax import lax
from jax.sharding import PartitionSpec as P

HEADS = 8
KEY = 256
VAL = 512


EPSILON = 1e-05
RETAIN_EPSILON = 0.05


def normalize_rows(field_in, offset=EPSILON):
    centre = jnp.mean(field_in, axis=-1, keepdims=True)
    centred = field_in - centre
    spread = jnp.mean(centred * centred, axis=-1, keepdims=True)
    return centred * lax.rsqrt(spread + offset)


def rotate(field_in, direction):
    length = field_in.shape[-3]
    breadth = field_in.shape[-1]
    half_width = breadth // 2
    columns = jnp.arange(half_width).astype(jnp.float32)
    angles = jnp.exp(-math.log(10000.0) * columns / (half_width - 1))
    zeta_scale = (2.0 * columns + 0.4 * breadth) / (1.4 * breadth)
    places = jnp.arange(length).astype(jnp.float32)[:, None]
    phases = places * angles[None, :]
    growth = jnp.exp(direction * places / 512.0 * jnp.log(zeta_scale)[None, :])
    cosine = (jnp.cos(phases) * growth)[:, None, :]
    sine_part = (jnp.sin(phases) * growth)[:, None, :]
    first_half = field_in[..., :half_width]
    second = field_in[..., half_width:]
    return jnp.concatenate(
        [first_half * cosine - second * sine_part, second * cosine + first_half * sine_part],
        axis=-1,
    )


def decay_mask(length, heads_count):
    log_decay = jnp.log(1.0 - jnp.exp2(-5.0 - jnp.arange(heads_count).astype(jnp.float32)))
    places = jnp.arange(length)
    distance = (places[:, None] - places[None, :]).astype(jnp.float32)
    decayed = jnp.where(
        distance[None] >= 0.0,
        jnp.exp(log_decay[:, None, None] * jnp.maximum(distance, 0.0)[None]),
        0.0,
    )
    return decayed * lax.rsqrt(jnp.sum(decayed, axis=-1, keepdims=True))


def shape_scores(raw_scores, decay):
    weighted = raw_scores * decay
    row_total = jnp.sum(weighted * weighted, axis=-1, keepdims=True)
    return weighted * lax.rsqrt(1.0 + row_total)


def gate_mix(retained, gate_proj):
    per_head = normalize_rows(retained.reshape(retained.shape[0], HEADS, -1), RETAIN_EPSILON)
    return jax.nn.silu(gate_proj) * per_head.reshape(retained.shape)


def times_rows(left_rows, right_rows):
    return lax.dot_general(
        left_rows, right_rows, (((0,), (0,)), ((), ())), preferred_element_type=jnp.float32
    )


def times_back(left_rows, right_rows):
    return lax.dot_general(
        left_rows, right_rows, (((1,), (1,)), ((), ())), preferred_element_type=jnp.float32
    )


def fetch_mixer(
    query_weight, key_weight, value_weight, gate_weight, mixer_gain, mixer_bias, step_fn, initial
):
    whole_set = (
        lax.all_gather(query_weight, ("fsdp", "dp"), axis=0, tiled=True),
        lax.all_gather(key_weight, ("fsdp", "dp"), axis=0, tiled=True),
        lax.all_gather(value_weight, ("fsdp", "dp"), axis=0, tiled=True),
        lax.all_gather(gate_weight, ("fsdp", "dp"), axis=0, tiled=True),
        lax.all_gather(mixer_gain, ("fsdp", "dp"), axis=0, tiled=True),
        lax.all_gather(mixer_bias, ("fsdp", "dp"), axis=0, tiled=True),
    )
    return step_fn(initial, whole_set, 0)


def fetch_output(output_weight, step_fn, initial):
    whole_set = lax.all_gather(output_weight, ("fsdp", "dp"), axis=0, tiled=True)
    return step_fn(initial, whole_set, 0)


def fetch_feed(feed_gate, feed_up, feed_gain, feed_bias, step_fn, initial):
    whole_set = (
        lax.all_gather(feed_gate, ("fsdp", "dp"), axis=0, tiled=True),
        lax.all_gather(feed_up, ("fsdp", "dp"), axis=0, tiled=True),
        lax.all_gather(feed_gain, ("fsdp", "dp"), axis=0, tiled=True),
        lax.all_gather(feed_bias, ("fsdp", "dp"), axis=0, tiled=True),
    )
    return step_fn(initial, whole_set, 0)


def fetch_down(feed_down, step_fn, initial):
    whole_set = lax.all_gather(feed_down, ("fsdp", "dp"), axis=0, tiled=True)
    return step_fn(initial, whole_set, 0)


def sum_model_rows(term_fn, local_rows):
    return lax.psum_scatter(
        term_fn(jnp.int32(0), lax.axis_size(("fsdp", "dp")) * local_rows),
        ("fsdp", "dp"),
        scatter_dimension=0,
        tiled=True,
    )


def sum_hidden_rows(term_fn, local_rows):
    return lax.psum_scatter(
        term_fn(jnp.int32(0), lax.axis_size(("fsdp", "dp")) * local_rows),
        ("fsdp", "dp"),
        scatter_dimension=0,
        tiled=True,
    )


def body(
    tokens,
    lengths,
    dealing,
    cotangent,
    query_weight,
    key_weight,
    value_weight,
    gate_weight,
    mixer_gain,
    mixer_bias,
    output_weight,
    feed_gate,
    feed_up,
    feed_down,
    feed_gain,
    feed_bias,
):
    seq_count, length, breadth = tokens.shape
    rows_count = seq_count * length
    value_width = value_weight.shape[1]
    hidden_width = feed_gate.shape[1]
    local_model = query_weight.shape[0]
    local_hidden = output_weight.shape[0]
    scale_factor = KEY ** (-0.5)
    group_devices = lax.axis_size("dp")
    block_span = group_devices * seq_count
    dp_index = lax.axis_index("dp")
    own_ids = (lax.axis_index("fsdp") * group_devices + dp_index) * seq_count + jnp.arange(
        seq_count, dtype=jnp.int32
    )
    targets = jnp.take(dealing, own_ids)
    target_rank = targets // block_span * seq_count + targets % seq_count
    piece = lax.all_gather(tokens, "fsdp", axis=0, tiled=True)
    group_ranks = jnp.arange(piece.shape[0], dtype=jnp.int32)
    matches = (target_rank[:, None] == group_ranks[None, :]).astype(jnp.bfloat16)
    arrived = jnp.einsum("jr,rld->jld", matches, piece, preferred_element_type=jnp.float32)
    residual_in = arrived.reshape(rows_count, breadth)
    places = jnp.arange(length, dtype=jnp.int32)
    live_mask = (places[None, :] < lengths[:, None]).astype(jnp.float32).reshape(rows_count, 1)
    upstream = cotangent.reshape(rows_count, breadth).astype(jnp.float32) * live_mask
    mixer_hat, mixer_pull = jax.vjp(normalize_rows, residual_in)
    zero_model = jnp.zeros((rows_count, breadth), jnp.float32)
    zero_value = jnp.zeros((rows_count, value_width), jnp.float32)
    zero_hidden = jnp.zeros((rows_count, hidden_width), jnp.float32)
    zero_feature = jnp.zeros((breadth,), jnp.float32)

    def mixer_forward(running, pieces, first_row):
        piece_query, piece_key, piece_value, piece_gate, piece_gain, piece_bias = pieces
        normed = (
            mixer_hat * piece_gain.astype(jnp.float32) + piece_bias.astype(jnp.float32)
        ).astype(jnp.bfloat16)
        queries = jnp.dot(normed, piece_query, preferred_element_type=jnp.float32)
        key_proj = jnp.dot(normed, piece_key, preferred_element_type=jnp.float32)
        value_proj = jnp.dot(normed, piece_value, preferred_element_type=jnp.float32)
        gate_proj = jnp.dot(normed, piece_gate, preferred_element_type=jnp.float32)
        return (queries, key_proj, value_proj, gate_proj, normed)

    queries, key_proj, value_proj, gate_proj, mixer_normed = fetch_mixer(
        query_weight,
        key_weight,
        value_weight,
        gate_weight,
        mixer_gain,
        mixer_bias,
        mixer_forward,
        (
            zero_model,
            zero_model,
            zero_value,
            zero_value,
            jnp.zeros((rows_count, breadth), jnp.bfloat16),
        ),
    )
    query_rot, query_pull = jax.vjp(
        lambda field_in: rotate(field_in, 1.0), queries.reshape(seq_count, length, HEADS, KEY)
    )
    key_rot, key_pull = jax.vjp(
        lambda field_in: rotate(field_in, -1.0), key_proj.reshape(seq_count, length, HEADS, KEY)
    )
    query_low = query_rot.astype(jnp.bfloat16)
    key_low = key_rot.astype(jnp.bfloat16)
    value_low = value_proj.astype(jnp.bfloat16).reshape(seq_count, length, HEADS, VAL)
    decay = decay_mask(length, HEADS)
    raw_scores = (
        jnp.einsum("nlhk,nmhk->nhlm", query_low, key_low, preferred_element_type=jnp.float32)
        * scale_factor
    )
    shaped, shape_pull = jax.vjp(lambda scores_in: shape_scores(scores_in, decay), raw_scores)
    shaped_low = shaped.astype(jnp.bfloat16)
    retained = jnp.einsum(
        "nhlm,nmhv->nlhv", shaped_low, value_low, preferred_element_type=jnp.float32
    ).reshape(rows_count, value_width)
    gated_full, gate_pull = jax.vjp(gate_mix, retained, gate_proj)
    gated_low = gated_full.astype(jnp.bfloat16)

    def output_forward(running, shard_rows, first_row):
        return jnp.dot(gated_low, shard_rows, preferred_element_type=jnp.float32)

    mixer_out = fetch_output(output_weight, output_forward, zero_model)
    hidden_state = residual_in + mixer_out
    feed_hat, feed_pull = jax.vjp(normalize_rows, hidden_state)

    def feed_forward(running, pieces, first_row):
        piece_gate, piece_up, piece_gain, piece_bias = pieces
        normed = (
            feed_hat * piece_gain.astype(jnp.float32) + piece_bias.astype(jnp.float32)
        ).astype(jnp.bfloat16)
        gate_pre = jnp.dot(normed, piece_gate, preferred_element_type=jnp.float32)
        up_pre = jnp.dot(normed, piece_up, preferred_element_type=jnp.float32)
        return (gate_pre, up_pre, normed)

    gate_pre, up_pre, feed_normed = fetch_feed(
        feed_gate,
        feed_up,
        feed_gain,
        feed_bias,
        feed_forward,
        (zero_hidden, zero_hidden, jnp.zeros((rows_count, breadth), jnp.bfloat16)),
    )
    activated_full, act_pull = jax.vjp(
        lambda gate_in, up_in: jax.nn.gelu(gate_in, approximate=False) * up_in, gate_pre, up_pre
    )
    activated = activated_full.astype(jnp.bfloat16)

    def down_forward(running, shard_rows, first_row):
        return jnp.dot(activated, shard_rows, preferred_element_type=jnp.float32)

    feed_out = fetch_down(feed_down, down_forward, zero_model)
    out_tokens = (
        (live_mask * (hidden_state + feed_out))
        .astype(jnp.bfloat16)
        .reshape(seq_count, length, breadth)
    )
    down_low = upstream.astype(jnp.bfloat16)

    def down_backward(running, shard_rows, first_row):
        return times_back(down_low, shard_rows)

    act_grad = fetch_down(feed_down, down_backward, zero_hidden)
    gate_pre_grad, up_pre_grad = act_pull(act_grad)
    gate_pre_low = gate_pre_grad.astype(jnp.bfloat16)
    up_pre_low = up_pre_grad.astype(jnp.bfloat16)

    def feed_backward(running, pieces, first_row):
        piece_gate, piece_up, piece_gain, piece_bias = pieces
        normed_grad = times_back(gate_pre_low, piece_gate) + times_back(up_pre_low, piece_up)
        hat_grad = normed_grad * piece_gain.astype(jnp.float32)
        gain_part = jnp.sum(normed_grad * feed_hat, axis=0)
        bias_part = jnp.sum(normed_grad, axis=0)
        return (hat_grad, gain_part, bias_part)

    feed_hat_grad, feed_gain_part, feed_bias_part = fetch_feed(
        feed_gate,
        feed_up,
        feed_gain,
        feed_bias,
        feed_backward,
        (zero_model, zero_feature, zero_feature),
    )
    state_grad = upstream + feed_pull(feed_hat_grad)[0]
    out_grad_low = state_grad.astype(jnp.bfloat16)

    def output_backward(running, shard_rows, first_row):
        return times_back(out_grad_low, shard_rows)

    gated_grad = fetch_output(output_weight, output_backward, zero_value)
    retained_grad, gate_proj_grad = gate_pull(gated_grad)
    retained_low = retained_grad.astype(jnp.bfloat16).reshape(seq_count, length, HEADS, VAL)
    gate_grad_low = gate_proj_grad.astype(jnp.bfloat16)
    value_grad = jnp.einsum(
        "nhlm,nlhv->nmhv", shaped_low, retained_low, preferred_element_type=jnp.float32
    )
    value_grad_low = value_grad.reshape(rows_count, value_width).astype(jnp.bfloat16)
    shaped_grad = jnp.einsum(
        "nlhv,nmhv->nhlm", retained_low, value_low, preferred_element_type=jnp.float32
    )
    score_grad = shape_pull(shaped_grad)[0].astype(jnp.bfloat16)
    query_rot_grad = (
        jnp.einsum("nhlm,nmhk->nlhk", score_grad, key_low, preferred_element_type=jnp.float32)
        * scale_factor
    )
    key_rot_grad = (
        jnp.einsum("nhlm,nlhk->nmhk", score_grad, query_low, preferred_element_type=jnp.float32)
        * scale_factor
    )
    query_grad_low = query_pull(query_rot_grad)[0].reshape(rows_count, breadth).astype(jnp.bfloat16)
    key_grad_low = key_pull(key_rot_grad)[0].reshape(rows_count, breadth).astype(jnp.bfloat16)

    def mixer_backward(running, pieces, first_row):
        piece_query, piece_key, piece_value, piece_gate, piece_gain, piece_bias = pieces
        normed_grad = (
            times_back(query_grad_low, piece_query)
            + times_back(key_grad_low, piece_key)
            + times_back(value_grad_low, piece_value)
            + times_back(gate_grad_low, piece_gate)
        )
        hat_grad = normed_grad * piece_gain.astype(jnp.float32)
        gain_part = jnp.sum(normed_grad * mixer_hat, axis=0)
        bias_part = jnp.sum(normed_grad, axis=0)
        return (hat_grad, gain_part, bias_part)

    mixer_hat_grad, mixer_gain_part, mixer_bias_part = fetch_mixer(
        query_weight,
        key_weight,
        value_weight,
        gate_weight,
        mixer_gain,
        mixer_bias,
        mixer_backward,
        (zero_model, zero_feature, zero_feature),
    )
    grad_sequences = (
        (state_grad + mixer_pull(mixer_hat_grad)[0])
        .astype(jnp.bfloat16)
        .reshape(seq_count, length, breadth)
    )
    piece = lax.all_gather(grad_sequences, "fsdp", axis=0, tiled=True)
    group_ranks = jnp.arange(piece.shape[0], dtype=jnp.int32)
    sources = group_ranks // seq_count * block_span + dp_index * seq_count + group_ranks % seq_count
    destinations = jnp.take(dealing, sources)
    matches = (own_ids[:, None] == destinations[None, :]).astype(jnp.bfloat16)
    input_grad = jnp.einsum(
        "jr,rld->jld", matches, piece, preferred_element_type=jnp.float32
    ).astype(jnp.bfloat16)
    mixer_gain_grad, mixer_bias_grad, feed_gain_grad, feed_bias_grad = (
        lax.psum_scatter(mixer_gain_part, ("fsdp", "dp"), scatter_dimension=0, tiled=True),
        lax.psum_scatter(mixer_bias_part, ("fsdp", "dp"), scatter_dimension=0, tiled=True),
        lax.psum_scatter(feed_gain_part, ("fsdp", "dp"), scatter_dimension=0, tiled=True),
        lax.psum_scatter(feed_bias_part, ("fsdp", "dp"), scatter_dimension=0, tiled=True),
    )

    def model_terms(first_row, span_rows):
        return jnp.concatenate(
            [
                jnp.concatenate(
                    [
                        times_rows(mixer_normed, query_grad_low),
                        times_rows(mixer_normed, key_grad_low),
                        times_rows(mixer_normed, value_grad_low),
                        times_rows(mixer_normed, gate_grad_low),
                    ],
                    axis=1,
                ),
                times_rows(feed_normed, gate_pre_low),
                times_rows(feed_normed, up_pre_low),
            ],
            axis=1,
        )

    def hidden_terms(first_row, span_rows):
        return jnp.concatenate(
            [times_rows(gated_low, out_grad_low), times_rows(activated, down_low)], axis=1
        )

    model_grads = sum_model_rows(model_terms, local_model)
    hidden_grads = sum_hidden_rows(hidden_terms, local_hidden)
    split_point = 2 * breadth + 2 * value_width
    mixer_grads = model_grads[:, :split_point]
    feed_grads = model_grads[:, split_point:]
    output_grad = hidden_grads[:, :breadth]
    down_grad = hidden_grads[:, breadth:]
    query_weight_grad = mixer_grads[:, :breadth]
    key_weight_grad = mixer_grads[:, breadth : 2 * breadth]
    value_weight_grad = mixer_grads[:, 2 * breadth : 2 * breadth + value_width]
    gate_weight_grad = mixer_grads[:, 2 * breadth + value_width :]
    feed_gate_grad = feed_grads[:, :hidden_width]
    feed_up_grad = feed_grads[:, hidden_width:]
    return (
        out_tokens,
        input_grad,
        query_weight_grad,
        key_weight_grad,
        value_weight_grad,
        gate_weight_grad,
        mixer_gain_grad,
        mixer_bias_grad,
        output_grad,
        feed_gate_grad,
        feed_up_grad,
        down_grad,
        feed_gain_grad,
        feed_bias_grad,
    )


def solution(mesh):
    in_specs = (
        P(("fsdp", "dp"), None, None),
        P(("fsdp", "dp")),
        P(),
        P(("fsdp", "dp"), None, None),
        P(("fsdp", "dp"), None),
        P(("fsdp", "dp"), None),
        P(("fsdp", "dp"), None),
        P(("fsdp", "dp"), None),
        P(("fsdp", "dp")),
        P(("fsdp", "dp")),
        P(("fsdp", "dp"), None),
        P(("fsdp", "dp"), None),
        P(("fsdp", "dp"), None),
        P(("fsdp", "dp"), None),
        P(("fsdp", "dp")),
        P(("fsdp", "dp")),
    )
    out_specs = (
        P(("fsdp", "dp"), None, None),
        P(("fsdp", "dp"), None, None),
        P(("fsdp", "dp"), None),
        P(("fsdp", "dp"), None),
        P(("fsdp", "dp"), None),
        P(("fsdp", "dp"), None),
        P(("fsdp", "dp")),
        P(("fsdp", "dp")),
        P(("fsdp", "dp"), None),
        P(("fsdp", "dp"), None),
        P(("fsdp", "dp"), None),
        P(("fsdp", "dp"), None),
        P(("fsdp", "dp")),
        P(("fsdp", "dp")),
    )
    return jax.shard_map(body, mesh=mesh, in_specs=in_specs, out_specs=out_specs, check_vma=False)
```

profile of v0, /device:TPU:0, one launch (start us, length us, event | category | flops | bytes accessed | tf_op | source)
XLA Modules:
  0.0 3635.5 jit_solution(9217731905129564449)
XLA Ops:
  16.4 43.6 %all-reduce.13 = (bf16[2048]{0:T(1024)(128)(2,1)S(1)}, bf16[2048]{0:T(1024)(128)(2,1)S(1)}, bf16[2048]{0:T(1024)(128)(2,1)S(1)}, bf16[2048]{0:T(1024)(128)(2,1)S(1)}) all-reduce(bf16[2048]{0:T(1024)(128)(2,1)S(1)} %dynamic-update-slice.2, bf16[2048]{0:T(1024)(128)(2,1)S(1)} %dynamic-update-slice.1, ...), channel_id=1, replica_groups=mesh['fsdp'=4,'dp'=8] {'fsdp','dp'}, use_global_device_ids=true, to_apply=%add.5 | all-reduce | flops 8192 | bytes 32768
  66.4 5.5 fusion.15
  75.3 71.3 %all-gather.20.cloned.1.call-done = bf16[2048,2048]{1,0:T(8,128)(2,1)} async-done(((bf16[64,2048]{1,0:T(8,128)(2,1)}), bf16[2048,2048]{1,0:T(8,128)(2,1)}) %all-gather.20.cloned.1.call-update) | async-done | bytes 8388624 | tf_op jit(solution)/shard_map/all_gather | solution.py:84
  146.5 5.7 fusion.84
  154.4 70.8 %all-gather.18.cloned.1.call-done = bf16[2048,2048]{1,0:T(8,128)(2,1)} async-done(((bf16[64,2048]{1,0:T(8,128)(2,1)}), bf16[2048,2048]{1,0:T(8,128)(2,1)}) %all-gather.18.cloned.1.call-update) | async-done | bytes 8388624 | tf_op jit(solution)/shard_map/all_gather | solution.py:83
  225.3 5.7 fusion.83
  236.6 104.5 %all-gather.16.cloned.1.call-done = bf16[2048,4096]{1,0:T(8,128)(2,1)} async-done(((bf16[64,4096]{1,0:T(8,128)(2,1)}), bf16[2048,4096]{1,0:T(8,128)(2,1)}) %all-gather.16.cloned.1.call-update) | async-done | bytes 16777232 | tf_op jit(solution)/shard_map/all_gather | solution.py:85
  341.2 8.5 convolution_convert_fusion
  354.3 5.7 copy.131
  360.0 5.6 copy.129
  367.9 5.7 copy.130
  373.6 83.0 %all-gather.14.cloned.1.call-done = bf16[2048,4096]{1,0:T(8,128)(2,1)} async-done(((bf16[64,4096]{1,0:T(8,128)(2,1)}), bf16[2048,4096]{1,0:T(8,128)(2,1)}) %all-gather.14.cloned.1.call-update) | async-done | bytes 16777232 | tf_op jit(solution)/shard_map/all_gather | solution.py:86
  456.6 16.8 multiply_convert_fusion.2
  473.5 98.7 %all-gather.22.cloned.1.call-done = bf16[4096,2048]{1,0:T(8,128)(2,1)} async-done(((bf16[128,2048]{1,0:T(8,128)(2,1)}), bf16[4096,2048]{1,0:T(8,128)(2,1)}) %all-gather.22.cloned.1.call-update) | async-done | bytes 16777232 | tf_op jit(solution)/shard_map/all_gather | solution.py:94
  572.1 9.4 fusion.82
  583.3 104.5 %all-gather.24.cloned.1.call-done = bf16[2048,4096]{1,0:T(8,128)(2,1)} async-done(((bf16[64,4096]{1,0:T(8,128)(2,1)}), bf16[2048,4096]{1,0:T(8,128)(2,1)}) %all-gather.24.cloned.1.call-update) | async-done | bytes 16777232 | tf_op jit(solution)/shard_map/all_gather | solution.py:100
  687.8 10.1 fusion.85
  697.9 105.6 %all-gather.28.cloned.1.call-done = bf16[4096,2048]{1,0:T(8,128)(2,1)} async-done(((bf16[128,2048]{1,0:T(8,128)(2,1)}), bf16[4096,2048]{1,0:T(8,128)(2,1)}) %all-gather.28.cloned.1.call-update) | async-done | bytes 16777232 | tf_op jit(solution)/shard_map/all_gather | solution.py:109
  803.4 19.8 multiply_convert_fusion
  823.2 95.8 %all-gather.26.cloned.1.call-done = bf16[2048,4096]{1,0:T(8,128)(2,1)} async-done(((bf16[64,4096]{1,0:T(8,128)(2,1)}), bf16[2048,4096]{1,0:T(8,128)(2,1)}) %all-gather.26.cloned.1.call-update) | async-done | bytes 16777232 | tf_op jit(solution)/shard_map/all_gather | solution.py:101
  919.1 17.2 add_convert_fusion
  936.3 12.3 fusion.86
  948.5 14.6 multiply_reduce_fusion.2
  967.8 13.3 fusion.6
  981.1 5.6 copy.133
  986.7 4.2 multiply_reduce_fusion
  994.0 5.8 copy.142
  1002.1 5.6 copy.132
  1007.7 10.6 fusion.2
  1041.4 6.2 fusion.87
  1047.6 7.1 convolution_add_fusion.2
  1054.7 12.8 convolution_add_fusion.1
  1067.6 14.3 multiply_reduce_fusion.3
  1086.2 15.7 fusion.88
  1101.9 13.8 fusion.40
  1115.7 44.1 %pad_maximum_fusion = f32[4096,4096]{0,1:T(8,128)} fusion(f32[4096,2048]{0,1:T(8,128)} %fusion.40, f32[4096,2048]{0,1:T(8,128)} %fusion.88), kind=kLoop, calls=%fused_computation.1 | loop fusion | flops 16777216 | bytes 134217728 | tf_op jit(solution)/shard_map/concatenate | solution.py:382
  1161.3 8.4 convolution_dynamic-update-slice_fusion.5
  1169.7 8.4 convolution_dynamic-update-slice_fusion.4
  1178.1 13.8 convolution_dynamic-update-slice_fusion.3
  1191.8 13.6 convolution_dynamic-update-slice_fusion.2
  1205.5 13.6 convolution_dynamic-update-slice_fusion.1
  1219.1 13.6 convolution_dynamic-update-slice_fusion
  1233.9 41.3 %all-reduce.12 = (f32[2048]{0:T(1024)S(1)}, f32[2048]{0:T(1024)S(1)}, f32[2048]{0:T(1024)S(1)}, f32[2048]{0:T(1024)S(1)}) all-reduce(f32[2048]{0:T(1024)S(1)} %copy-done.71, f32[2048]{0:T(1024)S(1)} %copy-done.72, f32[2048]{0:T(1024)S(1)} %copy-done.69, f32[2048]{0:T(1024)S(1)} %copy-done.70), channel_id=4, replica_groups=mesh['fsdp'=4,'dp'=8] {'fsdp','dp'}, use_global_device_ids=true, to_apply=%region_17.18.clone | all-reduce | flops 8192 | bytes 65536
  1277.6 12.1 fusion.19
  1289.7 5.5 fusion.13
  1296.9 571.8 %reduce-scatter.5.cloned.1.call-done = f32[128,4096]{0,1:T(8,128)} async-done(((f32[4096,4096]{0,1:T(8,128)}), f32[128,4096]{0,1:T(8,128)}) %reduce-scatter.5.cloned.1.call-update) | async-done | bytes 2097168 | tf_op jit(solution)/shard_map/reduce_scatter | solution.py:123
  1872.9 1748.9 %reduce-scatter.3.cloned.1.call-done = f32[64,20480]{1,0:T(8,128)} async-done(((f32[2048,20480]{1,0:T(8,128)}), f32[64,20480]{1,0:T(8,128)}) %reduce-scatter.3.cloned.1.call-update) | async-done | bytes 5242896 | tf_op jit(solution)/shard_map/reduce_scatter | solution.py:114
  3624.1 4.3 fusion.77
  (272 shorter events, 84.1 us)
Async XLA Ops:
  7.2 6.3 copy-start
  7.2 8.2 copy-start.76
  7.2 8.5 copy-start.77
  7.2 8.7 copy-start.78
  7.2 9.0 copy-start.79
  7.2 59.2 %all-gather.12.cloned.1.call-start = ((), (), s32[]{:S(2)}) async-start(), calls=%async_computation.2 | async-start | bytes 5242880 | tf_op jit(solution)/shard_map/all_gather | solution.py:164
  8.0 138.6 %all-gather.20.cloned.1.call-start = ((), (), s32[]{:S(2)}) async-start(), calls=%async_computation.6 | async-start | bytes 8650752 | tf_op jit(solution)/shard_map/all_gather | solution.py:84
  8.7 216.5 %all-gather.18.cloned.1.call-start = ((), (), s32[]{:S(2)}) async-start(), calls=%async_computation.5 | async-start | bytes 8650752 | tf_op jit(solution)/shard_map/all_gather | solution.py:83
  9.4 331.7 %all-gather.16.cloned.1.call-start = ((), (), s32[]{:S(2)}) async-start(), calls=%async_computation.4 | async-start | bytes 17301504 | tf_op jit(solution)/shard_map/all_gather | solution.py:85
  10.0 446.6 %all-gather.14.cloned.1.call-start = ((), (), s32[]{:S(2)}) async-start(), calls=%async_computation.3 | async-start | bytes 17301504 | tf_op jit(solution)/shard_map/all_gather | solution.py:86
  10.6 561.5 %all-gather.22.cloned.1.call-start = ((), (), s32[]{:S(2)}) async-start(), calls=%async_computation.7 | async-start | bytes 17301504 | tf_op jit(solution)/shard_map/all_gather | solution.py:94
  11.2 676.6 %all-gather.24.cloned.1.call-start = ((), (), s32[]{:S(2)}) async-start(), calls=%async_computation.8 | async-start | bytes 17301504 | tf_op jit(solution)/shard_map/all_gather | solution.py:100
  11.9 791.5 %all-gather.28.cloned.1.call-start = ((), (), s32[]{:S(2)}) async-start(), calls=%async_computation.10 | async-start | bytes 17301504 | tf_op jit(solution)/shard_map/all_gather | solution.py:109
  12.7 906.4 %all-gather.26.cloned.1.call-start = ((), (), s32[]{:S(2)}) async-start(), calls=%async_computation.9 | async-start | bytes 17301504 | tf_op jit(solution)/shard_map/all_gather | solution.py:101
  13.4 1276.3 %all-gather.30.cloned.1.call-start = ((), (), s32[]{:S(2)}) async-start(), calls=%async_computation.13 | async-start | bytes 5242880 | tf_op jit(solution)/shard_map/all_gather | solution.py:348
  60.6 13.2 copy-start.53
  64.3 168.6 %copy-start.41 = (f32[256,128]{1,0:T(8,128)}, f32[256,128]{1,0:T(8,128)S(1)}, u32[]{:S(2)}) copy-start(f32[256,128]{1,0:T(8,128)S(1)} %get-tuple-element.118) | copy-start | bytes 393220
  64.3 169.6 %copy-start.37 = (f32[256,128]{1,0:T(8,128)}, f32[256,128]{1,0:T(8,128)S(1)}, u32[]{:S(2)}) copy-start(f32[256,128]{1,0:T(8,128)S(1)} %get-tuple-element.114) | copy-start | bytes 393220
  64.3 169.7 %copy-start.39 = (f32[256,128]{1,0:T(8,128)}, f32[256,128]{1,0:T(8,128)S(1)}, u32[]{:S(2)}) copy-start(f32[256,128]{1,0:T(8,128)S(1)} %get-tuple-element.115) | copy-start | bytes 393220
  66.4 8.0 copy-start.58
  75.3 381.4 %copy-start.7 = (bf16[256,2048]{1,0:T(8,128)(2,1)}, bf16[256,2048]{1,0:T(8,128)(2,1)S(1)}, u32[]{:S(2)}) copy-start(bf16[256,2048]{1,0:T(8,128)(2,1)S(1)} %add_convert_fusion.5) | copy-start | bytes 3145732
  236.6 113.1 %copy-start.59 = (f32[8,256]{1,0:T(8,128)}, f32[8,256]{1,0:T(8,128)S(1)}, u32[]{:S(2)}) copy-start(f32[8,256]{1,0:T(8,128)S(1)} %get-tuple-element.120) | copy-start | bytes 24580
  236.6 113.1 %copy-start.51 = (f32[8,256]{1,0:T(8,128)}, f32[8,256]{1,0:T(8,128)S(1)}, u32[]{:S(2)}) copy-start(f32[8,256]{1,0:T(8,128)S(1)} %add_rsqrt_fusion) | copy-start | bytes 24580
  341.2 8.6 copy-start.5
  572.1 10.7 copy-start.57
  583.3 335.8 %copy-start.14 = (bf16[256,2048]{1,0:T(8,128)(2,1)}, bf16[256,2048]{1,0:T(8,128)(2,1)S(1)}, u32[]{:S(2)}) copy-start(bf16[256,2048]{1,0:T(8,128)(2,1)S(1)} %add_convert_fusion.4) | copy-start | bytes 3145732
  583.3 220.1 %copy-start.63 = (f32[256]{0:T(256)S(1)}, f32[256]{0:T(256)}, u32[]{:S(2)}) copy-start(f32[256]{0:T(256)} %compare_convert_fusion) | copy-start | bytes 3076
  963.1 4.3 copy-start.16
  967.8 13.4 copy-start.23
  986.7 4.6 copy-start.3
  986.7 5.9 copy-start.4
  1022.4 4.1 copy-start.52
  1041.4 6.2 copy-start.20
  1054.7 12.9 copy-start.54
  1054.7 12.9 copy-start.62
  1054.7 12.9 copy-start.68
  1067.6 14.4 copy-start.66
  1086.1 782.5 %reduce-scatter.5.cloned.1.call-start = ((), (), s32[]{:S(2)}) async-start(), calls=%async_computation.12 | async-start | bytes 69206016 | tf_op jit(solution)/shard_map/reduce_scatter | solution.py:123
  1086.2 15.7 copy-start.25
  1159.8 9.9 copy-start.21
  1159.8 2462.0 %reduce-scatter.3.cloned.1.call-start = ((), (), s32[]{:S(2)}) async-start(), calls=%async_computation.11 | async-start | bytes 173015040 | tf_op jit(solution)/shard_map/reduce_scatter | solution.py:114
  1169.7 8.4 copy-start.17
  1178.1 13.8 copy-start.28
  1191.8 13.7 copy-start.15
  1191.8 13.7 copy-start.27
  1205.5 13.6 copy-start.26
  1232.7 45.0 %copy-start.11 = (f32[256,2048]{1,0:T(8,128)S(1)}, f32[256,2048]{1,0:T(8,128)}, u32[]{:S(2)}) copy-start(f32[256,2048]{1,0:T(8,128)} %copy-done.10) | copy-start | bytes 6291460
  1232.7 45.0 %copy-start.64 = (f32[256]{0:T(256)S(1)}, f32[256]{0:T(256)}, u32[]{:S(2)}) copy-start(f32[256]{0:T(256)} %compare_convert_fusion) | copy-start | bytes 3076
  (44 other events, 73.8 us)
Sparse Core Ops, SparseCore 0:
  9.9 56.5 all-gather.11
  69.4 77.0 all-gather.19
  149.5 75.6 all-gather.17
  228.1 112.9 all-gather.15
  344.0 112.5 all-gather.13
  459.5 112.5 all-gather.21
  575.1 112.5 all-gather.23
  690.8 112.5 all-gather.27
  806.4 112.5 all-gather.25
  1086.2 50.7 all-gather.29
  1159.9 708.6 reduce-scatter.4
  1870.9 1750.9 reduce-scatter.2
where the time goes:
time: 3640 us
  waiting for transfers between devices  3060 us (84%)
  matrix products  308 us (8%)
  blocking collectives  84.9 us (2%)
  local copies, waits for them, and re-layouts  81.5 us (2%)
  other arithmetic  81.5 us (2%)
    reduce_scatter x1, waiting for transfers between devices, sum_model_rows(): lax.psum_scatter(term_fn(jnp.int32(0), lax.axis_size(('fsdp', 'dp')) * lo...  1750 us
    reduce_scatter x1, waiting for transfers between devices, sum_hidden_rows(): lax.psum_scatter(term_fn(jnp.int32(0), lax.axis_size(('fsdp', 'dp')) * lo...  572 us
    all_gather x1, waiting for transfers between devices, fetch_down(): whole_set = lax.all_gather(feed_down, ('fsdp', 'dp'), axis=0, tiled=True)  106 us
    all_gather x1, waiting for transfers between devices, fetch_mixer(): lax.all_gather(value_weight, ('fsdp', 'dp'), axis=0, tiled=True)  105 us
    all_gather x1, waiting for transfers between devices, fetch_feed(): lax.all_gather(feed_gate, ('fsdp', 'dp'), axis=0, tiled=True)  104 us
    dot_general x8, matrix products, times_rows(): lax.dot_general(left_rows, right_rows, (((0,), (0,)), ((), ())), preferre...  101 us
    dot_general x8, matrix products, times_back(): lax.dot_general(left_rows, right_rows, (((1,), (1,)), ((), ())), preferre...  100 us
    all_gather x1, waiting for transfers between devices, fetch_output(): lax.all_gather(output_weight, ('fsdp', 'dp'), axis=0, tiled=True)  98.7 us
  transfers between devices with their start and end apart: 12, of which 11 were waited for; matrix products, arithmetic and copies ran while one was open for 8% of the time, Pallas kernels for 0%

commit v1 on v0

v1 whole, which is shorter than its diff:
```python
import math

import jax
import jax.numpy as jnp
from jax import lax
from jax.sharding import Mesh, PartitionSpec as P

HEADS = 8
KEY = 256
VAL = 512
EPSILON = 1e-05
RETAIN_EPSILON = 0.05

GROUP = ("y", "x", "core")
EVERY = ("y", "x", "z", "core")
F32 = jnp.float32
BF16 = jnp.bfloat16


def normalize_rows(field_in, offset=EPSILON):
    centre = jnp.mean(field_in, axis=-1, keepdims=True)
    centred = field_in - centre
    spread = jnp.mean(centred * centred, axis=-1, keepdims=True)
    return centred * lax.rsqrt(spread + offset)


def rotate(field_in, direction):
    length = field_in.shape[-2]
    breadth = field_in.shape[-1]
    half_width = breadth // 2
    columns = jnp.arange(half_width).astype(F32)
    angles = jnp.exp(-math.log(10000.0) * columns / (half_width - 1))
    zeta_scale = (2.0 * columns + 0.4 * breadth) / (1.4 * breadth)
    places = jnp.arange(length).astype(F32)[:, None]
    phases = places * angles[None, :]
    growth = jnp.exp(direction * places / 512.0 * jnp.log(zeta_scale)[None, :])
    cosine = jnp.cos(phases) * growth
    sine_part = jnp.sin(phases) * growth
    first_half = field_in[..., :half_width]
    second = field_in[..., half_width:]
    return jnp.concatenate(
        [first_half * cosine - second * sine_part, second * cosine + first_half * sine_part],
        axis=-1,
    )


def decay_mask(length, head):
    log_decay = jnp.log(1.0 - jnp.exp2(-5.0 - head.astype(F32)))
    places = jnp.arange(length)
    distance = (places[:, None] - places[None, :]).astype(F32)
    decayed = jnp.where(distance >= 0.0, jnp.exp(log_decay * jnp.maximum(distance, 0.0)), 0.0)
    return decayed * lax.rsqrt(jnp.sum(decayed, axis=-1, keepdims=True))


def shape_scores(raw_scores, decay):
    weighted = raw_scores * decay
    row_total = jnp.sum(weighted * weighted, axis=-1, keepdims=True)
    return weighted * lax.rsqrt(1.0 + row_total)


def gate_mix(retained, gate_proj):
    return jax.nn.silu(gate_proj) * normalize_rows(retained, RETAIN_EPSILON)


def dot(left, right):
    return jnp.dot(left, right, preferred_element_type=F32)


def dot_rows(left, right):
    return lax.dot_general(left, right, (((0,), (0,)), ((), ())), preferred_element_type=F32)


def dot_back(left, right):
    return lax.dot_general(left, right, (((1,), (1,)), ((), ())), preferred_element_type=F32)


def swap(field_in, axis):
    return lax.ppermute(field_in, axis, [(0, 1), (1, 0)])


def spread_blocks(own):
    half = own.shape[0] // 2
    from_x = swap(own, "x")
    from_y = swap(own, "y")
    upper = swap(from_y[:half], "x")
    lower = swap(from_x[half:], "y")
    mine = [own, from_x, from_y, jnp.concatenate([upper, lower], axis=0)]
    blocks = []
    for block in mine:
        blocks += [block, swap(block, "core")]
    return blocks


def sum_blocks(partial):
    half = partial.shape[1] // 2
    pairs = partial.reshape(4, 2, *partial.shape[1:])
    arrived = swap(pairs[:, 1], "core")
    summed = pairs[:, 0].astype(F32) + arrived.astype(F32)
    across = summed[3].astype(BF16)
    upper = swap(across[:half], "x")
    lower = swap(across[half:], "y")
    to_y = jnp.concatenate([summed[2, :half] + upper.astype(F32), summed[2, half:]], axis=0)
    to_x = jnp.concatenate([summed[1, :half], summed[1, half:] + lower.astype(F32)], axis=0)
    from_y = swap(to_y.astype(BF16), "y")
    from_x = swap(to_x.astype(BF16), "x")
    return summed[0] + from_y.astype(F32) + from_x.astype(F32)


def body(
    tokens,
    lengths,
    dealing,
    cotangent,
    query_weight,
    key_weight,
    value_weight,
    gate_weight,
    mixer_gain,
    mixer_bias,
    output_weight,
    feed_gate,
    feed_up,
    feed_down,
    feed_gain,
    feed_bias,
):
    _, length, breadth = tokens.shape
    layers = lax.axis_size("z")
    local_model = query_weight.shape[0]
    local_hidden = feed_down.shape[0]
    local_value = output_weight.shape[0]
    group = 8
    half_layers = layers // 2
    hidden = local_hidden * layers
    scale_factor = KEY ** (-0.5)
    fsdp_index = lax.axis_index("y") * 2 + lax.axis_index("x")
    core = lax.axis_index("core")
    layer = lax.axis_index("z")
    head = fsdp_index * 2 + core

    def across_group(packed):
        return lax.all_to_all(packed, GROUP, 0, 0, tiled=True)

    def gather_layers(packed):
        width = packed.shape[-1]
        return lax.all_gather(
            packed.reshape(4, 2 * local_model, width), "z", axis=1, tiled=True
        ).reshape(-1, width)

    def value_columns(weight):
        split = weight.reshape(local_model, 4, 2, half_layers, 2, local_value)
        return split.transpose(1, 2, 0, 4, 3, 5).reshape(group, local_model, VAL)

    def hidden_columns(weight):
        split = weight.reshape(local_model, 4, layers, 2, local_hidden)
        return split.transpose(1, 3, 0, 2, 4).reshape(group, local_model, hidden)

    def head_columns(weight):
        return weight.reshape(local_model, group, KEY).transpose(1, 0, 2)

    mixer_packed = jnp.concatenate(
        [
            head_columns(query_weight),
            head_columns(key_weight),
            value_columns(value_weight),
            value_columns(gate_weight),
        ],
        axis=2,
    )
    mixer_weight = gather_layers(across_group(mixer_packed))
    features = lax.all_gather(
        jnp.stack([mixer_gain, mixer_bias, feed_gain, feed_bias]), EVERY, axis=1, tiled=True
    ).astype(F32)
    out_weight = lax.all_gather(output_weight, "z", axis=0, tiled=True)
    out_weight = lax.all_to_all(out_weight, "core", 0, 0, tiled=True)
    feed_packed = jnp.concatenate([hidden_columns(feed_gate), hidden_columns(feed_up)], axis=2)
    feed_weight = gather_layers(across_group(feed_packed))
    down_weight = lax.all_gather(feed_down, "z", axis=0, tiled=True)

    def slot_of(bits_f, bits_c):
        member_f = fsdp_index ^ bits_f
        member_c = core ^ bits_c
        number = (member_f * layers + layer) * 2 + member_c
        return (fsdp_index ^ (dealing[number] // (2 * layers))) * 2 + bits_c

    to_slot = jnp.stack([slot_of(j // 2, j % 2) for j in range(group)])
    own_number = (fsdp_index * layers + layer) * 2 + core
    back_f = jnp.int32(0)
    for bits in range(4):
        back_f = jnp.where(to_slot[bits * 2] == 0, bits, back_f)
    own_sequence = back_f * 2
    slots = jnp.arange(group, dtype=jnp.int32)
    to_sequence = jnp.sum(
        jnp.where(to_slot[None, :] == slots[:, None], slots[None, :], 0), axis=1
    )

    token_blocks = spread_blocks(tokens[0])
    token_all = jnp.stack(token_blocks)
    residual_in = lax.dynamic_index_in_dim(token_all, to_slot[0], 0, keepdims=False).astype(F32)
    mixer_normed = (
        normalize_rows(token_all.astype(F32)) * features[0] + features[1]
    ).astype(BF16).reshape(group * length, breadth)

    places = jnp.arange(length, dtype=jnp.int32)
    live_mask = (places < lengths[0]).astype(F32)[:, None]
    upstream = cotangent[0].astype(F32) * live_mask
    down_low = jnp.stack(spread_blocks(upstream.astype(BF16))).reshape(group * length, breadth)

    projected = dot(mixer_normed, mixer_weight).reshape(group, length, -1)
    queries = projected[..., :KEY]
    key_proj = projected[..., KEY : 2 * KEY]
    value_low = projected[..., 2 * KEY : 2 * KEY + VAL].astype(BF16)
    gate_proj = projected[..., 2 * KEY + VAL :]
    query_rot, query_pull = jax.vjp(lambda field_in: rotate(field_in, 1.0), queries)
    key_rot, key_pull = jax.vjp(lambda field_in: rotate(field_in, -1.0), key_proj)
    query_low = query_rot.astype(BF16)
    key_low = key_rot.astype(BF16)
    decay = decay_mask(length, head)
    raw_scores = (
        jnp.einsum("nlk,nmk->nlm", query_low, key_low, preferred_element_type=F32) * scale_factor
    )
    shaped, shape_pull = jax.vjp(lambda scores_in: shape_scores(scores_in, decay), raw_scores)
    shaped_low = shaped.astype(BF16)
    retained = jnp.einsum("nlm,nmv->nlv", shaped_low, value_low, preferred_element_type=F32)
    gated_full, gate_pull = jax.vjp(gate_mix, retained, gate_proj)
    gated_low = jnp.take(gated_full.astype(BF16), to_slot, axis=0).reshape(group * length, VAL)

    mixer_part = dot(gated_low, out_weight).astype(BF16).reshape(group, length, breadth)
    hidden_state = residual_in + sum_blocks(mixer_part)
    feed_hat, feed_pull = jax.vjp(normalize_rows, hidden_state)
    own_normed = (feed_hat * features[2] + features[3]).astype(BF16)
    feed_normed = jnp.stack(spread_blocks(own_normed)).reshape(group * length, breadth)

    feed_pre = dot(feed_normed, feed_weight)
    gate_pre = feed_pre[:, :hidden]
    up_pre = feed_pre[:, hidden:]
    activated_full, act_pull = jax.vjp(
        lambda gate_in, up_in: jax.nn.gelu(gate_in, approximate=False) * up_in, gate_pre, up_pre
    )
    activated = activated_full.astype(BF16)
    feed_part = dot(activated, down_weight).astype(BF16).reshape(group, length, breadth)

    act_grad = dot_back(down_low, down_weight)
    gate_pre_grad, up_pre_grad = act_pull(act_grad)
    pre_low = jnp.concatenate([gate_pre_grad.astype(BF16), up_pre_grad.astype(BF16)], axis=1)
    normed_part = dot_back(pre_low, feed_weight).astype(BF16).reshape(group, length, breadth)
    feed_normed_grad = sum_blocks(normed_part)
    feed_gain_part = jnp.sum(feed_normed_grad * feed_hat, axis=0)
    feed_bias_part = jnp.sum(feed_normed_grad, axis=0)
    state_grad = upstream + feed_pull(feed_normed_grad * features[2])[0]
    own_grad_low = state_grad.astype(BF16)
    out_grad_blocks = jnp.stack(spread_blocks(own_grad_low))
    out_grad_low = out_grad_blocks.reshape(group * length, breadth)

    out_tokens = (live_mask * (hidden_state + sum_blocks(feed_part))).astype(BF16)

    def scatter_layers(grads):
        width = grads.shape[-1]
        return lax.psum_scatter(
            grads.astype(BF16).reshape(4, -1, width), "z", scatter_dimension=1, tiled=True
        ).reshape(group, local_model, width)

    down_grad = lax.psum_scatter(
        dot_rows(activated, down_low).astype(BF16), "z", scatter_dimension=0, tiled=True
    ).astype(F32)
    feed_grads = across_group(scatter_layers(dot_rows(feed_normed, pre_low))).astype(F32)

    gated_grad = jnp.take(
        dot_back(out_grad_low, out_weight).reshape(group, length, VAL), to_sequence, axis=0
    )
    out_weight_grad = dot_rows(gated_low, out_grad_low).astype(BF16)
    out_weight_grad = lax.all_to_all(out_weight_grad, "core", 0, 0, tiled=True)
    output_grad = lax.psum_scatter(out_weight_grad, "z", scatter_dimension=0, tiled=True).astype(F32)

    retained_grad, gate_proj_grad = gate_pull(gated_grad)
    retained_low = retained_grad.astype(BF16)
    value_grad = jnp.einsum("nlm,nlv->nmv", shaped_low, retained_low, preferred_element_type=F32)
    shaped_grad = jnp.einsum("nlv,nmv->nlm", retained_low, value_low, preferred_element_type=F32)
    score_grad = shape_pull(shaped_grad)[0].astype(BF16)
    query_rot_grad = (
        jnp.einsum("nlm,nmk->nlk", score_grad, key_low, preferred_element_type=F32) * scale_factor
    )
    key_rot_grad = (
        jnp.einsum("nlm,nlk->nmk", score_grad, query_low, preferred_element_type=F32) * scale_factor
    )
    mixer_grad_low = jnp.concatenate(
        [
            query_pull(query_rot_grad)[0].astype(BF16),
            key_pull(key_rot_grad)[0].astype(BF16),
            value_grad.astype(BF16),
            gate_proj_grad.astype(BF16),
        ],
        axis=2,
    ).reshape(group * length, -1)
    mixer_grads = across_group(scatter_layers(dot_rows(mixer_normed, mixer_grad_low))).astype(F32)
    mixer_part_grad = dot_back(mixer_grad_low, mixer_weight).astype(BF16)
    mixer_normed_grad = sum_blocks(mixer_part_grad.reshape(group, length, breadth))
    mixer_hat, mixer_pull = jax.vjp(normalize_rows, tokens[0].astype(F32))
    mixer_gain_part = jnp.sum(mixer_normed_grad * mixer_hat, axis=0)
    mixer_bias_part = jnp.sum(mixer_normed_grad, axis=0)
    slot_grad = lax.dynamic_index_in_dim(out_grad_blocks, own_sequence, 0, keepdims=False)
    input_grad = (
        slot_grad.astype(F32) + mixer_pull(mixer_normed_grad * features[0])[0]
    ).astype(BF16)

    feature_grads = lax.psum_scatter(
        jnp.stack([mixer_gain_part, mixer_bias_part, feed_gain_part, feed_bias_part]),
        EVERY,
        scatter_dimension=1,
        tiled=True,
    )

    def head_back(grads):
        return grads.transpose(1, 0, 2).reshape(local_model, -1)

    def value_back(grads):
        split = grads.reshape(4, 2, local_model, 2, half_layers, local_value)
        return split.transpose(2, 0, 1, 4, 3, 5).reshape(local_model, -1)

    def hidden_back(grads):
        split = grads.reshape(4, 2, local_model, layers, local_hidden)
        return split.transpose(2, 0, 3, 1, 4).reshape(local_model, -1)

    return (
        out_tokens[None],
        input_grad[None],
        head_back(mixer_grads[..., :KEY]),
        head_back(mixer_grads[..., KEY : 2 * KEY]),
        value_back(mixer_grads[..., 2 * KEY : 2 * KEY + VAL]),
        value_back(mixer_grads[..., 2 * KEY + VAL :]),
        feature_grads[0],
        feature_grads[1],
        output_grad,
        hidden_back(feed_grads[..., :hidden]),
        hidden_back(feed_grads[..., hidden:]),
        down_grad,
        feature_grads[2],
        feature_grads[3],
    )


def solution(mesh):
    layers = mesh.shape["dp"] // 2
    fine = Mesh(mesh.devices.reshape(2, 2, layers, 2), EVERY)
    sequences = P(EVERY, None, None)
    rows = P(EVERY, None)
    vector = P(EVERY)
    in_specs = (
        (sequences, vector, P(), sequences)
        + (rows,) * 4
        + (vector,) * 2
        + (rows,) * 4
        + (vector,) * 2
    )
    out_specs = (
        (sequences,) * 2 + (rows,) * 4 + (vector,) * 2 + (rows,) * 4 + (vector,) * 2
    )
    return jax.shard_map(body, mesh=fine, in_specs=in_specs, out_specs=out_specs, check_vma=False)
```

time: 3640 us -> 935 us (0.26)
  waiting for transfers between devices: 3060 us -> 377 us
  matrix products: 308 us -> 166 us
  starting transfers between devices: 0.46 us -> 60.7 us
    reduce_scatter x2 -> x4, waiting for transfers between devices: 2320 us -> 30 us  [the longest x2 30 us: scatter_layers(): lax.psum_scatter(grads.astype(BF16).reshape(4, -1, width), 'z', scatter_d...]
    all_gather x10 -> x4, waiting for transfers between devices: 736 us -> 19.3 us  [the longest x2 19.3 us: gather_layers(): lax.all_gather(packed.reshape(4, 2 * local_model, width), 'z', axis=1, ti...]
    ppermute x0 -> x52, waiting for transfers between devices: none -> 192 us  [swap(): return lax.ppermute(field_in, axis, [(0, 1), (1, 0)])]
    dot_general x32 -> x18, matrix products: 308 us -> 166 us  [the longest x4 60.8 us: dot_back(): lax.dot_general(left, right, (((1,), (1,)), ((), ())), preferred_element_...]
    unnamed x12 -> x10, waiting for transfers between devices: 5.76 us -> 136 us
    unnamed x2 -> x0, blocking collectives: 84.9 us -> none
    all_gather x0 -> x1, blocking collectives: none -> 44.1 us  [body(): lax.all_gather(jnp.stack([mixer_gain, mixer_bias, feed_gain, feed_bias]),...]
    concatenate x3 -> x11, other arithmetic: 44.9 us -> 6.72 us  [the longest x1 2.9 us: body(): jnp.concatenate([query_pull(query_rot_grad)[0].astype(BF16), key_pull(key...]
  transfers between devices with their start and end apart: 12 -> 66, of which waited for: 11 -> 29; matrix products, arithmetic and copies ran while one was open for 8% -> 33% of each run, Pallas kernels for 0% -> 0%
where the time goes in v1:
time: 935 us; the launch traced here: 925 us
  waiting for transfers between devices  377 us (40%)
  matrix products  166 us (18%)
  local copies, waits for them, and re-layouts  111 us (12%)
  other arithmetic  103 us (11%)
  blocking collectives  70.2 us (8%)
  starting transfers between devices  60.7 us (6%)
  between operations  37.3 us (4%)
    ppermute x52, waiting for transfers between devices, swap(): return lax.ppermute(field_in, axis, [(0, 1), (1, 0)])  192 us
    unnamed x10, waiting for transfers between devices  136 us
    dot_general x4, matrix products, dot_back(): lax.dot_general(left, right, (((1,), (1,)), ((), ())), preferred_element_...  60.8 us
    unnamed x189, local copies, waits for them, and re-layouts  59 us
    dot_general x4, matrix products, dot_rows(): lax.dot_general(left, right, (((0,), (0,)), ((), ())), preferred_element_...  52.3 us
    dot_general x4, matrix products, dot(): return jnp.dot(left, right, preferred_element_type=F32)  44.2 us
    all_gather x1, blocking collectives, body(): lax.all_gather(jnp.stack([mixer_gain, mixer_bias, feed_gain, feed_bias]),...  44.1 us
    ppermute x52, starting transfers between devices, swap(): return lax.ppermute(field_in, axis, [(0, 1), (1, 0)])  38.2 us
  transfers between devices with their start and end apart: 66, of which 29 were waited for; matrix products, arithmetic and copies ran while one was open for 33% of the time, Pallas kernels for 0%

profile of v1, /device:TPU:0, one launch (start us, length us, event | category | flops | bytes accessed | tf_op | source)
XLA Modules:
  0.0 924.9 jit_solution(7152669037854200962)
XLA Ops:
  13.2 26.2 %all_to_all.44 = bf16[8,64,1536]{2,1,0:T(8,128)(2,1)} all-to-all(bf16[8,64,1536]{2,1,0:T(8,128)(2,1)S(1)} %pad_maximum_fusion.4), channel_id=1, replica_groups=mesh['y'=2,'x'=2,'z'=4,'core'=2] {'y','x','core'}, dimensions={0} | all-to-all | bytes 3145728 | tf_op jit(solution)/shard_map/all_to_all | solution.py:142
  44.3 3.8 all-to-all-start.2
  70.0 44.1 %all-gather = bf16[32,64,4]{1,2,0:T(4,128)(2,1)S(1)} all-gather(bf16[1,64,4]{1,2,0:T(4,128)(2,1)S(1)} %maximum_bitcast_fusion), channel_id=1, replica_groups=mesh['y'=2,'x'=2,'z'=4,'core'=2] {'y','x','z','core'}, dimensions={0}, use_global_device_ids=true | all-gather | bytes 16896 | tf_op jit(solution)/shard_map/all_gather | solution.py:171
  126.1 7.2 collective-permute-done.5
  141.2 4.7 convert_reduce_fusion
  149.4 4.8 all-to-all-start.1
  154.7 19.3 %all-gather.6.cloned.1.call-done = bf16[4,512,1536]{2,1,0:T(8,128)(2,1)} async-done(((bf16[4,128,1536]{2,1,0:T(8,128)(2,1)}), bf16[4,512,1536]{2,1,0:T(8,128)(2,1)}) %all-gather.6.cloned.1.call-update) | async-done | bytes 6291472 | tf_op jit(solution)/shard_map/all_gather | solution.py:146
  174.0 17.5 %fusion.7 = f32[8,256,1536]{2,1,0:T(8,128)S(1)} fusion(bf16[2048,1536,1]{1,0,2:T(8,128)(2,1)} %bitcast.465, bf16[8,256,2048]{2,1,0:T(8,128)(2,1)} %bitcast_dynamic-update-slice_fusion.23, f32[2048]{0:T(1024)S(1)} %bitcast.455, f32[2048]{0:T(1024)S(1)} %bitcast.437, f32[8,256]{1,0:T(8,128)S(1)} %add_rsqrt_fusion, f32[8,256]{1,0:T(8,128)S(1)} %broadcast_multiply_fusion.2), kind=kOutput, calls=%fused_computation.23 | convolution fusion | flops 12910067712 | bytes 27295744 | tf_op jit(solution)/shard_map/dot_general | solution.py:66
  204.5 7.1 convolution_convert_fusion.3
  222.2 21.6 %collective-permute-done.29 = bf16[256,2048]{1,0:T(8,128)(2,1)S(1)} collective-permute-done((bf16[256,2048]{1,0:T(8,128)(2,1)}, bf16[256,2048]{1,0:T(8,128)(2,1)S(1)}, u32[]{:S(2)}, u32[]{:S(2)}) %collective-permute-start.29) | collective-permute-done | bytes 1048608 | tf_op jit(solution)/shard_map/ppermute | solution.py:78
  250.7 5.6 fusion.90
  260.2 10.8 %collective-permute-done.9 = bf16[128,2048]{1,0:T(8,128)(2,1)S(1)} collective-permute-done((bf16[128,2048]{1,0:T(8,128)(2,1)S(1)}, bf16[128,2048]{1,0:T(8,128)(2,1)S(1)}, u32[]{:S(2)}, u32[]{:S(2)}) %collective-permute-start.9) | collective-permute-done | bytes 524320 | tf_op jit(solution)/shard_map/ppermute | solution.py:78
  277.6 19.4 %collective-permute-done.12 = bf16[256,2048]{1,0:T(8,128)(2,1)S(1)} collective-permute-done((bf16[256,2048]{1,0:T(8,128)(2,1)S(1)}, bf16[256,2048]{1,0:T(8,128)(2,1)S(1)}, u32[]{:S(2)}, u32[]{:S(2)}) %collective-permute-start.12) | collective-permute-done | bytes 1048608 | tf_op jit(solution)/shard_map/ppermute | solution.py:78
  307.6 17.2 %collective-permute-done.14 = bf16[256,2048]{1,0:T(8,128)(2,1)S(1)} collective-permute-done((bf16[256,2048]{1,0:T(8,128)(2,1)S(1)}, bf16[256,2048]{1,0:T(8,128)(2,1)S(1)}, u32[]{:S(2)}, u32[]{:S(2)}) %collective-permute-start.14) | collective-permute-done | bytes 1048608 | tf_op jit(solution)/shard_map/ppermute | solution.py:78
  332.1 9.7 %collective-permute-done.18 = bf16[128,2048]{1,0:T(8,128)(2,1)S(1)} collective-permute-done((bf16[128,2048]{1,0:T(8,128)(2,1)S(1)}, bf16[128,2048]{1,0:T(8,128)(2,1)S(1)}, u32[]{:S(2)}, u32[]{:S(2)}) %collective-permute-start.18) | collective-permute-done | bytes 524320 | tf_op jit(solution)/shard_map/ppermute | solution.py:78
  347.2 14.8 %fusion.107 = f32[2048,1024]{0,1:T(8,128)} fusion(bf16[2048,2048]{1,0:T(8,128)(2,1)} %bitcast.74, bf16[2048,1024]{1,0:T(8,128)(2,1)} %bitcast.467), kind=kOutput, calls=%fused_computation.302 | convolution fusion | flops 8589934592 | bytes 20971520 | tf_op jit(solution)/shard_map/dot_general | solution.py:66
  362.1 21.7 %add_convert_fusion.1 = (bf16[2048,512]{0,1:T(8,128)(2,1)}, f32[2048,512]{0,1:T(8,128)S(1)}, f32[2048,512]{0,1:T(8,128)}) fusion(f32[2048,1024]{0,1:T(8,128)} %fusion.107, bf16[2048,2048]{1,0:T(8,128)(2,1)} %bitcast.443, bf16[512,2048]{1,0:T(8,128)(2,1)} %all-gather.12.cloned.1.call-done), kind=kOutput, calls=%fused_computation.42 | convolution fusion | flops 4371513344 | bytes 29360128 | tf_op jit(solution)/shard_map/dot_general | solution.py:74
  383.8 8.1 multiply_convert_fusion
  391.9 12.7 %convolution_convert_fusion.1 = bf16[2048,2048]{1,0:T(8,128)(2,1)S(1)} fusion(bf16[2048,1024]{1,0:T(8,128)(2,1)} %bitcast.468, bf16[2048,512]{0,1:T(8,128)(2,1)} %get-tuple-element.45, bf16[2048,512]{0,1:T(8,128)(2,1)} %get-tuple-element.30), kind=kOutput, calls=%fused_computation.16 | convolution fusion | flops 8602517504 | bytes 16777216 | tf_op jit(solution)/shard_map/dot_general | solution.py:74
  409.9 4.9 convolution_convert_fusion.2
  417.2 3.2 copy-done.12
  420.5 13.0 %convolution_convert_fusion.4 = bf16[2048,1024]{1,0:T(8,128)(2,1)} fusion(bf16[2048,2048]{1,0:T(8,128)(2,1)} %bitcast.74, bf16[2048,512]{0,1:T(8,128)(2,1)S(1)} %copy-done.22, bf16[2048,512]{0,1:T(8,128)(2,1)S(1)} %copy-done.73), kind=kOutput, calls=%fused_computation.63 | convolution fusion | flops 8600420352 | bytes 16777216 | tf_op jit(solution)/shard_map/dot_general | solution.py:70
  433.6 8.9 fusion.92
  444.8 8.0 fusion.91
  461.9 7.6 collective-permute-done.22
  472.8 19.1 %collective-permute-done.38 = bf16[256,2048]{1,0:T(8,128)(2,1)S(1)} collective-permute-done((bf16[256,2048]{1,0:T(8,128)(2,1)S(1)}, bf16[256,2048]{1,0:T(8,128)(2,1)S(1)}, u32[]{:S(2)}, u32[]{:S(2)}) %collective-permute-start.38) | collective-permute-done | bytes 1048608 | tf_op jit(solution)/shard_map/ppermute | solution.py:78
  495.3 18.1 %collective-permute-done.25 = bf16[256,2048]{1,0:T(8,128)(2,1)S(1)} collective-permute-done((bf16[256,2048]{1,0:T(8,128)(2,1)S(1)}, bf16[256,2048]{1,0:T(8,128)(2,1)S(1)}, u32[]{:S(2)}, u32[]{:S(2)}) %collective-permute-start.25) | collective-permute-done | bytes 1048608 | tf_op jit(solution)/shard_map/ppermute | solution.py:78
  519.2 6.0 convolution_convert_fusion.5
  525.3 15.9 %collective-permute-done.40 = bf16[256,2048]{1,0:T(8,128)(2,1)S(1)} collective-permute-done((bf16[256,2048]{1,0:T(8,128)(2,1)S(1)}, bf16[256,2048]{1,0:T(8,128)(2,1)S(1)}, u32[]{:S(2)}, u32[]{:S(2)}) %collective-permute-start.40) | collective-permute-done | bytes 1048608 | tf_op jit(solution)/shard_map/ppermute | solution.py:78
  549.3 8.6 collective-permute-done.44
  563.4 9.1 bitcast_convert_fusion.1
  572.5 4.9 all-to-all-start.4
  577.4 10.5 %fusion.108 = f32[8,256,512]{2,1,0:T(8,128)} fusion(bf16[8,256,2048]{2,1,0:T(8,128)(2,1)} %bitcast_dynamic-update-slice_fusion, bf16[512,2048,1]{1,0,2:T(8,128)(2,1)} %bitcast.118), kind=kOutput, calls=%fused_computation.303 | convolution fusion | flops 4294967296 | bytes 14680064 | tf_op jit(solution)/shard_map/dot_general | solution.py:74
  587.9 5.0 gather_fusion.1
  592.9 7.3 multiply_reduce_fusion
  604.5 3.7 multiply_reduce_fusion.3
  615.3 24.2 %bitcast_convert_fusion = bf16[2048,1536]{1,0:T(8,128)(2,1)} fusion(bf16[8,256,2048]{2,1,0:T(8,128)(2,1)} %bitcast_dynamic-update-slice_fusion.23, f32[2048]{0:T(1024)S(1)} %bitcast.456, f32[2048]{0:T(1024)S(1)} %bitcast.438, f32[8,256]{1,0:T(8,128)S(1)} %copy-done.63, f32[8,256]{1,0:T(8,128)S(1)} %copy-done.59, ...), kind=kOutput, calls=%fused_computation.10 | convolution fusion | flops 12938379264 | bytes 21004288 | tf_op jit(solution)/shard_map/dot_general | solution.py:70
  644.0 15.9 %convolution_convert_fusion = bf16[2048,2048]{1,0:T(8,128)(2,1)S(1)} fusion(bf16[2048,1536]{1,0:T(8,128)(2,1)S(1)} %bitcast.413, bf16[2048,1536]{1,0:T(8,128)(2,1)} %bitcast.466), kind=kOutput, calls=%fused_computation.15 | convolution fusion | flops 12889096192 | bytes 20971520 | tf_op jit(solution)/shard_map/dot_general | solution.py:74
  660.7 6.9 collective-permute-done.47
  667.6 7.6 fusion.93
  678.5 3.7 all-to-all-start.5
  682.3 9.0 collective-permute-done.48
  695.3 3.9 collective-permute-start.51
  714.1 10.5 %collective-permute-done.51 = bf16[256,2048]{1,0:T(8,128)(2,1)} collective-permute-done((bf16[256,2048]{1,0:T(8,128)(2,1)}, bf16[256,2048]{1,0:T(8,128)(2,1)}, u32[]{:S(2)}, u32[]{:S(2)}) %collective-permute-start.51) | collective-permute-done | bytes 1048608 | tf_op jit(solution)/shard_map/ppermute | solution.py:78
  724.8 3.1 fusion.24
  728.0 30.0 %reduce-scatter.8.cloned.1.call-done = bf16[4,128,1536]{2,1,0:T(8,128)(2,1)} async-done(((bf16[4,512,1536]{2,1,0:T(8,128)(2,1)}), bf16[4,128,1536]{2,1,0:T(8,128)(2,1)}) %reduce-scatter.8.cloned.1.call-update) | async-done | bytes 1572880 | tf_op jit(solution)/shard_map/reduce_scatter | solution.py:259
  758.0 4.3 all-to-all-start.3
  768.0 135.6 %reduce-scatter.16.cloned.1.call-done = f32[64,4]{1,0:T(8,128)} async-done(((f32[2048,4]{1,0:T(8,128)}), f32[64,4]{1,0:T(8,128)}) %reduce-scatter.16.cloned.1.call-update) | async-done | bytes 1040
  (448 shorter events, 202.8 us)
Async XLA Ops:
  7.2 142.2 %all-gather.8.cloned.1.call-start = ((), (), s32[]{:S(2)}) async-start(), calls=%async_computation.12 | async-start | bytes 2621440 | tf_op jit(solution)/shard_map/all_gather | solution.py:174
  7.9 166.1 %all-gather.6.cloned.1.call-start = ((), (), s32[]{:S(2)}) async-start(), calls=%async_computation.11 | async-start | bytes 7864320 | tf_op jit(solution)/shard_map/all_gather | solution.py:146
  39.5 78.5 %collective-permute-start.3 = (bf16[256,2048]{1,0:T(8,128)(2,1)S(1)}, bf16[256,2048]{1,0:T(8,128)(2,1)}, u32[]{:S(2)}, u32[]{:S(2)}) collective-permute-start(bf16[256,2048]{1,0:T(8,128)(2,1)S(1)} %bitcast.401), channel_id=1, source_target_pairs={{0,16},{16,0},{1,17},{17,1},{2,18},{18,2},{3,19},{19,3},{4,20},{20... | collective-permute-start | bytes 3145736 | tf_op jit(solution)/shard_map/ppermute | solution.py:78
  40.1 79.0 %collective-permute-start.1 = (bf16[256,2048]{1,0:T(8,128)(2,1)S(1)}, bf16[256,2048]{1,0:T(8,128)(2,1)}, u32[]{:S(2)}, u32[]{:S(2)}) collective-permute-start(bf16[256,2048]{1,0:T(8,128)(2,1)S(1)} %bitcast.402), channel_id=1, source_target_pairs={{0,8},{8,0},{1,9},{9,1},{2,10},{10,2},{3,11},{11,3},{4,12},{12,4},... | collective-permute-start | bytes 3145736 | tf_op jit(solution)/shard_map/ppermute | solution.py:78
  40.6 80.8 %collective-permute-start = (bf16[256,2048]{1,0:T(8,128)(2,1)S(1)}, bf16[256,2048]{1,0:T(8,128)(2,1)}, u32[]{:S(2)}, u32[]{:S(2)}) collective-permute-start(bf16[256,2048]{1,0:T(8,128)(2,1)S(1)} %bitcast.403), channel_id=1, source_target_pairs={{0,1},{1,0},{2,3},{3,2},{4,5},{5,4},{6,7},{7,6},{8,9},{9,8},{10,11... | collective-permute-start | bytes 3145736 | tf_op jit(solution)/shard_map/ppermute | solution.py:78
  44.3 72.6 %all-to-all-start.2 = ((bf16[8,64,1024]{2,1,0:T(8,128)(2,1)}), bf16[8,64,1024]{2,1,0:T(8,128)(2,1)S(1)}, u32[]{:S(2)}, u32[]{:S(2)}) async-start(bf16[8,64,1024]{2,1,0:T(8,128)(2,1)} %pad_maximum_fusion.9), calls=%async_computation.2 | async-start | bytes 2097152 | tf_op jit(solution)/shard_map/all_to_all | solution.py:142
  48.1 299.2 %all-gather.10.cloned.1.call-start = ((), (), s32[]{:S(2)}) async-start(), calls=%async_computation.13 | async-start | bytes 5242880 | tf_op jit(solution)/shard_map/all_gather | solution.py:146
  120.9 17.1 %collective-permute-start.4 = (bf16[256,2048]{1,0:T(8,128)(2,1)}, bf16[256,2048]{1,0:T(8,128)(2,1)S(1)}, u32[]{:S(2)}, u32[]{:S(2)}) collective-permute-start(bf16[256,2048]{1,0:T(8,128)(2,1)} %collective-permute-done.3), channel_id=1, source_target_pairs={{0,1},{1,0},{2,3},{3,2},{4,5},{5,4},{6,7},{7,6},{8,9},{9,8},{10,11... | collective-permute-start | bytes 3145736 | tf_op jit(solution)/shard_map/ppermute | solution.py:78
  149.4 55.1 %all-to-all-start.1 = ((bf16[2,256,2048]{2,1,0:T(8,128)(2,1)}), bf16[2,256,2048]{2,1,0:T(8,128)(2,1)}, u32[]{:S(2)}, u32[]{:S(2)}) async-start(bf16[2,256,2048]{2,1,0:T(8,128)(2,1)} %bitcast.422), calls=%async_computation.1 | async-start | bytes 4194304 | tf_op jit(solution)/shard_map/all_to_all | solution.py:175
  154.2 207.9 %all-gather.12.cloned.1.call-start = ((), (), s32[]{:S(2)}) async-start(), calls=%async_computation.14 | async-start | bytes 2621440 | tf_op jit(solution)/shard_map/all_gather | solution.py:178
  216.1 34.7 %collective-permute-start.8 = (bf16[4,256,2048]{2,1,0:T(8,128)(2,1)}, bf16[4,256,2048]{2,1,0:T(8,128)(2,1)}, u32[]{:S(2)}, u32[]{:S(2)}) collective-permute-start(bf16[4,256,2048]{2,1,0:T(8,128)(2,1)} %slice_bitcast_fusion.6), channel_id=1, source_target_pairs={{0,1},{1,0},{2,3},{3,2},{4,5},{5,4},{6,7},{7,6},{8,9},{9,8},{10,11... | collective-permute-start | bytes 12582920 | tf_op jit(solution)/shard_map/ppermute | solution.py:78
  218.0 25.8 %collective-permute-start.29 = (bf16[256,2048]{1,0:T(8,128)(2,1)}, bf16[256,2048]{1,0:T(8,128)(2,1)S(1)}, u32[]{:S(2)}, u32[]{:S(2)}) collective-permute-start(bf16[256,2048]{1,0:T(8,128)(2,1)} %fusion.30), channel_id=1, source_target_pairs={{0,16},{16,0},{1,17},{17,1},{2,18},{18,2},{3,19},{19,3},{4,20},{20... | collective-permute-start | bytes 3145736 | tf_op jit(solution)/shard_map/ppermute | solution.py:78
  219.5 26.6 %collective-permute-start.27 = (bf16[256,2048]{1,0:T(8,128)(2,1)}, bf16[256,2048]{1,0:T(8,128)(2,1)S(1)}, u32[]{:S(2)}, u32[]{:S(2)}) collective-permute-start(bf16[256,2048]{1,0:T(8,128)(2,1)} %fusion.30), channel_id=1, source_target_pairs={{0,8},{8,0},{1,9},{9,1},{2,10},{10,2},{3,11},{11,3},{4,12},{12,4},... | collective-permute-start | bytes 3145736 | tf_op jit(solution)/shard_map/ppermute | solution.py:78
  220.9 27.5 %collective-permute-start.26 = (bf16[256,2048]{1,0:T(8,128)(2,1)}, bf16[256,2048]{1,0:T(8,128)(2,1)}, u32[]{:S(2)}, u32[]{:S(2)}) collective-permute-start(bf16[256,2048]{1,0:T(8,128)(2,1)} %fusion.30), channel_id=1, source_target_pairs={{0,1},{1,0},{2,3},{3,2},{4,5},{5,4},{6,7},{7,6},{8,9},{9,8},{10,11... | collective-permute-start | bytes 3145736 | tf_op jit(solution)/shard_map/ppermute | solution.py:78
  220.9 457.6 %reduce-scatter.12.cloned.1.call-start = ((), (), s32[]{:S(2)}) async-start(), calls=%async_computation.17 | async-start | bytes 5242880 | tf_op jit(solution)/shard_map/reduce_scatter | solution.py:259
  246.9 27.4 %collective-permute-start.32 = (bf16[128,2048]{1,0:T(8,128)(2,1)}, bf16[128,2048]{1,0:T(8,128)(2,1)}, u32[]{:S(2)}, u32[]{:S(2)}) collective-permute-start(bf16[128,2048]{1,0:T(8,128)(2,1)} %slice.368), channel_id=1, source_target_pairs={{0,16},{16,0},{1,17},{17,1},{2,18},{18,2},{3,19},{19,3},{4,20},{20... | collective-permute-start | bytes 1572872 | tf_op jit(solution)/shard_map/ppermute | solution.py:78
  248.4 54.8 %collective-permute-start.30 = (bf16[256,2048]{1,0:T(8,128)(2,1)S(1)}, bf16[256,2048]{1,0:T(8,128)(2,1)}, u32[]{:S(2)}, u32[]{:S(2)}) collective-permute-start(bf16[256,2048]{1,0:T(8,128)(2,1)S(1)} %collective-permute-done.29), channel_id=1, source_target_pairs={{0,1},{1,0},{2,3},{3,2},{4,5},{5,4},{6,7},{7,6},{8,9},{9,8},{10,11... | collective-permute-start | bytes 3145736 | tf_op jit(solution)/shard_map/ppermute | solution.py:78
  258.8 16.7 %collective-permute-start.28 = (bf16[256,2048]{1,0:T(8,128)(2,1)S(1)}, bf16[256,2048]{1,0:T(8,128)(2,1)S(1)}, u32[]{:S(2)}, u32[]{:S(2)}) collective-permute-start(bf16[256,2048]{1,0:T(8,128)(2,1)S(1)} %copy-done.19), channel_id=1, source_target_pairs={{0,1},{1,0},{2,3},{3,2},{4,5},{5,4},{6,7},{7,6},{8,9},{9,8},{10,11... | collective-permute-start | bytes 3145736 | tf_op jit(solution)/shard_map/ppermute | solution.py:78
  272.1 25.0 %collective-permute-start.12 = (bf16[256,2048]{1,0:T(8,128)(2,1)S(1)}, bf16[256,2048]{1,0:T(8,128)(2,1)S(1)}, u32[]{:S(2)}, u32[]{:S(2)}) collective-permute-start(bf16[256,2048]{1,0:T(8,128)(2,1)S(1)} %pad_maximum_fusion.8), channel_id=1, source_target_pairs={{0,8},{8,0},{1,9},{9,1},{2,10},{10,2},{3,11},{11,3},{4,12},{12,4},... | collective-permute-start | bytes 3145736 | tf_op jit(solution)/shard_map/ppermute | solution.py:78
  273.3 24.3 %collective-permute-start.10 = (bf16[256,2048]{1,0:T(8,128)(2,1)S(1)}, bf16[256,2048]{1,0:T(8,128)(2,1)S(1)}, u32[]{:S(2)}, u32[]{:S(2)}) collective-permute-start(bf16[256,2048]{1,0:T(8,128)(2,1)S(1)} %pad_maximum_fusion.7), channel_id=1, source_target_pairs={{0,16},{16,0},{1,17},{17,1},{2,18},{18,2},{3,19},{19,3},{4,20},{20... | collective-permute-start | bytes 3145736 | tf_op jit(solution)/shard_map/ppermute | solution.py:78
  275.4 31.1 %collective-permute-start.33 = (bf16[256,2048]{1,0:T(8,128)(2,1)S(1)}, bf16[256,2048]{1,0:T(8,128)(2,1)S(1)}, u32[]{:S(2)}, u32[]{:S(2)}) collective-permute-start(bf16[256,2048]{1,0:T(8,128)(2,1)S(1)} %constant_dynamic-update-slice_fusion.5), channel_id=1, source_target_pairs={{0,1},{1,0},{2,3},{3,2},{4,5},{5,4},{6,7},{7,6},{8,9},{9,8},{10,11... | collective-permute-start | bytes 3145736 | tf_op jit(solution)/shard_map/ppermute | solution.py:78
  301.3 23.6 %collective-permute-start.14 = (bf16[256,2048]{1,0:T(8,128)(2,1)S(1)}, bf16[256,2048]{1,0:T(8,128)(2,1)S(1)}, u32[]{:S(2)}, u32[]{:S(2)}) collective-permute-start(bf16[256,2048]{1,0:T(8,128)(2,1)S(1)} %get-tuple-element.33), channel_id=1, source_target_pairs={{0,8},{8,0},{1,9},{9,1},{2,10},{10,2},{3,11},{11,3},{4,12},{12,4},... | collective-permute-start | bytes 3145736 | tf_op jit(solution)/shard_map/ppermute | solution.py:78
  302.6 27.4 %collective-permute-start.13 = (bf16[256,2048]{1,0:T(8,128)(2,1)S(1)}, bf16[256,2048]{1,0:T(8,128)(2,1)S(1)}, u32[]{:S(2)}, u32[]{:S(2)}) collective-permute-start(bf16[256,2048]{1,0:T(8,128)(2,1)S(1)} %get-tuple-element.33), channel_id=1, source_target_pairs={{0,1},{1,0},{2,3},{3,2},{4,5},{5,4},{6,7},{7,6},{8,9},{9,8},{10,11... | collective-permute-start | bytes 3145736 | tf_op jit(solution)/shard_map/ppermute | solution.py:78
  302.6 26.0 %collective-permute-start.16 = (bf16[256,2048]{1,0:T(8,128)(2,1)S(1)}, bf16[256,2048]{1,0:T(8,128)(2,1)S(1)}, u32[]{:S(2)}, u32[]{:S(2)}) collective-permute-start(bf16[256,2048]{1,0:T(8,128)(2,1)S(1)} %get-tuple-element.33), channel_id=1, source_target_pairs={{0,16},{16,0},{1,17},{17,1},{2,18},{18,2},{3,19},{19,3},{4,20},{20... | collective-permute-start | bytes 3145736 | tf_op jit(solution)/shard_map/ppermute | solution.py:78
  324.9 16.9 %collective-permute-start.19 = (bf16[128,2048]{1,0:T(8,128)(2,1)S(1)}, bf16[128,2048]{1,0:T(8,128)(2,1)S(1)}, u32[]{:S(2)}, u32[]{:S(2)}) collective-permute-start(bf16[128,2048]{1,0:T(8,128)(2,1)S(1)} %slice.355), channel_id=1, source_target_pairs={{0,16},{16,0},{1,17},{17,1},{2,18},{18,2},{3,19},{19,3},{4,20},{20... | collective-permute-start | bytes 1572872 | tf_op jit(solution)/shard_map/ppermute | solution.py:78
  409.4 24.2 %collective-permute-start.34 = (bf16[4,256,2048]{2,1,0:T(8,128)(2,1)}, bf16[4,256,2048]{2,1,0:T(8,128)(2,1)}, u32[]{:S(2)}, u32[]{:S(2)}) collective-permute-start(bf16[4,256,2048]{2,1,0:T(8,128)(2,1)} %slice_bitcast_fusion.2), channel_id=1, source_target_pairs={{0,1},{1,0},{2,3},{3,2},{4,5},{5,4},{6,7},{7,6},{8,9},{9,8},{10,11... | collective-permute-start | bytes 12582920 | tf_op jit(solution)/shard_map/ppermute | solution.py:78
  420.4 24.5 %collective-permute-start.21 = (bf16[4,256,2048]{2,1,0:T(8,128)(2,1)}, bf16[4,256,2048]{2,1,0:T(8,128)(2,1)}, u32[]{:S(2)}, u32[]{:S(2)}) collective-permute-start(bf16[4,256,2048]{2,1,0:T(8,128)(2,1)} %slice_bitcast_fusion.4), channel_id=1, source_target_pairs={{0,1},{1,0},{2,3},{3,2},{4,5},{5,4},{6,7},{7,6},{8,9},{9,8},{10,11... | collective-permute-start | bytes 12582920 | tf_op jit(solution)/shard_map/ppermute | solution.py:78
  433.6 267.8 %reduce-scatter.14.cloned.1.call-start = ((), (), s32[]{:S(2)}) async-start(), calls=%async_computation.18 | async-start | bytes 2621440 | tf_op jit(solution)/shard_map/reduce_scatter | solution.py:263
  454.6 14.9 %collective-permute-start.22 = (bf16[128,2048]{1,0:T(8,128)(2,1)S(1)}, bf16[128,2048]{1,0:T(8,128)(2,1)S(1)}, u32[]{:S(2)}, u32[]{:S(2)}) collective-permute-start(bf16[128,2048]{1,0:T(8,128)(2,1)S(1)} %get-tuple-element.69), channel_id=1, source_target_pairs={{0,8},{8,0},{1,9},{9,1},{2,10},{10,2},{3,11},{11,3},{4,12},{12,4},... | collective-permute-start | bytes 1572872 | tf_op jit(solution)/shard_map/ppermute | solution.py:78
  459.8 32.1 %collective-permute-start.38 = (bf16[256,2048]{1,0:T(8,128)(2,1)S(1)}, bf16[256,2048]{1,0:T(8,128)(2,1)S(1)}, u32[]{:S(2)}, u32[]{:S(2)}) collective-permute-start(bf16[256,2048]{1,0:T(8,128)(2,1)S(1)} %pad_maximum_fusion.13), channel_id=1, source_target_pairs={{0,8},{8,0},{1,9},{9,1},{2,10},{10,2},{3,11},{11,3},{4,12},{12,4},... | collective-permute-start | bytes 3145736 | tf_op jit(solution)/shard_map/ppermute | solution.py:78
  461.4 31.1 %collective-permute-start.36 = (bf16[256,2048]{1,0:T(8,128)(2,1)S(1)}, bf16[256,2048]{1,0:T(8,128)(2,1)S(1)}, u32[]{:S(2)}, u32[]{:S(2)}) collective-permute-start(bf16[256,2048]{1,0:T(8,128)(2,1)S(1)} %pad_maximum_fusion.12), channel_id=1, source_target_pairs={{0,16},{16,0},{1,17},{17,1},{2,18},{18,2},{3,19},{19,3},{4,20},{20... | collective-permute-start | bytes 3145736 | tf_op jit(solution)/shard_map/ppermute | solution.py:78
  470.4 43.0 %collective-permute-start.25 = (bf16[256,2048]{1,0:T(8,128)(2,1)S(1)}, bf16[256,2048]{1,0:T(8,128)(2,1)S(1)}, u32[]{:S(2)}, u32[]{:S(2)}) collective-permute-start(bf16[256,2048]{1,0:T(8,128)(2,1)S(1)} %pad_maximum_fusion.11), channel_id=1, source_target_pairs={{0,8},{8,0},{1,9},{9,1},{2,10},{10,2},{3,11},{11,3},{4,12},{12,4},... | collective-permute-start | bytes 3145736 | tf_op jit(solution)/shard_map/ppermute | solution.py:78
  472.0 41.7 %collective-permute-start.23 = (bf16[256,2048]{1,0:T(8,128)(2,1)S(1)}, bf16[256,2048]{1,0:T(8,128)(2,1)S(1)}, u32[]{:S(2)}, u32[]{:S(2)}) collective-permute-start(bf16[256,2048]{1,0:T(8,128)(2,1)S(1)} %pad_maximum_fusion.10), channel_id=1, source_target_pairs={{0,16},{16,0},{1,17},{17,1},{2,18},{18,2},{3,19},{19,3},{4,20},{20... | collective-permute-start | bytes 3145736 | tf_op jit(solution)/shard_map/ppermute | solution.py:78
  517.2 24.0 %collective-permute-start.40 = (bf16[256,2048]{1,0:T(8,128)(2,1)S(1)}, bf16[256,2048]{1,0:T(8,128)(2,1)S(1)}, u32[]{:S(2)}, u32[]{:S(2)}) collective-permute-start(bf16[256,2048]{1,0:T(8,128)(2,1)S(1)} %get-tuple-element.26), channel_id=1, source_target_pairs={{0,8},{8,0},{1,9},{9,1},{2,10},{10,2},{3,11},{11,3},{4,12},{12,4},... | collective-permute-start | bytes 3145736 | tf_op jit(solution)/shard_map/ppermute | solution.py:78
  518.6 27.3 %collective-permute-start.39 = (bf16[256,2048]{1,0:T(8,128)(2,1)S(1)}, bf16[256,2048]{1,0:T(8,128)(2,1)}, u32[]{:S(2)}, u32[]{:S(2)}) collective-permute-start(bf16[256,2048]{1,0:T(8,128)(2,1)S(1)} %get-tuple-element.26), channel_id=1, source_target_pairs={{0,1},{1,0},{2,3},{3,2},{4,5},{5,4},{6,7},{7,6},{8,9},{9,8},{10,11... | collective-permute-start | bytes 3145736 | tf_op jit(solution)/shard_map/ppermute | solution.py:78
  518.6 26.0 %collective-permute-start.42 = (bf16[256,2048]{1,0:T(8,128)(2,1)S(1)}, bf16[256,2048]{1,0:T(8,128)(2,1)S(1)}, u32[]{:S(2)}, u32[]{:S(2)}) collective-permute-start(bf16[256,2048]{1,0:T(8,128)(2,1)S(1)} %get-tuple-element.26), channel_id=1, source_target_pairs={{0,16},{16,0},{1,17},{17,1},{2,18},{18,2},{3,19},{19,3},{4,20},{20... | collective-permute-start | bytes 3145736 | tf_op jit(solution)/shard_map/ppermute | solution.py:78
  541.2 16.7 %collective-permute-start.45 = (bf16[128,2048]{1,0:T(8,128)(2,1)S(1)}, bf16[128,2048]{1,0:T(8,128)(2,1)S(1)}, u32[]{:S(2)}, u32[]{:S(2)}) collective-permute-start(bf16[128,2048]{1,0:T(8,128)(2,1)S(1)} %slice.379), channel_id=1, source_target_pairs={{0,16},{16,0},{1,17},{17,1},{2,18},{18,2},{3,19},{19,3},{4,20},{20... | collective-permute-start | bytes 1572872 | tf_op jit(solution)/shard_map/ppermute | solution.py:78
  545.4 14.8 %collective-permute-start.43 = (bf16[256,2048]{1,0:T(8,128)(2,1)S(1)}, bf16[256,2048]{1,0:T(8,128)(2,1)S(1)}, u32[]{:S(2)}, u32[]{:S(2)}) collective-permute-start(bf16[256,2048]{1,0:T(8,128)(2,1)S(1)} %collective-permute-done.42), channel_id=1, source_target_pairs={{0,1},{1,0},{2,3},{3,2},{4,5},{5,4},{6,7},{7,6},{8,9},{9,8},{10,11... | collective-permute-start | bytes 3145736 | tf_op jit(solution)/shard_map/ppermute | solution.py:78
  572.5 31.9 %all-to-all-start.4 = ((bf16[2,256,2048]{2,1,0:T(8,128)(2,1)}), bf16[2,256,2048]{2,1,0:T(8,128)(2,1)}, u32[]{:S(2)}, u32[]{:S(2)}) async-start(bf16[2,256,2048]{2,1,0:T(8,128)(2,1)} %bitcast.147), calls=%async_computation.5 | async-start | bytes 4194304 | tf_op jit(solution)/shard_map/all_to_all | solution.py:272
  577.4 134.6 %reduce-scatter.10.cloned.1.call-start = ((), (), s32[]{:S(2)}) async-start(), calls=%async_computation.16 | async-start | bytes 2621440 | tf_op jit(solution)/shard_map/reduce_scatter | solution.py:273
  604.5 153.5 %reduce-scatter.8.cloned.1.call-start = ((), (), s32[]{:S(2)}) async-start(), calls=%async_computation.15 | async-start | bytes 7864320 | tf_op jit(solution)/shard_map/reduce_scatter | solution.py:259
  676.2 15.0 %collective-permute-start.48 = (bf16[128,2048]{1,0:T(8,128)(2,1)}, bf16[128,2048]{1,0:T(8,128)(2,1)S(1)}, u32[]{:S(2)}, u32[]{:S(2)}) collective-permute-start(bf16[128,2048]{1,0:T(8,128)(2,1)} %get-tuple-element.61), channel_id=1, source_target_pairs={{0,8},{8,0},{1,9},{9,1},{2,10},{10,2},{3,11},{11,3},{4,12},{12,4},... | collective-permute-start | bytes 1572872 | tf_op jit(solution)/shard_map/ppermute | solution.py:78
  677.1 14.9 %collective-permute-start.50 = (bf16[128,2048]{1,0:T(8,128)(2,1)S(1)}, bf16[128,2048]{1,0:T(8,128)(2,1)}, u32[]{:S(2)}, u32[]{:S(2)}) collective-permute-start(bf16[128,2048]{1,0:T(8,128)(2,1)S(1)} %get-tuple-element.62), channel_id=1, source_target_pairs={{0,16},{16,0},{1,17},{17,1},{2,18},{18,2},{3,19},{19,3},{4,20},{20... | collective-permute-start | bytes 1572872 | tf_op jit(solution)/shard_map/ppermute | solution.py:78
  678.5 25.0 %all-to-all-start.5 = ((bf16[8,64,1024]{2,1,0:T(8,128)(2,1)}), bf16[8,64,1024]{2,1,0:T(8,128)(2,1)S(1)}, u32[]{:S(2)}, u32[]{:S(2)}) async-start(bf16[8,64,1024]{2,1,0:T(8,128)(2,1)} %bitcast.429), calls=%async_computation.8 | async-start | bytes 2097152 | tf_op jit(solution)/shard_map/all_to_all | solution.py:142
  695.3 29.3 %collective-permute-start.51 = (bf16[256,2048]{1,0:T(8,128)(2,1)}, bf16[256,2048]{1,0:T(8,128)(2,1)}, u32[]{:S(2)}, u32[]{:S(2)}) collective-permute-start(bf16[256,2048]{1,0:T(8,128)(2,1)} %pad_maximum_fusion.15), channel_id=1, source_target_pairs={{0,8},{8,0},{1,9},{9,1},{2,10},{10,2},{3,11},{11,3},{4,12},{12,4},... | collective-permute-start | bytes 3145736 | tf_op jit(solution)/shard_map/ppermute | solution.py:78
  700.3 24.6 %collective-permute-start.49 = (bf16[256,2048]{1,0:T(8,128)(2,1)}, bf16[256,2048]{1,0:T(8,128)(2,1)}, u32[]{:S(2)}, u32[]{:S(2)}) collective-permute-start(bf16[256,2048]{1,0:T(8,128)(2,1)} %pad_maximum_fusion.14), channel_id=1, source_target_pairs={{0,16},{16,0},{1,17},{17,1},{2,18},{18,2},{3,19},{19,3},{4,20},{20... | collective-permute-start | bytes 3145736 | tf_op jit(solution)/shard_map/ppermute | solution.py:78
  758.0 149.0 %all-to-all-start.3 = ((bf16[8,64,1536]{2,1,0:T(8,128)(2,1)}), bf16[8,64,1536]{2,1,0:T(8,128)(2,1)}, u32[]{:S(2)}, u32[]{:S(2)}) async-start(bf16[8,64,1536]{2,1,0:T(8,128)(2,1)} %bitcast.428), calls=%async_computation.4 | async-start | bytes 3145728 | tf_op jit(solution)/shard_map/all_to_all | solution.py:142
  762.3 141.3 %reduce-scatter.16.cloned.1.call-start = ((), (), s32[]{:S(2)}) async-start(), calls=%async_computation.19 | async-start | bytes 1081344
  (94 other events, 1270.1 us)
Sparse Core Ops, SparseCore 0:
  9.6 48.3 all-gather.7
  59.5 114.3 all-gather.5
  176.1 78.9 all-gather.9
  256.6 44.1 all-gather.11
  433.7 74.2 reduce-scatter.11
  525.4 41.1 reduce-scatter.13
  604.6 41.1 reduce-scatter.9
  648.0 109.9 reduce-scatter.7
  765.9 137.6 reduce-scatter.15

commit v2 on v1

v2 whole, which is shorter than its diff:
```python
import math

import jax
import jax.numpy as jnp
from jax import lax
from jax.experimental import pallas as pl
from jax.experimental.pallas import tpu as pltpu
from jax.sharding import Mesh, PartitionSpec as P

HEADS = 8
KEY = 256
VAL = 512
EPSILON = 1e-05
RETAIN_EPSILON = 0.05
SCALE = KEY ** (-0.5)

EVERY = ("y", "x", "z", "core")
MEMBERS = ("y", "x", "core")
GROUP = 8
F32 = jnp.float32
BF16 = jnp.bfloat16


def dot(left, right):
    return jnp.dot(left, right, preferred_element_type=F32)


def dot_rows(left, right):
    return lax.dot_general(left, right, (((0,), (0,)), ((), ())), preferred_element_type=F32)


def dot_back(left, right):
    return lax.dot_general(left, right, (((1,), (1,)), ((), ())), preferred_element_type=F32)


def statistics(field_in, offset):
    centred = field_in - jnp.mean(field_in, axis=-1, keepdims=True)
    inverse = lax.rsqrt(jnp.mean(centred * centred, axis=-1, keepdims=True) + offset)
    return centred * inverse, inverse


def pull_back(hat, inverse, grad):
    return inverse * (
        grad
        - jnp.mean(grad, axis=-1, keepdims=True)
        - hat * jnp.mean(grad * hat, axis=-1, keepdims=True)
    )


def rotation_tables(length):
    half_width = KEY // 2
    columns = jnp.arange(half_width).astype(F32)
    angles = jnp.exp(-math.log(10000.0) * columns / (half_width - 1))
    zeta_scale = (2.0 * columns + 0.4 * KEY) / (1.4 * KEY)
    places = jnp.arange(length).astype(F32)[:, None]
    phases = places * angles[None, :]
    tables = []
    for direction in (1.0, -1.0):
        growth = jnp.exp(direction * places / 512.0 * jnp.log(zeta_scale)[None, :])
        tables += [jnp.cos(phases) * growth, jnp.sin(phases) * growth]
    return jnp.stack(tables)


def decay_mask(length, head):
    log_decay = jnp.log(1.0 - jnp.exp2(-5.0 - head.astype(F32)))
    places = jnp.arange(length)
    distance = (places[:, None] - places[None, :]).astype(F32)
    decayed = jnp.where(distance >= 0.0, jnp.exp(log_decay * jnp.maximum(distance, 0.0)), 0.0)
    return decayed * lax.rsqrt(jnp.sum(decayed, axis=-1, keepdims=True))


def read_rows(refs):
    return jnp.concatenate([ref[...] for ref in refs], axis=0) if len(refs) > 1 else refs[0][...]


def turn(field_in, cosine, sine):
    first, second = field_in[:, : KEY // 2], field_in[:, KEY // 2 :]
    return jnp.concatenate([first * cosine - second * sine, second * cosine + first * sine], axis=1)


def turn_back(field_in, cosine, sine):
    first, second = field_in[:, : KEY // 2], field_in[:, KEY // 2 :]
    return jnp.concatenate([first * cosine + second * sine, second * cosine - first * sine], axis=1)


def whole_spec(array):
    zeros = (0,) * array.ndim
    return pl.BlockSpec(array.shape, lambda i: zeros, pipeline_mode=pl.Buffered(1))


def pair_spec(shape, number):
    return pl.BlockSpec((2,) + shape, lambda i: (number,) + (0,) * len(shape))


def chunk_call(body_fn, name, number, pieces, shared, saved_in, buffers, shapes, parts, flops, tokens=()):
    flat = [piece for side in pieces for piece in side]
    counts = [len(side) for side in pieces]
    total = len(flat) + len(shared) + len(saved_in)
    carried = [] if buffers is None else list(buffers)

    def kernel(*refs):
        sides, at = [], 0
        for count in counts:
            sides.append(refs[at : at + count])
            at += count
        body_fn(sides, refs[at : at + len(shared)], refs[at + len(shared) : total], refs[total + len(carried) + len(tokens) :])

    outs = [jax.ShapeDtypeStruct((GROUP,) + shape, dtype) for shape, dtype in shapes]
    outs += [jax.ShapeDtypeStruct(shape, dtype) for shape, dtype in parts]
    operands = [*flat, *shared, *saved_in, *carried, *tokens]
    size = sum(math.prod(o.shape) * o.dtype.itemsize for o in [*flat, *shared])
    return pl.pallas_call(
        kernel,
        grid=(1,),
        out_shape=outs,
        in_specs=[whole_spec(o) for o in [*flat, *shared]]
        + [pair_spec(o.shape[1:], number) for o in saved_in]
        + [pl.BlockSpec(memory_space=pl.ANY) for _ in [*carried, *tokens]],
        out_specs=[pair_spec(shape, number) for shape, _ in shapes]
        + [pl.BlockSpec(shape, lambda i: (0, 0)) for shape, _ in parts],
        input_output_aliases={total + i: i for i in range(len(carried))},
        compiler_params=pltpu.CompilerParams(vmem_limit_bytes=56 * 1024 * 1024),
        cost_estimate=pl.CostEstimate(flops=flops, bytes_accessed=size, transcendentals=0),
        name=name,
    )(*operands)


def mixer_forward(sides, shared, saved_in, outs):
    features, tables, decay, weight, weight_o = shared
    normed_out, qkv_out, gate_out, gated_out = outs[:4]
    parts = outs[4:]
    cos_q, sin_q, cos_k, sin_k = (tables[i] for i in range(4))
    for s, side in enumerate(sides):
        hat, _ = statistics(read_rows(side).astype(F32), EPSILON)
        normed = (hat * features[0:1, :] + features[1:2, :]).astype(BF16)
        normed_out[s] = normed
        projected = dot(normed, weight[...])
        query_low = turn(projected[:, :KEY], cos_q, sin_q).astype(BF16)
        key_low = turn(projected[:, KEY : 2 * KEY], cos_k, sin_k).astype(BF16)
        value_low = projected[:, 2 * KEY : 2 * KEY + VAL].astype(BF16)
        gate = projected[:, 2 * KEY + VAL :]
        weighted = dot_back(query_low, key_low) * SCALE * decay[...]
        shaped = weighted * lax.rsqrt(1.0 + jnp.sum(weighted * weighted, axis=-1, keepdims=True))
        retained = dot(shaped.astype(BF16), value_low)
        retained_hat, _ = statistics(retained, RETAIN_EPSILON)
        qkv_out[s, :, :KEY] = query_low
        qkv_out[s, :, KEY : 2 * KEY] = key_low
        qkv_out[s, :, 2 * KEY :] = value_low
        gate_out[s] = gate
        gated = (gate * jax.nn.sigmoid(gate) * retained_hat).astype(BF16)
        gated_out[s] = gated
        parts[s][...] = dot(gated, weight_o[...]).astype(BF16)


def mixer_backward(sides, shared, saved_in, outs):
    tables, decay_ref, weight, weight_o = shared
    qkv, gate_ref = saved_in
    og_out, qk_out, vg_out = outs[:3]
    parts = outs[3:]
    cos_q, sin_q, cos_k, sin_k = (tables[i] for i in range(4))
    decay = decay_ref[...]
    for s, side in enumerate(sides):
        out_grad = read_rows(side)
        og_out[s] = out_grad
        gated_grad = dot_back(out_grad, weight_o[...])
        query_low = qkv[s, :, :KEY]
        key_low = qkv[s, :, KEY : 2 * KEY]
        value_low = qkv[s, :, 2 * KEY :]
        weighted = dot_back(query_low, key_low) * SCALE * decay
        inverse_c = lax.rsqrt(1.0 + jnp.sum(weighted * weighted, axis=-1, keepdims=True))
        shaped_low = (weighted * inverse_c).astype(BF16)
        retained_hat, inverse = statistics(dot(shaped_low, value_low), RETAIN_EPSILON)
        gate = gate_ref[s]
        sig = jax.nn.sigmoid(gate)
        gate_grad = (gated_grad * retained_hat * (sig * (1.0 + gate * (1.0 - sig)))).astype(BF16)
        retained_low = pull_back(retained_hat, inverse, gated_grad * (gate * sig)).astype(BF16)
        value_grad = dot_rows(shaped_low, retained_low).astype(BF16)
        shaped_grad = dot_back(retained_low, value_low)
        row_sum = jnp.sum(shaped_grad * weighted, axis=-1, keepdims=True)
        cubed = inverse_c * inverse_c * inverse_c
        score_grad = (decay * (shaped_grad * inverse_c - weighted * (row_sum * cubed))).astype(BF16)
        query_grad = turn_back(dot(score_grad, key_low) * SCALE, cos_q, sin_q).astype(BF16)
        key_grad = turn_back(dot_rows(score_grad, query_low) * SCALE, cos_k, sin_k).astype(BF16)
        both = jnp.concatenate([query_grad, key_grad], axis=1)
        value_gate = jnp.concatenate([value_grad, gate_grad], axis=1)
        qk_out[s] = both
        vg_out[s] = value_gate
        parts[s][...] = dot_back(jnp.concatenate([both, value_gate], axis=1), weight[...]).astype(BF16)


def feed_forward(sides, shared, saved_in, outs):
    (weight,) = shared
    normed_out, act_out, slopes_out, done = outs
    hidden = act_out.shape[2]
    done[...] = jnp.zeros_like(done)
    for s, side in enumerate(sides):
        normed = read_rows(side)
        normed_out[s] = normed
        pre = dot(normed, weight[...])
        gate_pre, up_pre = pre[:, :hidden], pre[:, hidden:]
        phi = 0.5 * (1.0 + lax.erf(gate_pre * math.sqrt(0.5)))
        gelu = gate_pre * phi
        slope = phi + gate_pre * (jnp.exp(-0.5 * gate_pre * gate_pre) * (1.0 / math.sqrt(2.0 * math.pi)))
        act_out[s] = (gelu * up_pre).astype(BF16)
        slopes_out[s, :, :hidden] = up_pre * slope
        slopes_out[s, :, hidden:] = gelu


def feed_backward(sides, shared, saved_in, outs):
    weight, down = shared
    act_ref, slopes, upstream_ref = saved_in
    pre_out = outs[0]
    feed_parts, normed_parts = outs[1:3], outs[3:5]
    for s in range(2):
        act_grad = dot_back(upstream_ref[s], down[...])
        low = (jnp.concatenate([act_grad, act_grad], axis=1) * slopes[s]).astype(BF16)
        pre_out[s] = low
        normed_parts[s][...] = dot_back(low, weight[...]).astype(BF16)
        feed_parts[s][...] = dot(act_ref[s], down[...]).astype(BF16)


def swap(field_in, axis):
    return lax.ppermute(field_in, axis, [(0, 1), (1, 0)])


def swap_both(field_in, axes):
    return lax.ppermute(field_in, axes, [(0, 3), (1, 2), (2, 1), (3, 0)])


def after(values, *tokens):
    anywhere = pl.BlockSpec(memory_space=pl.ANY)
    held = pl.pallas_call(
        lambda *refs: None,
        out_shape=[jax.ShapeDtypeStruct(v.shape, v.dtype) for v in values],
        in_specs=[anywhere] * (len(values) + len(tokens)),
        out_specs=[anywhere] * len(values),
        input_output_aliases={i: i for i in range(len(values))},
        cost_estimate=pl.CostEstimate(flops=0, bytes_accessed=0, transcendentals=0),
        name="after",
    )(*values, *tokens)
    return list(held)


def pair_up(pieces):
    return pieces, [swap(piece, "core") for piece in pieces]


def spread(own):
    half = own.shape[0] // 2
    from_x = swap(own, "x")
    from_y = swap(own, "y")
    upper = swap(from_y[:half], "x")
    lower = swap(from_x[half:], "y")
    return [pair_up(pieces) for pieces in ([own], [from_x], [from_y], [upper, lower])]


def chunks_in_turn(own, call):
    half = own.shape[0] // 2
    from_x = swap(own, "x")
    from_y = swap(own, "y")
    results = [call(0, pair_up([own]), [])]
    from_x, from_y = after([from_x, from_y], results[0][-1])
    upper = swap(from_y[:half], "x")
    lower = swap(from_x[half:], "y")
    chunk_x, chunk_y = pair_up([from_x]), pair_up([from_y])
    results.append(call(1, chunk_x, results))
    across = after([upper, lower], results[1][-1])
    chunk_across = pair_up(across)
    results.append(call(2, chunk_y, results))
    results.append(call(3, chunk_across, results))
    return results


def two_cores(pair):
    return pair[0].astype(F32) + swap(pair[1], "core").astype(F32)


def send(number, summed):
    summed = summed.astype(BF16)
    if number == 3:
        return swap_both(summed, ("y", "x"))
    return swap(summed, ("x", "y")[number - 1])


def add_up(own, arrived):
    return own + arrived[1].astype(F32) + arrived[2].astype(F32) + arrived[3].astype(F32)


def body(
    tokens,
    lengths,
    dealing,
    cotangent,
    query_weight,
    key_weight,
    value_weight,
    gate_weight,
    mixer_gain,
    mixer_bias,
    output_weight,
    feed_gate,
    feed_up,
    feed_down,
    feed_gain,
    feed_bias,
):
    _, length, breadth = tokens.shape
    layers = lax.axis_size("z")
    devices = 8 * layers
    local_model = query_weight.shape[0]
    local_hidden = feed_down.shape[0]
    local_value = output_weight.shape[0]
    hidden = local_hidden * layers
    half_layers = layers // 2
    fsdp_index = lax.axis_index("y") * 2 + lax.axis_index("x")
    core = lax.axis_index("core")
    layer = lax.axis_index("z")
    head = fsdp_index * 2 + core

    def to_members(packed, axes=MEMBERS):
        return lax.all_to_all(packed, axes, 0, 0, tiled=True)

    def gather_layers(mine):
        return lax.all_gather(
            mine.reshape(4, 2 * local_model, -1), "z", axis=1, tiled=True
        ).reshape(breadth, -1)

    def value_columns(weight):
        split = weight.reshape(local_model, 4, 2, half_layers, 2, local_value)
        return split.transpose(1, 2, 0, 4, 3, 5).reshape(GROUP, local_model, VAL)

    def head_columns(weight):
        return weight.reshape(local_model, HEADS, KEY).transpose(1, 0, 2)

    def hidden_columns(weight):
        split = weight.reshape(local_model, 4, layers, 2, local_hidden)
        return split.transpose(1, 3, 0, 2, 4).reshape(GROUP, local_model, hidden)

    weight_o = lax.all_gather(output_weight, "z", axis=0, tiled=True)
    mixer_mine = to_members(
        jnp.concatenate(
            [
                head_columns(query_weight),
                head_columns(key_weight),
                value_columns(value_weight),
                value_columns(gate_weight),
            ],
            axis=2,
        )
    )
    mixer_weight = gather_layers(mixer_mine)
    feed_packed = jnp.concatenate([hidden_columns(feed_gate), hidden_columns(feed_up)], axis=2)
    feed_mine = to_members(feed_packed)
    feed_weight = gather_layers(feed_mine)
    down_weight = lax.all_gather(feed_down, "z", axis=0, tiled=True)
    weight_o = to_members(weight_o, "core")

    vectors = jnp.stack([mixer_gain, mixer_bias, feed_gain, feed_bias])
    features = to_members(jnp.broadcast_to(vectors[None], (devices,) + vectors.shape), EVERY)
    features = features.transpose(1, 0, 2).reshape(4, breadth).astype(F32)

    slot_bits = []
    for bits_c in range(2):
        numbers = [
            ((fsdp_index ^ bits_f) * layers + layer) * 2 + (core ^ bits_c) for bits_f in range(4)
        ]
        slot_bits.append([fsdp_index ^ (dealing[n] // (2 * layers)) for n in numbers])
    sequence_in = []
    for slot in range(4):
        for bits_c in range(2):
            found = jnp.int32(0)
            for bits_f in range(1, 4):
                found = jnp.where(slot_bits[bits_c][bits_f] == slot, bits_f, found)
            sequence_in.append(found * 2 + bits_c)
    own_slot = slot_bits[0][0]

    places = jnp.arange(length, dtype=jnp.int32)
    live_mask = (places < lengths[0]).astype(F32)[:, None]
    upstream_own = (cotangent[0].astype(F32) * live_mask).astype(BF16)
    upstream_blocks = jnp.stack(
        [read for chunk in spread(upstream_own) for read in map(join, chunk)]
    )
    upstream_all = jnp.stack(
        [lax.dynamic_index_in_dim(upstream_blocks, n, 0, keepdims=False) for n in sequence_in]
    )

    tables = rotation_tables(length)
    decay = decay_mask(length, head)
    row_bytes = (length, breadth)
    saved, summed, arrived = None, [None] * 4, [None] * 4
    token_chunks = spread(tokens[0])
    order = (3, 1, 2, 0)
    for i, n in enumerate(order):
        results = chunk_call(
            mixer_forward,
            "mixer_forward",
            n,
            token_chunks[n],
            [features[:2], tables, decay, mixer_weight, weight_o],
            [],
            saved,
            [
                ((length, breadth), BF16),
                ((length, 2 * KEY + VAL), BF16),
                ((length, VAL), F32),
                ((length, VAL), BF16),
            ],
            [(row_bytes, BF16)] * 2,
            2 * 2 * length * breadth * 2048,
            [upstream_all] if i < 2 else [summed[order[i - 2]]],
        )
        saved = results[:4]
        summed[n] = two_cores(results[4:6])
        arrived[n] = send(n, summed[n]) if n else None
    mixer_normed, qkv_all, gate_all, gated_all = saved
    arrived[3] = after([arrived[3]], feed_weight)[0]
    hidden_state = tokens[0].astype(F32) + add_up(summed[0], arrived)

    feed_hat, feed_inverse = statistics(hidden_state, EPSILON)
    feed_own = (feed_hat * features[2] + features[3]).astype(BF16)

    def feed_call(n, chunk, earlier):
        return chunk_call(
            feed_forward,
            "feed_forward",
            n,
            chunk,
            [feed_weight],
            [],
            earlier[-1][:3] if earlier else None,
            [((length, breadth), BF16), ((length, hidden), BF16), ((length, 2 * hidden), F32)],
            [((8, 128), F32)],
            2 * 2 * length * breadth * hidden * 2,
            [down_weight] if n == 3 else [],
        )

    saved = chunks_in_turn(feed_own, feed_call)[-1][:3]
    feed_normed, activated, slopes = saved
    down_product = dot_rows(
        activated.reshape(GROUP * length, hidden), upstream_all.reshape(GROUP * length, breadth)
    ).astype(BF16)
    down_grad = lax.psum_scatter(down_product, "z", scatter_dimension=0, tiled=True)

    saved, summed, arrived, feed_parts = None, [None] * 4, [None] * 4, [None] * 4
    for i, n in enumerate(order):
        results = chunk_call(
            feed_backward,
            "feed_backward",
            n,
            [],
            [feed_weight, down_weight],
            [activated, slopes, upstream_all],
            saved,
            [((length, 2 * hidden), BF16)],
            [(row_bytes, BF16)] * 4,
            2 * 2 * length * breadth * hidden * 4,
            [down_product] if i < 2 else [summed[order[i - 2]]],
        )
        saved = results[:1]
        feed_parts[n] = results[1:3]
        summed[n] = two_cores(results[3:5])
        arrived[n] = send(n, summed[n]) if n else None
    feed_product = dot_rows(
        feed_normed.reshape(GROUP * length, breadth),
        saved[0].reshape(GROUP * length, -1),
    ).astype(BF16)
    arrived = [None] + after(arrived[1:], feed_product, down_grad)
    feed_normed_grad = add_up(summed[0], arrived)
    feed_gain_part = jnp.sum(feed_normed_grad * feed_hat, axis=0)
    feed_bias_part = jnp.sum(feed_normed_grad, axis=0)
    state_grad = upstream_all[0].astype(F32) + pull_back(
        feed_hat, feed_inverse, feed_normed_grad * features[2]
    )
    own_grad_low = state_grad.astype(BF16)

    def sum_layers(grads):
        return lax.psum_scatter(
            grads.reshape(4, -1, grads.shape[-1]), "z", scatter_dimension=1, tiled=True
        )

    def to_owners(mine):
        return to_members(mine.reshape(GROUP, local_model, -1)).astype(F32)

    feed_summed = sum_layers(feed_product)
    feed_grads = to_owners(feed_summed)

    summed, grad_parts = [None] * 4, [None] * 4

    def backward_call(n, chunk, earlier):
        if n == 3:
            summed[1] = two_cores(earlier[1][3:5])
        return chunk_call(
            mixer_backward,
            "mixer_backward",
            n,
            chunk,
            [tables, decay, mixer_weight, weight_o],
            [qkv_all, gate_all],
            earlier[-1][:3] if earlier else None,
            [((length, breadth), BF16), ((length, 2 * KEY), BF16), ((length, 2 * VAL), BF16)],
            [(row_bytes, BF16)] * 2,
            2 * 2 * length * breadth * 2304,
            [summed[1], feed_summed] if n == 3 else [],
        )

    results = chunks_in_turn(own_grad_low, backward_call)
    saved = results[-1][:3]
    grad_parts = [result[3:5] for result in results]
    summed = [summed[1] if n == 1 else two_cores(grad_parts[n]) for n in range(4)]
    arrived = [None] + [send(n, summed[n]) for n in range(1, 4)]
    out_grad, qk_grad, vg_grad = (a.reshape(GROUP * length, -1) for a in saved)

    normed_rows = mixer_normed.reshape(GROUP * length, breadth)
    qk_product = dot_rows(normed_rows, qk_grad).astype(BF16)
    vg_product = dot_rows(normed_rows, vg_grad).astype(BF16)
    out_product = dot_rows(gated_all.reshape(GROUP * length, VAL), out_grad).astype(BF16)
    qk_grads = to_owners(sum_layers(qk_product))
    vg_grads = to_owners(sum_layers(vg_product))
    output_grad = lax.psum_scatter(
        to_members(out_product, "core"), "z", scatter_dimension=0, tiled=True
    ).astype(F32)

    held = after([part for pair in feed_parts for part in pair], grad_parts[1][0])
    feed_parts = [held[2 * n : 2 * n + 2] for n in range(4)]
    feed_terms = [two_cores(pair) for pair in feed_parts]
    feed_arrived = [None] + after([send(n, feed_terms[n]) for n in range(1, 4)], out_product)
    slot_out = (hidden_state + add_up(feed_terms[0], feed_arrived)).astype(BF16)
    half = length // 2
    from_x, from_y = swap(slot_out, "x"), swap(slot_out, "y")
    across = jnp.concatenate([swap(from_y[:half], "x"), swap(from_x[half:], "y")], axis=0)
    reached = jnp.stack([slot_out, from_x, from_y, across])
    chosen = lax.dynamic_index_in_dim(reached, own_slot, 0, keepdims=False)
    out_tokens = (live_mask * chosen.astype(F32)).astype(BF16)

    arrived = [None] + after(arrived[1:], out_product)
    mixer_normed_grad = add_up(summed[0], arrived)
    mixer_hat, mixer_inverse = statistics(tokens[0].astype(F32), EPSILON)
    mixer_gain_part = jnp.sum(mixer_normed_grad * mixer_hat, axis=0)
    mixer_bias_part = jnp.sum(mixer_normed_grad, axis=0)
    input_grad = (
        state_grad + pull_back(mixer_hat, mixer_inverse, mixer_normed_grad * features[0])
    ).astype(BF16)

    def vector_grads(*grads):
        split = jnp.stack(grads).reshape(len(grads), devices, -1).transpose(1, 0, 2)
        return jnp.sum(to_members(split, EVERY), axis=0)

    feed_vectors = vector_grads(feed_gain_part, feed_bias_part)
    mixer_vectors = vector_grads(mixer_gain_part, mixer_bias_part)

    def head_back(grads):
        return grads.transpose(1, 0, 2).reshape(local_model, -1)

    def value_back(grads):
        split = grads.reshape(4, 2, local_model, 2, half_layers, local_value)
        return split.transpose(2, 0, 1, 4, 3, 5).reshape(local_model, -1)

    def hidden_back(grads):
        split = grads.reshape(4, 2, local_model, layers, local_hidden)
        return split.transpose(2, 0, 3, 1, 4).reshape(local_model, -1)

    return (
        out_tokens[None],
        input_grad[None],
        head_back(qk_grads[..., :KEY]),
        head_back(qk_grads[..., KEY:]),
        value_back(vg_grads[..., :VAL]),
        value_back(vg_grads[..., VAL:]),
        mixer_vectors[0],
        mixer_vectors[1],
        output_grad,
        hidden_back(feed_grads[..., :hidden]),
        hidden_back(feed_grads[..., hidden:]),
        down_grad.astype(F32),
        feed_vectors[0],
        feed_vectors[1],
    )


def join(pieces):
    return jnp.concatenate(pieces, axis=0) if len(pieces) > 1 else pieces[0]


def solution(mesh):
    layers = mesh.shape["dp"] // 2
    fine = Mesh(mesh.devices.reshape(2, 2, layers, 2), EVERY)
    sequences = P(EVERY, None, None)
    rows = P(EVERY, None)
    vector = P(EVERY)
    in_specs = (
        (sequences, vector, P(), sequences)
        + (rows,) * 4
        + (vector,) * 2
        + (rows,) * 4
        + (vector,) * 2
    )
    out_specs = (sequences,) * 2 + (rows,) * 4 + (vector,) * 2 + (rows,) * 4 + (vector,) * 2
    return jax.shard_map(body, mesh=fine, in_specs=in_specs, out_specs=out_specs, check_vma=False)
```

time: 935 us -> 828 us (0.89)
  Pallas kernels: 0 us -> 169 us
  matrix products: 166 us -> 57.4 us
  waiting for transfers between devices: 377 us -> 293 us
  blocking collectives: 70.2 us -> 26.2 us
  other arithmetic: 103 us -> 75.4 us
  local copies, waits for them, and re-layouts: 111 us -> 85.5 us
  starting transfers between devices: 60.7 us -> 77.6 us
    pallas_call x0 -> x25, Pallas kernels: none -> 169 us  [the longest x16 169 us: chunk_call(): pl.pallas_call(kernel, grid=(1,), out_shape=outs, in_specs=[whole_spec(o)...]
    unnamed x10 -> x9, waiting for transfers between devices: 136 us -> 0.81 us
    dot_general x14 -> x0, matrix products: 113 us -> none  [the longest x4 60.8 us: dot_back(): lax.dot_general(left, right, (((1,), (1,)), ((), ())), preferred_element_...]
    all_to_all x5 -> x9, waiting for transfers between devices: 0.01 us -> 100 us  [to_members(): return lax.all_to_all(packed, axes, 0, 0, tiled=True)]
    ppermute x52 -> x64, waiting for transfers between devices: 192 us -> 133 us  [swap(): return lax.ppermute(field_in, axis, [(0, 1), (1, 0)])]
    all_gather x1 -> x0, blocking collectives: 44.1 us -> none  [body(): lax.all_gather(jnp.stack([mixer_gain, mixer_bias, feed_gain, feed_bias]),...]
    another operation x10 -> x4, other arithmetic: 35.5 us -> 3.23 us  [the longest x1 1.27 us: body(): reached = jnp.stack([slot_out, from_x, from_y, across])]
    ppermute x0 -> x4, waiting for transfers between devices: none -> 32.2 us  [swap_both(): return lax.ppermute(field_in, axes, [(0, 3), (1, 2), (2, 1), (3, 0)])]
  transfers between devices with their start and end apart: 66 -> 86, of which waited for: 29 -> 33; matrix products, arithmetic and copies ran while one was open for 33% -> 22% of each run, Pallas kernels for 0% -> 17%
where the time goes in v2:
time: 828 us; the launch traced here: 819 us
  waiting for transfers between devices  293 us (35%)
  Pallas kernels  169 us (20%)
  local copies, waits for them, and re-layouts  85.5 us (10%)
  starting transfers between devices  77.6 us (9%)
  other arithmetic  75.4 us (9%)
  matrix products  57.4 us (7%)
  between operations  34.6 us (4%)
  blocking collectives  26.2 us (3%)
    pallas_call x16, Pallas kernels, chunk_call(): pl.pallas_call(kernel, grid=(1,), out_shape=outs, in_specs=[whole_spec(o)...  169 us
    ppermute x64, waiting for transfers between devices, swap(): return lax.ppermute(field_in, axis, [(0, 1), (1, 0)])  133 us
    all_to_all x9, waiting for transfers between devices, to_members(): return lax.all_to_all(packed, axes, 0, 0, tiled=True)  100 us
    dot_general x5, matrix products, dot_rows(): lax.dot_general(left, right, (((0,), (0,)), ((), ())), preferred_element_...  57.4 us
    unnamed x125, local copies, waits for them, and re-layouts  39.1 us
    ppermute x64, starting transfers between devices, swap(): return lax.ppermute(field_in, axis, [(0, 1), (1, 0)])  36 us
    all_to_all x9, starting transfers between devices, to_members(): return lax.all_to_all(packed, axes, 0, 0, tiled=True)  32.3 us
    ppermute x4, waiting for transfers between devices, swap_both(): return lax.ppermute(field_in, axes, [(0, 3), (1, 2), (2, 1), (3, 0)])  32.2 us
  transfers between devices with their start and end apart: 86, of which 33 were waited for; matrix products, arithmetic and copies ran while one was open for 22% of the time, Pallas kernels for 17%

profile of v2, /device:TPU:0, one launch (start us, length us, event | category | flops | bytes accessed | tf_op | source)
XLA Modules:
  0.0 818.6 jit_solution(14580376445601587261)
XLA Ops:
  12.3 26.2 %all_to_all.63 = bf16[8,64,1536]{2,1,0:T(8,128)(2,1)} all-to-all(bf16[8,64,1536]{2,1,0:T(8,128)(2,1)S(1)} %pad_maximum_fusion), channel_id=1, replica_groups=mesh['y'=2,'x'=2,'z'=4,'core'=2] {'y','x','core'}, dimensions={0} | all-to-all | bytes 3145728 | tf_op jit(solution)/shard_map/all_to_all | solution.py:321
  45.3 4.0 all-to-all-start
  73.6 15.3 %all-to-all-done = bf16[32,2,128]{2,1,0:T(2,128)(2,1)S(1)} async-done(((bf16[32,2,128]{2,1,0:T(2,128)(2,1)}), bf16[32,2,128]{2,1,0:T(2,128)(2,1)S(1)}, u32[]{:S(2)}, u32[]{:S(2)}) %all-to-all-start) | async-done | bytes 16416 | tf_op jit(solution)/shard_map/all_to_all | solution.py:321
  96.5 11.3 %all-to-all-done.3 = bf16[8,64,1024]{2,1,0:T(8,128)(2,1)S(1)} async-done(((bf16[8,64,1024]{2,1,0:T(8,128)(2,1)}), bf16[8,64,1024]{2,1,0:T(8,128)(2,1)S(1)}, u32[]{:S(2)}, u32[]{:S(2)}) %all-to-all-start.3) | async-done | bytes 1048608 | tf_op jit(solution)/shard_map/all_to_all | solution.py:321
  125.5 5.5 collective-permute-done.15
  131.1 10.9 %collective-permute-done.6.refs_1_ = bf16[128,2048]{1,0:T(8,128)(2,1)} collective-permute-done((bf16[128,2048]{1,0:T(8,128)(2,1)S(1)}, bf16[128,2048]{1,0:T(8,128)(2,1)}, u32[]{:S(2)}, u32[]{:S(2)}) %collective-permute-start.6) | collective-permute-done | bytes 524320 | tf_op jit(solution)/shard_map/ppermute | solution.py:223
  166.6 7.3 all-gather.5.cloned.1.call-done
  174.0 12.0 %mixer_forward.4 = (bf16[8,256,2048]{2,1,0:T(8,128)(2,1)}, bf16[8,256,1024]{2,1,0:T(8,128)(2,1)}, f32[8,256,512]{2,1,0:T(8,128)}, bf16[8,256,512]{2,1,0:T(8,128)...) custom-call(bf16[128,2048]{1,0:T(8,128)(2,1)} %collective-permute-done.5.refs_0_, ...), custom_call_target="tpu_custom_call" | custom-call | flops 4294967296 | bytes 11288576 | tf_op jit(solution)/shard_map/mixer_forward/pallas_call | solution.py:112
  186.5 12.0 %mixer_forward.5 = (bf16[8,256,2048]{2,1,0:T(8,128)(2,1)}, bf16[8,256,1024]{2,1,0:T(8,128)(2,1)}, f32[8,256,512]{2,1,0:T(8,128)}, bf16[8,256,512]{2,1,0:T(8,128)...) custom-call(bf16[256,2048]{1,0:T(8,128)(2,1)} %collective-permute-do, ...), custom_call_target="tpu_custom_call", output_to_operand_aliasing={{0}: (7, {}), {1}: (8, {}), {2}: (9, {}), {3}: (10, {})} | custom-call | flops 4294967296 | bytes 11288576 | tf_op jit(solution)/shard_map/mixer_forward/pallas_call | solution.py:112
  201.8 12.4 %mixer_forward.6 = (bf16[8,256,2048]{2,1,0:T(8,128)(2,1)}, bf16[8,256,1024]{2,1,0:T(8,128)(2,1)}, f32[8,256,512]{2,1,0:T(8,128)}, bf16[8,256,512]{2,1,0:T(8,128)...) custom-call(bf16[256,2048]{1,0:T(8,128)(2,1)} %collective-permute-do, ...), custom_call_target="tpu_custom_call", output_to_operand_aliasing={{0}: (7, {}), {1}: (8, {}), {2}: (9, {}), {3}: (10, {})} | custom-call | flops 4294967296 | bytes 11288576 | tf_op jit(solution)/shard_map/mixer_forward/pallas_call | solution.py:112
  218.8 12.0 %mixer_forward.7 = (bf16[8,256,2048]{2,1,0:T(8,128)(2,1)}, bf16[8,256,1024]{2,1,0:T(8,128)(2,1)}, f32[8,256,512]{2,1,0:T(8,128)}, bf16[8,256,512]{2,1,0:T(8,128)...) custom-call(bf16[256,2048]{1,0:T(8,128)(2,1)} %bitcast.165, ...), custom_call_target="tpu_custom_call", output_to_operand_aliasing={{0}: (7, {}), {1}: (8, {}), {2}: (9, {}), {3}: (10, {})} | custom-call | flops 4294967296 | bytes 11288576 | tf_op jit(solution)/shard_map/mixer_forward/pallas_call | solution.py:112
  235.7 19.4 %all-gather.9.cloned.1.call-done = bf16[4,512,1024]{2,1,0:T(8,128)(2,1)} async-done(((bf16[4,128,1024]{2,1,0:T(8,128)(2,1)}), bf16[4,512,1024]{2,1,0:T(8,128)(2,1)}) %all-gather.9.cloned.1.call-update) | async-done | bytes 4194320 | tf_op jit(solution)/shard_map/all_gather | solution.py:324
  255.1 10.5 %collective-permute-done.24.refs_0_ = bf16[256,2048]{1,0:T(8,128)(2,1)S(1)} collective-permute-done((bf16[256,2048]{1,0:T(8,128)(2,1)S(1)}, bf16[256,2048]{1,0:T(8,128)(2,1)S(1)}, u32[]{:S(2)}, u32[]{:S(2)}) %collective-permute-start.24) | collective-permute-done | bytes 1048608 | tf_op jit(solution)/shard_map/ppermute | solution.py:227
  266.5 15.3 %collective-permute-done.23 = bf16[256,2048]{1,0:T(8,128)(2,1)} collective-permute-done((bf16[256,2048]{1,0:T(8,128)(2,1)}, bf16[256,2048]{1,0:T(8,128)(2,1)}, u32[]{:S(2)}, u32[]{:S(2)}) %collective-permute-start.23) | collective-permute-done | bytes 1048608 | tf_op jit(solution)/shard_map/ppermute | solution.py:223
  281.9 4.3 fusion.36
  290.8 6.8 feed_forward.4
  297.6 15.1 %collective-permute-done.26.refs_1_ = bf16[256,2048]{1,0:T(8,128)(2,1)S(1)} collective-permute-done((bf16[256,2048]{1,0:T(8,128)(2,1)S(1)}, bf16[256,2048]{1,0:T(8,128)(2,1)S(1)}, u32[]{:S(2)}, u32[]{:S(2)}) %collective-permute-start.26) | collective-permute-done | bytes 1048608 | tf_op jit(solution)/shard_map/ppermute | solution.py:223
  319.7 6.8 feed_forward.5
  332.2 6.9 feed_forward.6
  340.0 6.9 feed_forward.7
  346.9 10.2 %bitcast_convert_fusion.4.refs_5_.refs_6_ = bf16[512,2048]{1,0:T(8,128)(2,1)} fusion(bf16[8,256,512]{2,1,0:T(8,128)(2,1)} %get-tuple-element.152.refs_2_, bf16[8,256,2048]{2,1,0:T(8,128)(2,1)} %dynamic-slice_dynamic-update-slice_fusion.refs_9_.refs_11_.refs_4_), kind=kOutput, calls=%fused_computation.8 | convolution fusion | flops 4296015872 | bytes 12582912 | tf_op jit(solution)/shard_map/dot_general | solution.py:29
  357.0 9.9 %feed_backward.4 = (bf16[8,256,1024]{2,1,0:T(8,128)(2,1)}, bf16[256,2048]{1,0:T(8,128)(2,1)}, bf16[256,2048]{1,0:T(8,128)(2,1)}, bf16[256,2048]{1,0:T(8,128)(2,1)}, bf16[256,2048]{1,0:T(8,128)(2,1)}) custom-call(bf16[2048,1024]{1,0:T(8,128)(2,1)} %bitcast.153, bf16[512,2048]{1,0:T(8,128)(2,1)} %all-gather.11.cloned.1.call-done.refs_8_.refs_1_, ...), custom_call_target="tpu_custom_call" | custom-call | flops 4294967296 | bytes 6291456 | tf_op jit(solution)/shard_map/feed_backward/pallas_call | solution.py:112
  367.5 10.3 %feed_backward.5 = (bf16[8,256,1024]{2,1,0:T(8,128)(2,1)}, bf16[256,2048]{1,0:T(8,128)(2,1)}, bf16[256,2048]{1,0:T(8,128)(2,1)}, bf16[256,2048]{1,0:T(8,128)(2,1)}, bf16[256,2048]{1,0:T(8,128)(2,1)}) custom-call(bf16[2048,1024]{1,0:T(8,128)(2,1)} %bitcast.154, ...), custom_call_target="tpu_custom_call", output_to_operand_aliasing={{0}: (5, {})} | custom-call | flops 4294967296 | bytes 6291456 | tf_op jit(solution)/shard_map/feed_backward/pallas_call | solution.py:112
  380.5 10.2 %feed_backward.6 = (bf16[8,256,1024]{2,1,0:T(8,128)(2,1)}, bf16[256,2048]{1,0:T(8,128)(2,1)}, bf16[256,2048]{1,0:T(8,128)(2,1)}, bf16[256,2048]{1,0:T(8,128)(2,1)}, bf16[256,2048]{1,0:T(8,128)(2,1)}) custom-call(bf16[2048,1024]{1,0:T(8,128)(2,1)} %bitcast.155, ...), custom_call_target="tpu_custom_call", output_to_operand_aliasing={{0}: (5, {})} | custom-call | flops 4294967296 | bytes 6291456 | tf_op jit(solution)/shard_map/feed_backward/pallas_call | solution.py:112
  392.8 10.2 %feed_backward.7 = (bf16[8,256,1024]{2,1,0:T(8,128)(2,1)}, bf16[256,2048]{1,0:T(8,128)(2,1)}, bf16[256,2048]{1,0:T(8,128)(2,1)}, bf16[256,2048]{1,0:T(8,128)(2,1)}, bf16[256,2048]{1,0:T(8,128)(2,1)}) custom-call(bf16[2048,1024]{1,0:T(8,128)(2,1)} %bitcast.156, ...), custom_call_target="tpu_custom_call", output_to_operand_aliasing={{0}: (5, {})} | custom-call | flops 4294967296 | bytes 6291456 | tf_op jit(solution)/shard_map/feed_backward/pallas_call | solution.py:112
  403.0 14.0 %bitcast_convert_fusion.1.refs_3_ = bf16[2048,1024]{1,0:T(8,128)(2,1)} fusion(bf16[8,256,2048]{2,1,0:T(8,128)(2,1)} %get-tuple-element.173, bf16[8,256,1024]{2,1,0:T(8,128)(2,1)} %get-tuple-element.174), kind=kOutput, calls=%fused_computation.1 | convolution fusion | flops 8592031744 | bytes 16777216 | tf_op jit(solution)/shard_map/dot_general | solution.py:29
  422.6 21.7 %collective-permute-done.40.refs_2_ = bf16[256,2048]{1,0:T(8,128)(2,1)S(1)} collective-permute-done((bf16[256,2048]{1,0:T(8,128)(2,1)}, bf16[256,2048]{1,0:T(8,128)(2,1)S(1)}, u32[]{:S(2)}, u32[]{:S(2)}) %collective-permute-start.40) | collective-permute-done | bytes 1048608 | tf_op jit(solution)/shard_map/ppermute | solution.py:227
  444.3 21.5 %collective-permute-done.37.refs_0_ = bf16[256,2048]{1,0:T(8,128)(2,1)} collective-permute-done((bf16[256,2048]{1,0:T(8,128)(2,1)}, bf16[256,2048]{1,0:T(8,128)(2,1)}, u32[]{:S(2)}, u32[]{:S(2)}) %collective-permute-start.37) | collective-permute-done | bytes 1048608 | tf_op jit(solution)/shard_map/ppermute | solution.py:223
  466.4 4.1 multiply_reduce_fusion
  477.6 13.1 %mixer_backward.4 = (bf16[8,256,2048]{2,1,0:T(8,128)(2,1)}, bf16[8,256,512]{2,1,0:T(8,128)(2,1)}, bf16[8,256,1024]{2,1,0:T(8,128)(2,1)}, bf16[256,2048]{1,0:T(8,128)(2,1)}, bf16[256,2048]{1,0:T(8,128)(2,1)}) custom-call(bf16[256,2048]{1,0:T(8,128)(2,1)} %copy-done.15, bf16[256,2048]{1,0:T(8,128)(2,1)} %copy-done.31, ...), custom_call_target="tpu_custom_call" | custom-call | flops 4831838208 | bytes 11272192 | tf_op jit(solution)/shard_map/mixer_backward/pallas_call | solution.py:112
  490.7 8.9 %collective-permute-done.42.refs_1_ = bf16[256,2048]{1,0:T(8,128)(2,1)S(1)} collective-permute-done((bf16[256,2048]{1,0:T(8,128)(2,1)S(1)}, bf16[256,2048]{1,0:T(8,128)(2,1)S(1)}, u32[]{:S(2)}, u32[]{:S(2)}) %collective-permute-start.42) | collective-permute-done | bytes 1048608 | tf_op jit(solution)/shard_map/ppermute | solution.py:223
  504.4 13.5 %mixer_backward.5 = (bf16[8,256,2048]{2,1,0:T(8,128)(2,1)}, bf16[8,256,512]{2,1,0:T(8,128)(2,1)}, bf16[8,256,1024]{2,1,0:T(8,128)(2,1)}, bf16[256,2048]{1,0:T(8,128)(2,1)}, bf16[256,2048]{1,0:T(8,128)(2,1)}) custom-call(bf16[256,2048]{1,0:T(8,128)(2,1)} %get-tuple-element.181.refs_0_, ...), custom_call_target="tpu_custom_call", output_to_operand_aliasing={{0}: (8, {}), {1}: (9, {}), {2}: (10, {})} | custom-call | flops 4831838208 | bytes 11272192 | tf_op jit(solution)/shard_map/mixer_backward/pallas_call | solution.py:112
  521.5 11.9 %collective-permute-done.52.refs_0_ = bf16[128,2048]{1,0:T(8,128)(2,1)S(1)} collective-permute-done((bf16[128,2048]{1,0:T(8,128)(2,1)S(1)}, bf16[128,2048]{1,0:T(8,128)(2,1)S(1)}, u32[]{:S(2)}, u32[]{:S(2)}) %collective-permute-start.52) | collective-permute-done | bytes 524320 | tf_op jit(solution)/shard_map/ppermute | solution.py:223
  535.9 13.1 %mixer_backward.6 = (bf16[8,256,2048]{2,1,0:T(8,128)(2,1)}, bf16[8,256,512]{2,1,0:T(8,128)(2,1)}, bf16[8,256,1024]{2,1,0:T(8,128)(2,1)}, bf16[256,2048]{1,0:T(8,128)(2,1)}, bf16[256,2048]{1,0:T(8,128)(2,1)}) custom-call(bf16[256,2048]{1,0:T(8,128)(2,1)} %get-tuple-element.195.refs_0_, ...), custom_call_target="tpu_custom_call", output_to_operand_aliasing={{0}: (8, {}), {1}: (9, {}), {2}: (10, {})} | custom-call | flops 4831838208 | bytes 11272192 | tf_op jit(solution)/shard_map/mixer_backward/pallas_call | solution.py:112
  552.3 13.2 %mixer_backward.7 = (bf16[8,256,2048]{2,1,0:T(8,128)(2,1)}, bf16[8,256,512]{2,1,0:T(8,128)(2,1)}, bf16[8,256,1024]{2,1,0:T(8,128)(2,1)}, bf16[256,2048]{1,0:T(8,128)(2,1)}, bf16[256,2048]{1,0:T(8,128)(2,1)}) custom-call(bf16[128,2048]{1,0:T(8,128)(2,1)} %get-tuple-element.197.refs_0_, ...), custom_call_target="tpu_custom_call", output_to_operand_aliasing={{0}: (10, {}), {1}: (11, {}), {2}: (12, {})} | custom-call | flops 4831838208 | bytes 11272192 | tf_op jit(solution)/shard_map/mixer_backward/pallas_call | solution.py:112
  565.5 9.9 %bitcast_convert_fusion.2 = bf16[2048,512]{1,0:T(8,128)(2,1)} fusion(bf16[8,256,2048]{2,1,0:T(8,128)(2,1)} %get-tuple-element.217, bf16[8,256,512]{2,1,0:T(8,128)(2,1)} %get-tuple-element.218), kind=kOutput, calls=%fused_computation.6 | convolution fusion | flops 4296015872 | bytes 12582912 | tf_op jit(solution)/shard_map/dot_general | solution.py:29
  575.7 14.2 %bitcast_convert_fusion = bf16[2048,1024]{1,0:T(8,128)(2,1)} fusion(bf16[8,256,2048]{2,1,0:T(8,128)(2,1)} %get-tuple-element.217, bf16[8,256,1024]{2,1,0:T(8,128)(2,1)} %get-tuple-element.219), kind=kOutput, calls=%fused_computation | convolution fusion | flops 8592031744 | bytes 16777216 | tf_op jit(solution)/shard_map/dot_general | solution.py:29
  603.4 9.1 %bitcast_convert_fusion.3.refs_3_ = bf16[512,2048]{1,0:T(8,128)(2,1)} fusion(bf16[8,256,512]{2,1,0:T(8,128)(2,1)S(1)} %copy-done.4, bf16[8,256,2048]{2,1,0:T(8,128)(2,1)} %get-tuple-element.205), kind=kOutput, calls=%fused_computation.7 | convolution fusion | flops 4296015872 | bytes 12582912 | tf_op jit(solution)/shard_map/dot_general | solution.py:29
  612.6 4.8 all-to-all-start.7
  617.4 4.9 collective-permute-done.47.refs_0_
  623.1 24.0 %collective-permute-done.49.refs_1_ = bf16[256,2048]{1,0:T(8,128)(2,1)} collective-permute-done((bf16[256,2048]{1,0:T(8,128)(2,1)}, bf16[256,2048]{1,0:T(8,128)(2,1)}, u32[]{:S(2)}, u32[]{:S(2)}) %collective-permute-start.49) | collective-permute-done | bytes 1048608 | tf_op jit(solution)/shard_map/ppermute | solution.py:223
  647.1 4.6 add_convert_fusion.2
  661.3 16.9 %all-to-all-done.9 = f32[32,1,128]{2,1,0:T(1,128)S(1)} async-done(((f32[32,1,128]{2,1,0:T(1,128)}), f32[32,1,128]{2,1,0:T(1,128)S(1)}, u32[]{:S(2)}, u32[]{:S(2)}) %all-to-all-start.9) | async-done | bytes 16416 | tf_op jit(solution)/shard_map/all_to_all | solution.py:321
  694.7 39.1 %all-to-all-done.8 = bf16[8,64,1024]{2,1,0:T(8,128)(2,1)S(1)} async-done(((bf16[8,64,1024]{2,1,0:T(8,128)(2,1)}), bf16[8,64,1024]{2,1,0:T(8,128)(2,1)S(1)}, u32[]{:S(2)}, u32[]{:S(2)}) %all-to-all-start.8) | async-done | bytes 1048608 | tf_op jit(solution)/shard_map/all_to_all | solution.py:321
  754.9 5.2 fusion.10
  777.4 6.5 all-to-all-done.4
  787.7 4.0 fusion.16
  797.1 5.9 all-to-all-done.5
  (403 shorter events, 228.2 us)
Async XLA Ops:
  7.2 152.8 %all-gather.7.cloned.1.call-start = ((), (), s32[]{:S(2)}) async-start(), calls=%async_computation.16 | async-start | bytes 2621440 | tf_op jit(solution)/shard_map/all_gather | solution.py:339
  7.9 166.1 %all-gather.5.cloned.1.call-start = ((), (), s32[]{:S(2)}) async-start(), calls=%async_computation.15 | async-start | bytes 7864320 | tf_op jit(solution)/shard_map/all_gather | solution.py:324
  40.5 68.3 %collective-permute-start.12 = (bf16[256,2048]{1,0:T(8,128)(2,1)}, bf16[256,2048]{1,0:T(8,128)(2,1)}, u32[]{:S(2)}, u32[]{:S(2)}) collective-permute-start(bf16[256,2048]{1,0:T(8,128)(2,1)} %fusion.14), channel_id=1, source_target_pairs={{0,16},{16,0},{1,17},{17,1},{2,18},{18,2},{3,19},{19,3},{4,20},{20... | collective-permute-start | bytes 3145736 | tf_op jit(solution)/shard_map/ppermute | solution.py:223
  41.1 54.2 %collective-permute-start.10 = (bf16[256,2048]{1,0:T(8,128)(2,1)}, bf16[256,2048]{1,0:T(8,128)(2,1)}, u32[]{:S(2)}, u32[]{:S(2)}) collective-permute-start(bf16[256,2048]{1,0:T(8,128)(2,1)} %fusion.14), channel_id=1, source_target_pairs={{0,8},{8,0},{1,9},{9,1},{2,10},{10,2},{3,11},{11,3},{4,12},{12,4},... | collective-permute-start | bytes 3145736 | tf_op jit(solution)/shard_map/ppermute | solution.py:223
  41.6 68.8 %collective-permute-start.9 = (bf16[256,2048]{1,0:T(8,128)(2,1)}, bf16[256,2048]{1,0:T(8,128)(2,1)}, u32[]{:S(2)}, u32[]{:S(2)}) collective-permute-start(bf16[256,2048]{1,0:T(8,128)(2,1)} %fusion.14), channel_id=1, source_target_pairs={{0,1},{1,0},{2,3},{3,2},{4,5},{5,4},{6,7},{7,6},{8,9},{9,8},{10,11... | collective-permute-start | bytes 3145736 | tf_op jit(solution)/shard_map/ppermute | solution.py:223
  41.6 74.6 %collective-permute-start.3 = (bf16[256,2048]{1,0:T(8,128)(2,1)S(1)}, bf16[256,2048]{1,0:T(8,128)(2,1)}, u32[]{:S(2)}, u32[]{:S(2)}) collective-permute-start(bf16[256,2048]{1,0:T(8,128)(2,1)S(1)} %bitcast.166), channel_id=1, source_target_pairs={{0,8},{8,0},{1,9},{9,1},{2,10},{10,2},{3,11},{11,3},{4,12},{12,4},... | collective-permute-start | bytes 3145736 | tf_op jit(solution)/shard_map/ppermute | solution.py:223
  43.1 74.9 %collective-permute-start.1 = (bf16[256,2048]{1,0:T(8,128)(2,1)S(1)}, bf16[256,2048]{1,0:T(8,128)(2,1)}, u32[]{:S(2)}, u32[]{:S(2)}) collective-permute-start(bf16[256,2048]{1,0:T(8,128)(2,1)S(1)} %bitcast.167), channel_id=1, source_target_pairs={{0,16},{16,0},{1,17},{17,1},{2,18},{18,2},{3,19},{19,3},{4,20},{20... | collective-permute-start | bytes 3145736 | tf_op jit(solution)/shard_map/ppermute | solution.py:223
  45.3 43.6 %all-to-all-start = ((bf16[32,2,128]{2,1,0:T(2,128)(2,1)}), bf16[32,2,128]{2,1,0:T(2,128)(2,1)S(1)}, u32[]{:S(2)}, u32[]{:S(2)}) async-start(bf16[32,2,128]{2,1,0:T(2,128)(2,1)} %reshape.650), calls=%async_computation | async-start | bytes 32768 | tf_op jit(solution)/shard_map/all_to_all | solution.py:321
  92.5 162.6 %all-gather.9.cloned.1.call-start = ((), (), s32[]{:S(2)}) async-start(), calls=%async_computation.17 | async-start | bytes 5242880 | tf_op jit(solution)/shard_map/all_gather | solution.py:324
  95.3 25.3 %collective-permute-start.11 = (bf16[256,2048]{1,0:T(8,128)(2,1)}, bf16[256,2048]{1,0:T(8,128)(2,1)S(1)}, u32[]{:S(2)}, u32[]{:S(2)}) collective-permute-start(bf16[256,2048]{1,0:T(8,128)(2,1)} %collective-permute-done.10), channel_id=1, source_target_pairs={{0,1},{1,0},{2,3},{3,2},{4,5},{5,4},{6,7},{7,6},{8,9},{9,8},{10,11... | collective-permute-start | bytes 3145736 | tf_op jit(solution)/shard_map/ppermute | solution.py:223
  110.4 32.0 %collective-permute-start.13 = (bf16[256,2048]{1,0:T(8,128)(2,1)}, bf16[256,2048]{1,0:T(8,128)(2,1)S(1)}, u32[]{:S(2)}, u32[]{:S(2)}) collective-permute-start(bf16[256,2048]{1,0:T(8,128)(2,1)} %collective-permute-done.12), channel_id=1, source_target_pairs={{0,1},{1,0},{2,3},{3,2},{4,5},{5,4},{6,7},{7,6},{8,9},{9,8},{10,11... | collective-permute-start | bytes 3145736 | tf_op jit(solution)/shard_map/ppermute | solution.py:223
  125.5 60.9 %collective-permute-start.4 = (bf16[256,2048]{1,0:T(8,128)(2,1)}, bf16[256,2048]{1,0:T(8,128)(2,1)}, u32[]{:S(2)}, u32[]{:S(2)}) collective-permute-start(bf16[256,2048]{1,0:T(8,128)(2,1)} %collective-permute-done.3.refs_0_), channel_id=1, source_target_pairs={{0,1},{1,0},{2,3},{3,2},{4,5},{5,4},{6,7},{7,6},{8,9},{9,8},{10,11... | collective-permute-start | bytes 3145736 | tf_op jit(solution)/shard_map/ppermute | solution.py:223
  163.8 175.2 %all-gather.11.cloned.1.call-start = ((), (), s32[]{:S(2)}) async-start(), calls=%async_computation.18 | async-start | bytes 2621440 | tf_op jit(solution)/shard_map/all_gather | solution.py:355
  216.4 50.2 %collective-permute-start.21 = (bf16[256,2048]{1,0:T(8,128)(2,1)}, bf16[256,2048]{1,0:T(8,128)(2,1)}, u32[]{:S(2)}, u32[]{:S(2)}) collective-permute-start(bf16[256,2048]{1,0:T(8,128)(2,1)} %get-tuple-element.244), channel_id=1, source_target_pairs={{0,8},{8,0},{1,9},{9,1},{2,10},{10,2},{3,11},{11,3},{4,12},{12,4},... | collective-permute-start | bytes 3145736 | tf_op jit(solution)/shard_map/ppermute | solution.py:223
  230.8 35.7 %collective-permute-start.20 = (bf16[256,2048]{1,0:T(8,128)(2,1)}, bf16[256,2048]{1,0:T(8,128)(2,1)}, u32[]{:S(2)}, u32[]{:S(2)}) collective-permute-start(bf16[256,2048]{1,0:T(8,128)(2,1)} %get-tuple-element.134), channel_id=1, source_target_pairs={{0,1},{1,0},{2,3},{3,2},{4,5},{5,4},{6,7},{7,6},{8,9},{9,8},{10,11... | collective-permute-start | bytes 3145736 | tf_op jit(solution)/shard_map/ppermute | solution.py:223
  231.0 34.5 %collective-permute-start.24 = (bf16[256,2048]{1,0:T(8,128)(2,1)S(1)}, bf16[256,2048]{1,0:T(8,128)(2,1)S(1)}, u32[]{:S(2)}, u32[]{:S(2)}) collective-permute-start(bf16[256,2048]{1,0:T(8,128)(2,1)S(1)} %get-tuple-element.246), channel_id=1, source_target_pairs={{0,24},{8,16},{16,8},{24,0},{1,25},{9,17},{17,9},{25,1},{2,26},{10... | collective-permute-start | bytes 3145736 | tf_op jit(solution)/shard_map/ppermute | solution.py:227
  234.0 47.9 %collective-permute-start.23 = (bf16[256,2048]{1,0:T(8,128)(2,1)}, bf16[256,2048]{1,0:T(8,128)(2,1)}, u32[]{:S(2)}, u32[]{:S(2)}) collective-permute-start(bf16[256,2048]{1,0:T(8,128)(2,1)} %add_convert_fusion.8), channel_id=1, source_target_pairs={{0,16},{16,0},{1,17},{17,1},{2,18},{18,2},{3,19},{19,3},{4,20},{20... | collective-permute-start | bytes 3145736 | tf_op jit(solution)/shard_map/ppermute | solution.py:223
  234.6 231.8 %reduce-scatter.6.cloned.1.call-start = ((), (), s32[]{:S(2)}) async-start(), calls=%async_computation.19 | async-start | bytes 2621440 | tf_op jit(solution)/shard_map/reduce_scatter | solution.py:442
  287.1 25.6 %collective-permute-start.26 = (bf16[256,2048]{1,0:T(8,128)(2,1)S(1)}, bf16[256,2048]{1,0:T(8,128)(2,1)S(1)}, u32[]{:S(2)}, u32[]{:S(2)}) collective-permute-start(bf16[256,2048]{1,0:T(8,128)(2,1)S(1)} %add_convert_fusion.7.refs_0_), channel_id=1, source_target_pairs={{0,16},{16,0},{1,17},{17,1},{2,18},{18,2},{3,19},{19,3},{4,20},{20... | collective-permute-start | bytes 3145736 | tf_op jit(solution)/shard_map/ppermute | solution.py:223
  287.8 25.3 %collective-permute-start.25 = (bf16[256,2048]{1,0:T(8,128)(2,1)S(1)}, bf16[256,2048]{1,0:T(8,128)(2,1)}, u32[]{:S(2)}, u32[]{:S(2)}) collective-permute-start(bf16[256,2048]{1,0:T(8,128)(2,1)S(1)} %add_convert_fusion.7.refs_0_), channel_id=1, source_target_pairs={{0,8},{8,0},{1,9},{9,1},{2,10},{10,2},{3,11},{11,3},{4,12},{12,4},... | collective-permute-start | bytes 3145736 | tf_op jit(solution)/shard_map/ppermute | solution.py:223
  367.0 185.3 %reduce-scatter.8.cloned.1.call-start = ((), (), s32[]{:S(2)}) async-start(), calls=%async_computation.20 | async-start | bytes 5242880 | tf_op jit(solution)/shard_map/reduce_scatter | solution.py:477
  390.7 28.8 %collective-permute-start.38 = (bf16[256,2048]{1,0:T(8,128)(2,1)}, bf16[256,2048]{1,0:T(8,128)(2,1)}, u32[]{:S(2)}, u32[]{:S(2)}) collective-permute-start(bf16[256,2048]{1,0:T(8,128)(2,1)} %get-tuple-element.172), channel_id=1, source_target_pairs={{0,1},{1,0},{2,3},{3,2},{4,5},{5,4},{6,7},{7,6},{8,9},{9,8},{10,11... | collective-permute-start | bytes 3145736 | tf_op jit(solution)/shard_map/ppermute | solution.py:223
  417.0 353.7 %reduce-scatter.10.cloned.1.call-start = ((), (), s32[]{:S(2)}) async-start(), calls=%async_computation.21 | async-start | bytes 2621440 | tf_op jit(solution)/shard_map/reduce_scatter | solution.py:477
  417.0 27.3 %collective-permute-start.40 = (bf16[256,2048]{1,0:T(8,128)(2,1)}, bf16[256,2048]{1,0:T(8,128)(2,1)S(1)}, u32[]{:S(2)}, u32[]{:S(2)}) collective-permute-start(bf16[256,2048]{1,0:T(8,128)(2,1)} %get-tuple-element.239), channel_id=1, source_target_pairs={{0,24},{8,16},{16,8},{24,0},{1,25},{9,17},{17,9},{25,1},{2,26},{10... | collective-permute-start | bytes 3145736 | tf_op jit(solution)/shard_map/ppermute | solution.py:227
  418.9 46.9 %collective-permute-start.37 = (bf16[256,2048]{1,0:T(8,128)(2,1)}, bf16[256,2048]{1,0:T(8,128)(2,1)}, u32[]{:S(2)}, u32[]{:S(2)}) collective-permute-start(bf16[256,2048]{1,0:T(8,128)(2,1)} %get-tuple-element.241), channel_id=1, source_target_pairs={{0,8},{8,0},{1,9},{9,1},{2,10},{10,2},{3,11},{11,3},{4,12},{12,4},... | collective-permute-start | bytes 3145736 | tf_op jit(solution)/shard_map/ppermute | solution.py:223
  421.5 44.9 %collective-permute-start.39 = (bf16[256,2048]{1,0:T(8,128)(2,1)S(1)}, bf16[256,2048]{1,0:T(8,128)(2,1)}, u32[]{:S(2)}, u32[]{:S(2)}) collective-permute-start(bf16[256,2048]{1,0:T(8,128)(2,1)S(1)} %add_convert_fusion.6), channel_id=1, source_target_pairs={{0,16},{16,0},{1,17},{17,1},{2,18},{18,2},{3,19},{19,3},{4,20},{20... | collective-permute-start | bytes 3145736 | tf_op jit(solution)/shard_map/ppermute | solution.py:223
  422.6 43.8 %collective-permute-start.36 = (bf16[256,2048]{1,0:T(8,128)(2,1)}, bf16[256,2048]{1,0:T(8,128)(2,1)}, u32[]{:S(2)}, u32[]{:S(2)}) collective-permute-start(bf16[256,2048]{1,0:T(8,128)(2,1)} %get-tuple-element.170), channel_id=1, source_target_pairs={{0,1},{1,0},{2,3},{3,2},{4,5},{5,4},{6,7},{7,6},{8,9},{9,8},{10,11... | collective-permute-start | bytes 3145736 | tf_op jit(solution)/shard_map/ppermute | solution.py:223
  474.0 25.6 %collective-permute-start.42 = (bf16[256,2048]{1,0:T(8,128)(2,1)S(1)}, bf16[256,2048]{1,0:T(8,128)(2,1)S(1)}, u32[]{:S(2)}, u32[]{:S(2)}) collective-permute-start(bf16[256,2048]{1,0:T(8,128)(2,1)S(1)} %get-tuple-element.232.refs_0_), channel_id=1, source_target_pairs={{0,16},{16,0},{1,17},{17,1},{2,18},{18,2},{3,19},{19,3},{4,20},{20... | collective-permute-start | bytes 3145736 | tf_op jit(solution)/shard_map/ppermute | solution.py:223
  474.9 25.4 %collective-permute-start.41 = (bf16[256,2048]{1,0:T(8,128)(2,1)S(1)}, bf16[256,2048]{1,0:T(8,128)(2,1)}, u32[]{:S(2)}, u32[]{:S(2)}) collective-permute-start(bf16[256,2048]{1,0:T(8,128)(2,1)S(1)} %get-tuple-element.232.refs_0_), channel_id=1, source_target_pairs={{0,8},{8,0},{1,9},{9,1},{2,10},{10,2},{3,11},{11,3},{4,12},{12,4},... | collective-permute-start | bytes 3145736 | tf_op jit(solution)/shard_map/ppermute | solution.py:223
  500.5 35.3 %collective-permute-start.56 = (bf16[256,2048]{1,0:T(8,128)(2,1)}, bf16[256,2048]{1,0:T(8,128)(2,1)}, u32[]{:S(2)}, u32[]{:S(2)}) collective-permute-start(bf16[256,2048]{1,0:T(8,128)(2,1)} %get-tuple-element.195.refs_0_), channel_id=1, source_target_pairs={{0,1},{1,0},{2,3},{3,2},{4,5},{5,4},{6,7},{7,6},{8,9},{9,8},{10,11... | collective-permute-start | bytes 3145736 | tf_op jit(solution)/shard_map/ppermute | solution.py:223
  517.9 31.1 %collective-permute-start.57 = (bf16[256,2048]{1,0:T(8,128)(2,1)}, bf16[256,2048]{1,0:T(8,128)(2,1)}, u32[]{:S(2)}, u32[]{:S(2)}) collective-permute-start(bf16[256,2048]{1,0:T(8,128)(2,1)} %get-tuple-element.196.refs_2_), channel_id=1, source_target_pairs={{0,1},{1,0},{2,3},{3,2},{4,5},{5,4},{6,7},{7,6},{8,9},{9,8},{10,11... | collective-permute-start | bytes 3145736 | tf_op jit(solution)/shard_map/ppermute | solution.py:223
  575.5 208.4 %reduce-scatter.12.cloned.1.call-start = ((), (), s32[]{:S(2)}) async-start(), calls=%async_computation.22 | async-start | bytes 5242880 | tf_op jit(solution)/shard_map/reduce_scatter | solution.py:477
  591.4 55.7 %collective-permute-start.45 = (bf16[256,2048]{1,0:T(8,128)(2,1)}, bf16[256,2048]{1,0:T(8,128)(2,1)}, u32[]{:S(2)}, u32[]{:S(2)}) collective-permute-start(bf16[256,2048]{1,0:T(8,128)(2,1)} %get-tuple-element.187), channel_id=1, source_target_pairs={{0,1},{1,0},{2,3},{3,2},{4,5},{5,4},{6,7},{7,6},{8,9},{9,8},{10,11... | collective-permute-start | bytes 3145736 | tf_op jit(solution)/shard_map/ppermute | solution.py:223
  591.9 63.2 %collective-permute-start.64 = (bf16[256,2048]{1,0:T(8,128)(2,1)}, bf16[256,2048]{1,0:T(8,128)(2,1)}, u32[]{:S(2)}, u32[]{:S(2)}) collective-permute-start(bf16[256,2048]{1,0:T(8,128)(2,1)} %get-tuple-element.211), channel_id=1, source_target_pairs={{0,1},{1,0},{2,3},{3,2},{4,5},{5,4},{6,7},{7,6},{8,9},{9,8},{10,11... | collective-permute-start | bytes 3145736 | tf_op jit(solution)/shard_map/ppermute | solution.py:223
  595.9 26.3 %collective-permute-start.47 = (bf16[256,2048]{1,0:T(8,128)(2,1)}, bf16[256,2048]{1,0:T(8,128)(2,1)}, u32[]{:S(2)}, u32[]{:S(2)}) collective-permute-start(bf16[256,2048]{1,0:T(8,128)(2,1)} %add_convert_fusion.5), channel_id=1, source_target_pairs={{0,8},{8,0},{1,9},{9,1},{2,10},{10,2},{3,11},{11,3},{4,12},{12,4},... | collective-permute-start | bytes 3145736 | tf_op jit(solution)/shard_map/ppermute | solution.py:223
  599.4 47.7 %collective-permute-start.49 = (bf16[256,2048]{1,0:T(8,128)(2,1)}, bf16[256,2048]{1,0:T(8,128)(2,1)}, u32[]{:S(2)}, u32[]{:S(2)}) collective-permute-start(bf16[256,2048]{1,0:T(8,128)(2,1)} %add_convert_fusion.4), channel_id=1, source_target_pairs={{0,16},{16,0},{1,17},{17,1},{2,18},{18,2},{3,19},{19,3},{4,20},{20... | collective-permute-start | bytes 3145736 | tf_op jit(solution)/shard_map/ppermute | solution.py:223
  601.7 45.5 %collective-permute-start.51 = (bf16[256,2048]{1,0:T(8,128)(2,1)}, bf16[256,2048]{1,0:T(8,128)(2,1)}, u32[]{:S(2)}, u32[]{:S(2)}) collective-permute-start(bf16[256,2048]{1,0:T(8,128)(2,1)} %add_convert_fusion.3), channel_id=1, source_target_pairs={{0,24},{8,16},{16,8},{24,0},{1,25},{9,17},{17,9},{25,1},{2,26},{10... | collective-permute-start | bytes 3145736 | tf_op jit(solution)/shard_map/ppermute | solution.py:227
  612.6 40.0 %all-to-all-start.7 = ((bf16[2,256,2048]{2,1,0:T(8,128)(2,1)}), bf16[2,256,2048]{2,1,0:T(8,128)(2,1)}, u32[]{:S(2)}, u32[]{:S(2)}) async-start(bf16[2,256,2048]{2,1,0:T(8,128)(2,1)} %bitcast.169), calls=%async_computation.11 | async-start | bytes 4194304 | tf_op jit(solution)/shard_map/all_to_all | solution.py:321
  622.3 130.9 %collective-permute-start.63 = (bf16[256,2048]{1,0:T(8,128)(2,1)}, bf16[256,2048]{1,0:T(8,128)(2,1)S(1)}, u32[]{:S(2)}, u32[]{:S(2)}) collective-permute-start(bf16[256,2048]{1,0:T(8,128)(2,1)} %get-tuple-element.237), channel_id=1, source_target_pairs={{0,8},{8,0},{1,9},{9,1},{2,10},{10,2},{3,11},{11,3},{4,12},{12,4},... | collective-permute-start | bytes 3145736 | tf_op jit(solution)/shard_map/ppermute | solution.py:223
  647.1 34.9 %collective-permute-start.66 = (bf16[256,2048]{1,0:T(8,128)(2,1)}, bf16[256,2048]{1,0:T(8,128)(2,1)}, u32[]{:S(2)}, u32[]{:S(2)}) collective-permute-start(bf16[256,2048]{1,0:T(8,128)(2,1)} %get-tuple-element.213), channel_id=1, source_target_pairs={{0,1},{1,0},{2,3},{3,2},{4,5},{5,4},{6,7},{7,6},{8,9},{9,8},{10,11... | collective-permute-start | bytes 3145736 | tf_op jit(solution)/shard_map/ppermute | solution.py:223
  651.7 36.1 %collective-permute-start.59 = (bf16[256,2048]{1,0:T(8,128)(2,1)}, bf16[256,2048]{1,0:T(8,128)(2,1)}, u32[]{:S(2)}, u32[]{:S(2)}) collective-permute-start(bf16[256,2048]{1,0:T(8,128)(2,1)} %add_convert_fusion.2), channel_id=1, source_target_pairs={{0,16},{16,0},{1,17},{17,1},{2,18},{18,2},{3,19},{19,3},{4,20},{20... | collective-permute-start | bytes 3145736 | tf_op jit(solution)/shard_map/ppermute | solution.py:223
  652.6 25.6 %all-to-all-start.9 = ((f32[32,1,128]{2,1,0:T(1,128)}), f32[32,1,128]{2,1,0:T(1,128)S(1)}, u32[]{:S(2)}, u32[]{:S(2)}) async-start(f32[32,1,128]{2,1,0:T(1,128)} %reshape.654), calls=%async_computation.14 | async-start | bytes 32768 | tf_op jit(solution)/shard_map/all_to_all | solution.py:321
  655.1 137.9 %reduce-scatter.14.cloned.1.call-start = ((), (), s32[]{:S(2)}) async-start(), calls=%async_computation.23 | async-start | bytes 2621440 | tf_op jit(solution)/shard_map/reduce_scatter | solution.py:519
  658.1 95.8 %collective-permute-start.65 = (bf16[256,2048]{1,0:T(8,128)(2,1)}, bf16[256,2048]{1,0:T(8,128)(2,1)S(1)}, u32[]{:S(2)}, u32[]{:S(2)}) collective-permute-start(bf16[256,2048]{1,0:T(8,128)(2,1)} %add_convert_fusion.1), channel_id=1, source_target_pairs={{0,16},{16,0},{1,17},{17,1},{2,18},{18,2},{3,19},{19,3},{4,20},{20... | collective-permute-start | bytes 3145736 | tf_op jit(solution)/shard_map/ppermute | solution.py:223
  659.8 90.3 %collective-permute-start.58 = (bf16[256,2048]{1,0:T(8,128)(2,1)}, bf16[256,2048]{1,0:T(8,128)(2,1)}, u32[]{:S(2)}, u32[]{:S(2)}) collective-permute-start(bf16[256,2048]{1,0:T(8,128)(2,1)} %add_convert_fusion.2), channel_id=1, source_target_pairs={{0,8},{8,0},{1,9},{9,1},{2,10},{10,2},{3,11},{11,3},{4,12},{12,4},... | collective-permute-start | bytes 3145736 | tf_op jit(solution)/shard_map/ppermute | solution.py:223
  678.2 55.6 %all-to-all-start.8 = ((bf16[8,64,1024]{2,1,0:T(8,128)(2,1)}), bf16[8,64,1024]{2,1,0:T(8,128)(2,1)S(1)}, u32[]{:S(2)}, u32[]{:S(2)}) async-start(bf16[8,64,1024]{2,1,0:T(8,128)(2,1)} %bitcast.172), calls=%async_computation.13 | async-start | bytes 2097152 | tf_op jit(solution)/shard_map/all_to_all | solution.py:321
  685.0 69.0 %collective-permute-start.67 = (bf16[256,2048]{1,0:T(8,128)(2,1)}, bf16[256,2048]{1,0:T(8,128)(2,1)}, u32[]{:S(2)}, u32[]{:S(2)}) collective-permute-start(bf16[256,2048]{1,0:T(8,128)(2,1)} %add_convert_fusion), channel_id=1, source_target_pairs={{0,24},{8,16},{16,8},{24,0},{1,25},{9,17},{17,9},{25,1},{2,26},{10... | collective-permute-start | bytes 3145736 | tf_op jit(solution)/shard_map/ppermute | solution.py:227
  687.8 67.1 %collective-permute-start.62 = (bf16[256,2048]{1,0:T(8,128)(2,1)}, bf16[256,2048]{1,0:T(8,128)(2,1)}, u32[]{:S(2)}, u32[]{:S(2)}) collective-permute-start(bf16[256,2048]{1,0:T(8,128)(2,1)} %get-tuple-element.180.refs_2_), channel_id=1, source_target_pairs={{0,1},{1,0},{2,3},{3,2},{4,5},{5,4},{6,7},{7,6},{8,9},{9,8},{10,11... | collective-permute-start | bytes 3145736 | tf_op jit(solution)/shard_map/ppermute | solution.py:223
  (90 other events, 823.8 us)
Sparse Core Ops, SparseCore 0:
  9.6 48.7 all-gather.6
  59.9 114.0 all-gather.4
  176.1 78.9 all-gather.8
  256.5 44.1 all-gather.10
  367.1 41.8 reduce-scatter.5
  417.1 74.6 reduce-scatter.7
  575.6 40.9 reduce-scatter.9
  618.8 76.2 reduce-scatter.11
  697.4 44.0 reduce-scatter.13

commit v3 on v2

--- a/solution.py
+++ b/solution.py
@@ -92,7 +92,7 @@
     return pl.BlockSpec((2,) + shape, lambda i: (number,) + (0,) * len(shape))
 
 
-def chunk_call(body_fn, name, number, pieces, shared, saved_in, buffers, shapes, parts, flops, tokens=()):
+def chunk_call(body_fn, name, number, pieces, shared, saved_in, buffers, shapes, parts, tokens=(), flops=0):
     flat = [piece for side in pieces for piece in side]
     counts = [len(side) for side in pieces]
     total = len(flat) + len(shared) + len(saved_in)
@@ -108,7 +108,6 @@
     outs = [jax.ShapeDtypeStruct((GROUP,) + shape, dtype) for shape, dtype in shapes]
     outs += [jax.ShapeDtypeStruct(shape, dtype) for shape, dtype in parts]
     operands = [*flat, *shared, *saved_in, *carried, *tokens]
-    size = sum(math.prod(o.shape) * o.dtype.itemsize for o in [*flat, *shared])
     return pl.pallas_call(
         kernel,
         grid=(1,),
@@ -120,7 +119,7 @@
         + [pl.BlockSpec(shape, lambda i: (0, 0)) for shape, _ in parts],
         input_output_aliases={total + i: i for i in range(len(carried))},
         compiler_params=pltpu.CompilerParams(vmem_limit_bytes=56 * 1024 * 1024),
-        cost_estimate=pl.CostEstimate(flops=flops, bytes_accessed=size, transcendentals=0),
+        cost_estimate=pl.CostEstimate(flops=flops, bytes_accessed=0, transcendentals=0),
         name=name,
     )(*operands)
 
@@ -256,16 +255,16 @@
 
 def chunks_in_turn(own, call):
     half = own.shape[0] // 2
-    from_x = swap(own, "x")
-    from_y = swap(own, "y")
-    results = [call(0, pair_up([own]), [])]
-    from_x, from_y = after([from_x, from_y], results[0][-1])
-    upper = swap(from_y[:half], "x")
-    lower = swap(from_x[half:], "y")
-    chunk_x, chunk_y = pair_up([from_x]), pair_up([from_y])
+    lower_x, upper_y = swap(own[half:], "x"), swap(own[:half], "y")
+    chunk_own = pair_up([own])
+    upper_x, lower_y = swap(own[:half], "x"), swap(own[half:], "y")
+    results = [call(0, chunk_own, [])]
+    lower_x, upper_y = after([lower_x, upper_y], results[0][-1])
+    lower, upper = swap(lower_x, "y"), swap(upper_y, "x")
+    upper_x, lower_y = after([upper_x, lower_y], lower_x)
+    chunk_x, chunk_y = pair_up([upper_x, lower_x]), pair_up([upper_y, lower_y])
     results.append(call(1, chunk_x, results))
-    across = after([upper, lower], results[1][-1])
-    chunk_across = pair_up(across)
+    chunk_across = pair_up(after([upper, lower], results[1][-1]))
     results.append(call(2, chunk_y, results))
     results.append(call(3, chunk_across, results))
     return results
@@ -275,15 +274,30 @@
     return pair[0].astype(F32) + swap(pair[1], "core").astype(F32)
 
 
-def send(number, summed):
-    summed = summed.astype(BF16)
-    if number == 3:
-        return swap_both(summed, ("y", "x"))
-    return swap(summed, ("x", "y")[number - 1])
-
-
-def add_up(own, arrived):
-    return own + arrived[1].astype(F32) + arrived[2].astype(F32) + arrived[3].astype(F32)
+class GroupSum:
+    def __init__(self):
+        self.passing = self.own = None
+        self.arrived = []
+
+    def terms(self, number, pair):
+        total = two_cores(pair)
+        half = total.shape[0] // 2
+        if number == 0:
+            self.own = total
+            return None
+        if number == 3:
+            total = total.astype(BF16)
+            self.passing = after([swap(total[half:], "y"), swap(total[:half], "x")])
+            return total
+        margins = ((half, 0), (0, half))[number - 1]
+        passed = jnp.pad(self.passing[number - 1], (margins, (0, 0)))
+        total = (total + passed.astype(F32)).astype(BF16)
+        self.arrived.append(swap(total, ("x", "y")[number - 1]))
+        return total
+
+    def total(self, *tokens):
+        arrived = after(self.arrived, *tokens) if tokens else self.arrived
+        return self.own + arrived[0].astype(F32) + arrived[1].astype(F32)
 
 
 def body(
@@ -387,7 +401,7 @@
     tables = rotation_tables(length)
     decay = decay_mask(length, head)
     row_bytes = (length, breadth)
-    saved, summed, arrived = None, [None] * 4, [None] * 4
+    saved, summed, leaving = None, GroupSum(), [upstream_all]
     token_chunks = spread(tokens[0])
     order = (3, 1, 2, 0)
     for i, n in enumerate(order):
@@ -406,15 +420,12 @@
                 ((length, VAL), BF16),
             ],
             [(row_bytes, BF16)] * 2,
-            2 * 2 * length * breadth * 2048,
-            [upstream_all] if i < 2 else [summed[order[i - 2]]],
+            leaving[: max(1, i)] if i < 3 else leaving,
         )
         saved = results[:4]
-        summed[n] = two_cores(results[4:6])
-        arrived[n] = send(n, summed[n]) if n else None
+        leaving.append(summed.terms(n, results[4:6]))
     mixer_normed, qkv_all, gate_all, gated_all = saved
-    arrived[3] = after([arrived[3]], feed_weight)[0]
-    hidden_state = tokens[0].astype(F32) + add_up(summed[0], arrived)
+    hidden_state = tokens[0].astype(F32) + summed.total(feed_weight)
 
     feed_hat, feed_inverse = statistics(hidden_state, EPSILON)
     feed_own = (feed_hat * features[2] + features[3]).astype(BF16)
@@ -430,7 +441,6 @@
             earlier[-1][:3] if earlier else None,
             [((length, breadth), BF16), ((length, hidden), BF16), ((length, 2 * hidden), F32)],
             [((8, 128), F32)],
-            2 * 2 * length * breadth * hidden * 2,
             [down_weight] if n == 3 else [],
         )
 
@@ -441,7 +451,7 @@
     ).astype(BF16)
     down_grad = lax.psum_scatter(down_product, "z", scatter_dimension=0, tiled=True)
 
-    saved, summed, arrived, feed_parts = None, [None] * 4, [None] * 4, [None] * 4
+    saved, summed, leaving, feed_parts = None, GroupSum(), [down_product], [None] * 4
     for i, n in enumerate(order):
         results = chunk_call(
             feed_backward,
@@ -453,19 +463,16 @@
             saved,
             [((length, 2 * hidden), BF16)],
             [(row_bytes, BF16)] * 4,
-            2 * 2 * length * breadth * hidden * 4,
-            [down_product] if i < 2 else [summed[order[i - 2]]],
+            leaving[: max(1, i)] if i < 3 else leaving,
         )
         saved = results[:1]
         feed_parts[n] = results[1:3]
-        summed[n] = two_cores(results[3:5])
-        arrived[n] = send(n, summed[n]) if n else None
+        leaving.append(summed.terms(n, results[3:5]))
     feed_product = dot_rows(
         feed_normed.reshape(GROUP * length, breadth),
         saved[0].reshape(GROUP * length, -1),
     ).astype(BF16)
-    arrived = [None] + after(arrived[1:], feed_product, down_grad)
-    feed_normed_grad = add_up(summed[0], arrived)
+    feed_normed_grad = summed.total(feed_product, down_grad)
     feed_gain_part = jnp.sum(feed_normed_grad * feed_hat, axis=0)
     feed_bias_part = jnp.sum(feed_normed_grad, axis=0)
     state_grad = upstream_all[0].astype(F32) + pull_back(
@@ -479,16 +486,12 @@
         )
 
     def to_owners(mine):
-        return to_members(mine.reshape(GROUP, local_model, -1)).astype(F32)
+        return to_members(mine.reshape(GROUP, local_model, -1))
 
     feed_summed = sum_layers(feed_product)
     feed_grads = to_owners(feed_summed)
 
-    summed, grad_parts = [None] * 4, [None] * 4
-
     def backward_call(n, chunk, earlier):
-        if n == 3:
-            summed[1] = two_cores(earlier[1][3:5])
         return chunk_call(
             mixer_backward,
             "mixer_backward",
@@ -499,20 +502,19 @@
             earlier[-1][:3] if earlier else None,
             [((length, breadth), BF16), ((length, 2 * KEY), BF16), ((length, 2 * VAL), BF16)],
             [(row_bytes, BF16)] * 2,
-            2 * 2 * length * breadth * 2304,
-            [summed[1], feed_summed] if n == 3 else [],
+            [],
+            2 * 10**10,
         )
 
     results = chunks_in_turn(own_grad_low, backward_call)
     saved = results[-1][:3]
-    grad_parts = [result[3:5] for result in results]
-    summed = [summed[1] if n == 1 else two_cores(grad_parts[n]) for n in range(4)]
-    arrived = [None] + [send(n, summed[n]) for n in range(1, 4)]
     out_grad, qk_grad, vg_grad = (a.reshape(GROUP * length, -1) for a in saved)
+    (qk_grad,) = after([qk_grad], feed_summed)
 
     normed_rows = mixer_normed.reshape(GROUP * length, breadth)
     qk_product = dot_rows(normed_rows, qk_grad).astype(BF16)
     vg_product = dot_rows(normed_rows, vg_grad).astype(BF16)
+    (out_grad,) = after([out_grad], feed_grads)
     out_product = dot_rows(gated_all.reshape(GROUP * length, VAL), out_grad).astype(BF16)
     qk_grads = to_owners(sum_layers(qk_product))
     vg_grads = to_owners(sum_layers(vg_product))
@@ -520,20 +522,23 @@
         to_members(out_product, "core"), "z", scatter_dimension=0, tiled=True
     ).astype(F32)
 
-    held = after([part for pair in feed_parts for part in pair], grad_parts[1][0])
-    feed_parts = [held[2 * n : 2 * n + 2] for n in range(4)]
-    feed_terms = [two_cores(pair) for pair in feed_parts]
-    feed_arrived = [None] + after([send(n, feed_terms[n]) for n in range(1, 4)], out_product)
-    slot_out = (hidden_state + add_up(feed_terms[0], feed_arrived)).astype(BF16)
+    held = after([part for pair in feed_parts for part in pair], results[1][-1])
+    summed = GroupSum()
+    for n in order:
+        summed.terms(n, held[2 * n : 2 * n + 2])
+    slot_out = (hidden_state + summed.total(out_product)).astype(BF16)
     half = length // 2
     from_x, from_y = swap(slot_out, "x"), swap(slot_out, "y")
     across = jnp.concatenate([swap(from_y[:half], "x"), swap(from_x[half:], "y")], axis=0)
+    (across,) = after([across], qk_grads)
     reached = jnp.stack([slot_out, from_x, from_y, across])
     chosen = lax.dynamic_index_in_dim(reached, own_slot, 0, keepdims=False)
     out_tokens = (live_mask * chosen.astype(F32)).astype(BF16)
 
-    arrived = [None] + after(arrived[1:], out_product)
-    mixer_normed_grad = add_up(summed[0], arrived)
+    summed = GroupSum()
+    for n in order:
+        summed.terms(n, results[n][3:5])
+    mixer_normed_grad = summed.total(out_product)
     mixer_hat, mixer_inverse = statistics(tokens[0].astype(F32), EPSILON)
     mixer_gain_part = jnp.sum(mixer_normed_grad * mixer_hat, axis=0)
     mixer_bias_part = jnp.sum(mixer_normed_grad, axis=0)
@@ -562,15 +567,15 @@
     return (
         out_tokens[None],
         input_grad[None],
-        head_back(qk_grads[..., :KEY]),
-        head_back(qk_grads[..., KEY:]),
-        value_back(vg_grads[..., :VAL]),
-        value_back(vg_grads[..., VAL:]),
+        head_back(qk_grads[..., :KEY].astype(F32)),
+        head_back(qk_grads[..., KEY:].astype(F32)),
+        value_back(vg_grads[..., :VAL].astype(F32)),
+        value_back(vg_grads[..., VAL:].astype(F32)),
         mixer_vectors[0],
         mixer_vectors[1],
         output_grad,
-        hidden_back(feed_grads[..., :hidden]),
-        hidden_back(feed_grads[..., hidden:]),
+        hidden_back(feed_grads[..., :hidden].astype(F32)),
+        hidden_back(feed_grads[..., hidden:].astype(F32)),
         down_grad.astype(F32),
         feed_vectors[0],
         feed_vectors[1],

time: 828 us -> 724 us (0.87)
  waiting for transfers between devices: 293 us -> 178 us
  starting transfers between devices: 77.6 us -> 87.5 us
    ppermute x64 -> x80, waiting for transfers between devices: 133 us -> 83.1 us  [swap(): return lax.ppermute(field_in, axis, [(0, 1), (1, 0)])]
    all_to_all x9 -> x8, waiting for transfers between devices: 100 us -> 60.8 us  [to_members(): return lax.all_to_all(packed, axes, 0, 0, tiled=True)]
    ppermute x4 -> x0, waiting for transfers between devices: 32.2 us -> none  [swap_both(): return lax.ppermute(field_in, axes, [(0, 3), (1, 2), (2, 1), (3, 0)])]
    ppermute x64 -> x80, starting transfers between devices: 36 us -> 53.4 us  [swap(): return lax.ppermute(field_in, axis, [(0, 1), (1, 0)])]
    reshape x6 -> x0, local copies, waits for them, and re-layouts: 9.26 us -> none  [the longest x4 6.71 us: hidden_back(): split = grads.reshape(4, 2, local_model, layers, local_hidden)]
    all_to_all x1 -> x2, blocking collectives: 26.2 us -> 32.5 us  [to_members(): return lax.all_to_all(packed, axes, 0, 0, tiled=True)]
    unnamed x125 -> x170, local copies, waits for them, and re-layouts: 39.1 us -> 42.7 us
    all_to_all x9 -> x8, starting transfers between devices: 32.3 us -> 32.9 us  [to_members(): return lax.all_to_all(packed, axes, 0, 0, tiled=True)]
  transfers between devices with their start and end apart: 86 -> 97, of which waited for: 33 -> 30; matrix products, arithmetic and copies ran while one was open for 22% -> 22% of each run, Pallas kernels for 17% -> 21%
where the time goes in v3:
time: 724 us; the launch traced here: 715 us
  waiting for transfers between devices  178 us (25%)
  Pallas kernels  169 us (23%)
  starting transfers between devices  87.5 us (12%)
  local copies, waits for them, and re-layouts  84.6 us (12%)
  other arithmetic  72.4 us (10%)
  matrix products  57 us (8%)
  between operations  34.5 us (5%)
  blocking collectives  32.5 us (4%)
    pallas_call x16, Pallas kernels, chunk_call(): pl.pallas_call(kernel, grid=(1,), out_shape=outs, in_specs=[whole_spec(o)...  169 us
    ppermute x80, waiting for transfers between devices, swap(): return lax.ppermute(field_in, axis, [(0, 1), (1, 0)])  83.1 us
    all_to_all x8, waiting for transfers between devices, to_members(): return lax.all_to_all(packed, axes, 0, 0, tiled=True)  60.8 us
    dot_general x5, matrix products, dot_rows(): lax.dot_general(left, right, (((0,), (0,)), ((), ())), preferred_element_...  57 us
    ppermute x80, starting transfers between devices, swap(): return lax.ppermute(field_in, axis, [(0, 1), (1, 0)])  53.4 us
    unnamed x170, local copies, waits for them, and re-layouts  42.7 us
    all_to_all x8, starting transfers between devices, to_members(): return lax.all_to_all(packed, axes, 0, 0, tiled=True)  32.9 us
    all_to_all x2, blocking collectives, to_members(): return lax.all_to_all(packed, axes, 0, 0, tiled=True)  32.5 us
  transfers between devices with their start and end apart: 97, of which 30 were waited for; matrix products, arithmetic and copies ran while one was open for 22% of the time, Pallas kernels for 21%

profile of v3, /device:TPU:0, one launch (start us, length us, event | category | flops | bytes accessed | tf_op | source)
XLA Modules:
  0.0 715.3 jit_solution(18356021150648808149)
XLA Ops:
  11.4 26.2 %all_to_all.63 = bf16[8,64,1536]{2,1,0:T(8,128)(2,1)} all-to-all(bf16[8,64,1536]{2,1,0:T(8,128)(2,1)S(1)} %pad_maximum_fusion), channel_id=1, replica_groups=mesh['y'=2,'x'=2,'z'=4,'core'=2] {'y','x','core'}, dimensions={0} | all-to-all | bytes 3145728 | tf_op jit(solution)/shard_map/all_to_all | solution.py:335
  44.4 4.0 all-to-all-start
  72.6 13.1 %all-to-all-done = bf16[32,2,128]{2,1,0:T(2,128)(2,1)S(1)} async-done(((bf16[32,2,128]{2,1,0:T(2,128)(2,1)}), bf16[32,2,128]{2,1,0:T(2,128)(2,1)S(1)}, u32[]{:S(2)}, u32[]{:S(2)}) %all-to-all-start) | async-done | bytes 16416 | tf_op jit(solution)/shard_map/all_to_all | solution.py:335
  85.7 3.6 all-to-all-start.3
  93.2 11.3 %all-to-all-done.3 = bf16[8,64,1024]{2,1,0:T(8,128)(2,1)S(1)} async-done(((bf16[8,64,1024]{2,1,0:T(8,128)(2,1)}), bf16[8,64,1024]{2,1,0:T(8,128)(2,1)S(1)}, u32[]{:S(2)}, u32[]{:S(2)}) %all-to-all-start.3) | async-done | bytes 1048608 | tf_op jit(solution)/shard_map/all_to_all | solution.py:335
  123.3 10.0 %collective-permute-done.15 = bf16[128,2048]{1,0:T(8,128)(2,1)S(1)} collective-permute-done((bf16[128,2048]{1,0:T(8,128)(2,1)S(1)}, bf16[128,2048]{1,0:T(8,128)(2,1)S(1)}, u32[]{:S(2)}, u32[]{:S(2)}) %collective-permute-start.15) | collective-permute-done | bytes 524320 | tf_op jit(solution)/shard_map/ppermute | solution.py:222
  152.3 3.8 all-to-all-start.2
  158.9 15.1 %all-gather.5.cloned.1.call-done = bf16[4,512,1536]{2,1,0:T(8,128)(2,1)} async-done(((bf16[4,128,1536]{2,1,0:T(8,128)(2,1)}), bf16[4,512,1536]{2,1,0:T(8,128)(2,1)}) %all-gather.5.cloned.1.call-update) | async-done | bytes 6291472 | tf_op jit(solution)/shard_map/all_gather | solution.py:338
  174.0 12.0 %mixer_forward.4 = (bf16[8,256,2048]{2,1,0:T(8,128)(2,1)}, bf16[8,256,1024]{2,1,0:T(8,128)(2,1)}, f32[8,256,512]{2,1,0:T(8,128)}, bf16[8,256,512]{2,1,0:T(8,128)...) custom-call(bf16[128,2048]{1,0:T(8,128)(2,1)} %collective-permute-done.5.refs_0_, ...), custom_call_target="tpu_custom_call" | custom-call | tf_op jit(solution)/shard_map/mixer_forward/pallas_call | solution.py:111
  186.5 12.0 %mixer_forward.5 = (bf16[8,256,2048]{2,1,0:T(8,128)(2,1)}, bf16[8,256,1024]{2,1,0:T(8,128)(2,1)}, f32[8,256,512]{2,1,0:T(8,128)}, bf16[8,256,512]{2,1,0:T(8,128)...) custom-call(bf16[256,2048]{1,0:T(8,128)(2,1)} %collective-permute-do, ...), custom_call_target="tpu_custom_call", output_to_operand_aliasing={{0}: (7, {}), {1}: (8, {}), {2}: (9, {}), {3}: (10, {})} | custom-call | tf_op jit(solution)/shard_map/mixer_forward/pallas_call | solution.py:111
  203.0 12.5 %mixer_forward.6 = (bf16[8,256,2048]{2,1,0:T(8,128)(2,1)}, bf16[8,256,1024]{2,1,0:T(8,128)(2,1)}, f32[8,256,512]{2,1,0:T(8,128)}, bf16[8,256,512]{2,1,0:T(8,128)...) custom-call(bf16[256,2048]{1,0:T(8,128)(2,1)} %collective-permute-do, ...), custom_call_target="tpu_custom_call", output_to_operand_aliasing={{0}: (7, {}), {1}: (8, {}), {2}: (9, {}), {3}: (10, {})} | custom-call | tf_op jit(solution)/shard_map/mixer_forward/pallas_call | solution.py:111
  224.6 12.0 %mixer_forward.7 = (bf16[8,256,2048]{2,1,0:T(8,128)(2,1)}, bf16[8,256,1024]{2,1,0:T(8,128)(2,1)}, f32[8,256,512]{2,1,0:T(8,128)}, bf16[8,256,512]{2,1,0:T(8,128)...) custom-call(bf16[256,2048]{1,0:T(8,128)(2,1)} %bitcast.161, ...), custom_call_target="tpu_custom_call", output_to_operand_aliasing={{0}: (7, {}), {1}: (8, {}), {2}: (9, {}), {3}: (10, {})} | custom-call | tf_op jit(solution)/shard_map/mixer_forward/pallas_call | solution.py:111
  237.8 17.3 %all-gather.9.cloned.1.call-done = bf16[4,512,1024]{2,1,0:T(8,128)(2,1)} async-done(((bf16[4,128,1024]{2,1,0:T(8,128)(2,1)}), bf16[4,512,1024]{2,1,0:T(8,128)(2,1)}) %all-gather.9.cloned.1.call-update) | async-done | bytes 4194320 | tf_op jit(solution)/shard_map/all_gather | solution.py:338
  256.1 3.9 fusion.31
  267.1 6.9 feed_forward.4
  278.7 9.0 %collective-permute-done.31.refs_0_ = bf16[128,2048]{1,0:T(8,128)(2,1)S(1)} collective-permute-done((bf16[128,2048]{1,0:T(8,128)(2,1)}, bf16[128,2048]{1,0:T(8,128)(2,1)S(1)}, u32[]{:S(2)}, u32[]{:S(2)}) %collective-permute-start.31) | collective-permute-done | bytes 524320 | tf_op jit(solution)/shard_map/ppermute | solution.py:222
  293.3 6.9 feed_forward.5
  305.6 6.9 feed_forward.6
  313.5 6.8 feed_forward.7
  320.3 10.2 %bitcast_convert_fusion.2.refs_5_.refs_6_ = bf16[512,2048]{1,0:T(8,128)(2,1)} fusion(bf16[8,256,512]{2,1,0:T(8,128)(2,1)} %get-tuple-element.169.refs_2_, bf16[8,256,2048]{2,1,0:T(8,128)(2,1)} %dynamic-slice_dynamic-update-slice_fusion.refs_9_.refs_11_.refs_4_), kind=kOutput, calls=%fused_computation.6 | convolution fusion | flops 4296015872 | bytes 12582912 | tf_op jit(solution)/shard_map/dot_general | solution.py:29
  330.5 9.9 %feed_backward.4 = (bf16[8,256,1024]{2,1,0:T(8,128)(2,1)}, bf16[256,2048]{1,0:T(8,128)(2,1)}, bf16[256,2048]{1,0:T(8,128)(2,1)}, bf16[256,2048]{1,0:T(8,128)(2,1)}, bf16[256,2048]{1,0:T(8,128)(2,1)}) custom-call(bf16[2048,1024]{1,0:T(8,128)(2,1)} %bitcast.140, bf16[512,2048]{1,0:T(8,128)(2,1)} %all-gather.11.cloned.1.call-done.refs_8_.refs_1_, ...), custom_call_target="tpu_custom_call" | custom-call | tf_op jit(solution)/shard_map/feed_backward/pallas_call | solution.py:111
  340.9 10.3 %feed_backward.5 = (bf16[8,256,1024]{2,1,0:T(8,128)(2,1)}, bf16[256,2048]{1,0:T(8,128)(2,1)}, bf16[256,2048]{1,0:T(8,128)(2,1)}, bf16[256,2048]{1,0:T(8,128)(2,1)}, bf16[256,2048]{1,0:T(8,128)(2,1)}) custom-call(bf16[2048,1024]{1,0:T(8,128)(2,1)} %bitcast.141, ...), custom_call_target="tpu_custom_call", output_to_operand_aliasing={{0}: (5, {})} | custom-call | tf_op jit(solution)/shard_map/feed_backward/pallas_call | solution.py:111
  354.6 10.0 %feed_backward.6 = (bf16[8,256,1024]{2,1,0:T(8,128)(2,1)}, bf16[256,2048]{1,0:T(8,128)(2,1)}, bf16[256,2048]{1,0:T(8,128)(2,1)}, bf16[256,2048]{1,0:T(8,128)(2,1)}, bf16[256,2048]{1,0:T(8,128)(2,1)}) custom-call(bf16[2048,1024]{1,0:T(8,128)(2,1)} %bitcast.142, ...), custom_call_target="tpu_custom_call", output_to_operand_aliasing={{0}: (5, {})} | custom-call | tf_op jit(solution)/shard_map/feed_backward/pallas_call | solution.py:111
  374.3 10.2 %feed_backward.7 = (bf16[8,256,1024]{2,1,0:T(8,128)(2,1)}, bf16[256,2048]{1,0:T(8,128)(2,1)}, bf16[256,2048]{1,0:T(8,128)(2,1)}, bf16[256,2048]{1,0:T(8,128)(2,1)}, bf16[256,2048]{1,0:T(8,128)(2,1)}) custom-call(bf16[2048,1024]{1,0:T(8,128)(2,1)} %bitcast.143, ...), custom_call_target="tpu_custom_call", output_to_operand_aliasing={{0}: (5, {})} | custom-call | tf_op jit(solution)/shard_map/feed_backward/pallas_call | solution.py:111
  384.4 14.0 %bitcast_convert_fusion.1.refs_2_ = bf16[2048,1024]{1,0:T(8,128)(2,1)} fusion(bf16[8,256,2048]{2,1,0:T(8,128)(2,1)} %get-tuple-element.192, bf16[8,256,1024]{2,1,0:T(8,128)(2,1)} %get-tuple-element.193), kind=kOutput, calls=%fused_computation.1 | convolution fusion | flops 8592031744 | bytes 16777216 | tf_op jit(solution)/shard_map/dot_general | solution.py:29
  412.4 13.0 %mixer_backward.4 = (bf16[8,256,2048]{2,1,0:T(8,128)(2,1)}, bf16[8,256,512]{2,1,0:T(8,128)(2,1)}, bf16[8,256,1024]{2,1,0:T(8,128)(2,1)}, bf16[256,2048]{1,0:T(8,128)(2,1)}, bf16[256,2048]{1,0:T(8,128)(2,1)}) custom-call(bf16[256,2048]{1,0:T(8,128)(2,1)} %copy-done.20, bf16[256,2048]{1,0:T(8,128)(2,1)} %collective-permute-done.51.refs_1_, ...), custom_call_target="tpu_custom_call" | custom-call | flops 20000000000 | tf_op jit(solution)/shard_map/mixer_backward/pallas_call | solution.py:111
  425.4 8.8 %collective-permute-done.50.refs_1_ = bf16[128,2048]{1,0:T(8,128)(2,1)} collective-permute-done((bf16[128,2048]{1,0:T(8,128)(2,1)}, bf16[128,2048]{1,0:T(8,128)(2,1)}, u32[]{:S(2)}, u32[]{:S(2)}) %collective-permute-start.50) | collective-permute-done | bytes 524320 | tf_op jit(solution)/shard_map/ppermute | solution.py:222
  439.0 13.4 %mixer_backward.5 = (bf16[8,256,2048]{2,1,0:T(8,128)(2,1)}, bf16[8,256,512]{2,1,0:T(8,128)(2,1)}, bf16[8,256,1024]{2,1,0:T(8,128)(2,1)}, bf16[256,2048]{1,0:T(8,128)(2,1)}, bf16[256,2048]{1,0:T(8,128)(2,1)}) custom-call(bf16[128,2048]{1,0:T(8,128)(2,1)} %get-tuple-element.200.refs_0_, ...), custom_call_target="tpu_custom_call", output_to_operand_aliasing={{0}: (10, {}), {1}: (11, {}), {2}: (12, {})} | custom-call | flops 20000000000 | tf_op jit(solution)/shard_map/mixer_backward/pallas_call | solution.py:111
  454.0 13.1 %mixer_backward.6 = (bf16[8,256,2048]{2,1,0:T(8,128)(2,1)}, bf16[8,256,512]{2,1,0:T(8,128)(2,1)}, bf16[8,256,1024]{2,1,0:T(8,128)(2,1)}, bf16[256,2048]{1,0:T(8,128)(2,1)}, bf16[256,2048]{1,0:T(8,128)(2,1)}) custom-call(bf16[128,2048]{1,0:T(8,128)(2,1)} %get-tuple-element.216.refs_0_, ...), custom_call_target="tpu_custom_call", output_to_operand_aliasing={{0}: (10, {}), {1}: (11, {}), {2}: (12, {})} | custom-call | flops 20000000000 | tf_op jit(solution)/shard_map/mixer_backward/pallas_call | solution.py:111
  468.1 13.1 %mixer_backward.7 = (bf16[8,256,2048]{2,1,0:T(8,128)(2,1)}, bf16[8,256,512]{2,1,0:T(8,128)(2,1)}, bf16[8,256,1024]{2,1,0:T(8,128)(2,1)}, bf16[256,2048]{1,0:T(8,128)(2,1)}, bf16[256,2048]{1,0:T(8,128)(2,1)}) custom-call(bf16[128,2048]{1,0:T(8,128)(2,1)} %get-tuple-element.217.refs_0_, ...), custom_call_target="tpu_custom_call", output_to_operand_aliasing={{0}: (10, {}), {1}: (11, {}), {2}: (12, {})} | custom-call | flops 20000000000 | tf_op jit(solution)/shard_map/mixer_backward/pallas_call | solution.py:111
  481.2 10.1 %convolution_convert_fusion = bf16[2048,512]{1,0:T(8,128)(2,1)} fusion(bf16[2048,2048]{1,0:T(8,128)(2,1)} %bitcast.152, bf16[2048,512]{1,0:T(8,128)(2,1)} %after.32), kind=kOutput, calls=%fused_computation.10 | convolution fusion | flops 4296015872 | bytes 12582912 | tf_op jit(solution)/shard_map/dot_general | solution.py:29
  491.4 14.0 %bitcast_convert_fusion = bf16[2048,1024]{1,0:T(8,128)(2,1)} fusion(bf16[8,256,2048]{2,1,0:T(8,128)(2,1)} %get-tuple-element.229, bf16[8,256,1024]{2,1,0:T(8,128)(2,1)} %get-tuple-element.241), kind=kOutput, calls=%fused_computation | convolution fusion | flops 8592031744 | bytes 16777216 | tf_op jit(solution)/shard_map/dot_general | solution.py:29
  517.7 8.9 %collective-permute-done.57.refs_0_ = bf16[128,2048]{1,0:T(8,128)(2,1)} collective-permute-done((bf16[128,2048]{1,0:T(8,128)(2,1)S(1)}, bf16[128,2048]{1,0:T(8,128)(2,1)}, u32[]{:S(2)}, u32[]{:S(2)}) %collective-permute-start.57) | collective-permute-done | bytes 524320 | tf_op jit(solution)/shard_map/ppermute | solution.py:222
  537.0 6.6 collective-permute-done.75.refs_0_
  548.0 3.8 all-to-all-start.4
  561.2 23.8 %all-to-all-done.4.refs_1_ = bf16[8,64,1024]{2,1,0:T(8,128)(2,1)S(1)} async-done(((bf16[8,64,1024]{2,1,0:T(8,128)(2,1)}), bf16[8,64,1024]{2,1,0:T(8,128)(2,1)S(1)}, u32[]{:S(2)}, u32[]{:S(2)}) %all-to-all-start.4) | async-done | bytes 1048608 | tf_op jit(solution)/shard_map/all_to_all | solution.py:335
  585.9 8.6 %convolution_convert_fusion.1.refs_2_ = bf16[512,2048]{1,0:T(8,128)(2,1)S(1)} fusion(bf16[2048,512]{1,0:T(8,128)(2,1)} %bitcast.165, bf16[2048,2048]{1,0:T(8,128)(2,1)} %after.30), kind=kOutput, calls=%fused_computation.11 | convolution fusion | flops 4296015872 | bytes 12582912 | tf_op jit(solution)/shard_map/dot_general | solution.py:29
  595.9 6.3 all_to_all.64
  602.1 4.2 all-to-all-start.9
  610.0 4.6 all-to-all-done.9
  617.2 3.6 add_convert_fusion.3
  622.5 11.1 %collective-permute-done.79.refs_1_ = bf16[256,2048]{1,0:T(8,128)(2,1)} collective-permute-done((bf16[256,2048]{1,0:T(8,128)(2,1)}, bf16[256,2048]{1,0:T(8,128)(2,1)}, u32[]{:S(2)}, u32[]{:S(2)}) %collective-permute-start.79) | collective-permute-done | bytes 1048608 | tf_op jit(solution)/shard_map/ppermute | solution.py:222
  633.6 4.8 fusion.10
  639.4 5.7 all-to-all-start.7
  647.7 8.4 %collective-permute-done.69 = bf16[256,2048]{1,0:T(8,128)(2,1)S(1)} collective-permute-done((bf16[256,2048]{1,0:T(8,128)(2,1)}, bf16[256,2048]{1,0:T(8,128)(2,1)S(1)}, u32[]{:S(2)}, u32[]{:S(2)}) %collective-permute-start.69) | collective-permute-done | bytes 1048608 | tf_op jit(solution)/shard_map/ppermute | solution.py:222
  662.3 3.8 all-to-all-start.5
  678.0 4.2 all-to-all-start.6
  692.2 5.4 all-to-all-done.6
  (482 shorter events, 223.7 us)
Async XLA Ops:
  7.2 145.1 %all-gather.7.cloned.1.call-start = ((), (), s32[]{:S(2)}) async-start(), calls=%async_computation.16 | async-start | bytes 2621440 | tf_op jit(solution)/shard_map/all_gather | solution.py:353
  7.9 166.1 %all-gather.5.cloned.1.call-start = ((), (), s32[]{:S(2)}) async-start(), calls=%async_computation.15 | async-start | bytes 7864320 | tf_op jit(solution)/shard_map/all_gather | solution.py:338
  37.6 69.6 %collective-permute-start.3 = (bf16[256,2048]{1,0:T(8,128)(2,1)S(1)}, bf16[256,2048]{1,0:T(8,128)(2,1)}, u32[]{:S(2)}, u32[]{:S(2)}) collective-permute-start(bf16[256,2048]{1,0:T(8,128)(2,1)S(1)} %bitcast.162), channel_id=1, source_target_pairs={{0,8},{8,0},{1,9},{9,1},{2,10},{10,2},{3,11},{11,3},{4,12},{12,4},... | collective-permute-start | bytes 3145736 | tf_op jit(solution)/shard_map/ppermute | solution.py:222
  38.3 67.3 %collective-permute-start.1 = (bf16[256,2048]{1,0:T(8,128)(2,1)S(1)}, bf16[256,2048]{1,0:T(8,128)(2,1)}, u32[]{:S(2)}, u32[]{:S(2)}) collective-permute-start(bf16[256,2048]{1,0:T(8,128)(2,1)S(1)} %bitcast.163), channel_id=1, source_target_pairs={{0,16},{16,0},{1,17},{17,1},{2,18},{18,2},{3,19},{19,3},{4,20},{20... | collective-permute-start | bytes 3145736 | tf_op jit(solution)/shard_map/ppermute | solution.py:222
  40.7 69.4 %collective-permute-start.9 = (bf16[256,2048]{1,0:T(8,128)(2,1)}, bf16[256,2048]{1,0:T(8,128)(2,1)}, u32[]{:S(2)}, u32[]{:S(2)}) collective-permute-start(bf16[256,2048]{1,0:T(8,128)(2,1)} %fusion.14), channel_id=1, source_target_pairs={{0,1},{1,0},{2,3},{3,2},{4,5},{5,4},{6,7},{7,6},{8,9},{9,8},{10,11... | collective-permute-start | bytes 3145736 | tf_op jit(solution)/shard_map/ppermute | solution.py:222
  40.7 51.4 %collective-permute-start.10 = (bf16[256,2048]{1,0:T(8,128)(2,1)}, bf16[256,2048]{1,0:T(8,128)(2,1)}, u32[]{:S(2)}, u32[]{:S(2)}) collective-permute-start(bf16[256,2048]{1,0:T(8,128)(2,1)} %fusion.14), channel_id=1, source_target_pairs={{0,8},{8,0},{1,9},{9,1},{2,10},{10,2},{3,11},{11,3},{4,12},{12,4},... | collective-permute-start | bytes 3145736 | tf_op jit(solution)/shard_map/ppermute | solution.py:222
  42.2 69.4 %collective-permute-start.12 = (bf16[256,2048]{1,0:T(8,128)(2,1)}, bf16[256,2048]{1,0:T(8,128)(2,1)}, u32[]{:S(2)}, u32[]{:S(2)}) collective-permute-start(bf16[256,2048]{1,0:T(8,128)(2,1)} %fusion.14), channel_id=1, source_target_pairs={{0,16},{16,0},{1,17},{17,1},{2,18},{18,2},{3,19},{19,3},{4,20},{20... | collective-permute-start | bytes 3145736 | tf_op jit(solution)/shard_map/ppermute | solution.py:222
  44.4 41.3 %all-to-all-start = ((bf16[32,2,128]{2,1,0:T(2,128)(2,1)}), bf16[32,2,128]{2,1,0:T(2,128)(2,1)S(1)}, u32[]{:S(2)}, u32[]{:S(2)}) async-start(bf16[32,2,128]{2,1,0:T(2,128)(2,1)} %reshape.720), calls=%async_computation | async-start | bytes 32768 | tf_op jit(solution)/shard_map/all_to_all | solution.py:335
  89.2 165.8 %all-gather.9.cloned.1.call-start = ((), (), s32[]{:S(2)}) async-start(), calls=%async_computation.17 | async-start | bytes 5242880 | tf_op jit(solution)/shard_map/all_gather | solution.py:338
  92.1 25.2 %collective-permute-start.11 = (bf16[256,2048]{1,0:T(8,128)(2,1)}, bf16[256,2048]{1,0:T(8,128)(2,1)S(1)}, u32[]{:S(2)}, u32[]{:S(2)}) collective-permute-start(bf16[256,2048]{1,0:T(8,128)(2,1)} %collective-permute-done.10), channel_id=1, source_target_pairs={{0,1},{1,0},{2,3},{3,2},{4,5},{5,4},{6,7},{7,6},{8,9},{9,8},{10,11... | collective-permute-start | bytes 3145736 | tf_op jit(solution)/shard_map/ppermute | solution.py:222
  110.1 23.2 %collective-permute-start.15 = (bf16[128,2048]{1,0:T(8,128)(2,1)S(1)}, bf16[128,2048]{1,0:T(8,128)(2,1)S(1)}, u32[]{:S(2)}, u32[]{:S(2)}) collective-permute-start(bf16[128,2048]{1,0:T(8,128)(2,1)S(1)} %slice.147), channel_id=1, source_target_pairs={{0,16},{16,0},{1,17},{17,1},{2,18},{18,2},{3,19},{19,3},{4,20},{20... | collective-permute-start | bytes 1572872 | tf_op jit(solution)/shard_map/ppermute | solution.py:222
  111.6 22.3 %collective-permute-start.13 = (bf16[256,2048]{1,0:T(8,128)(2,1)}, bf16[256,2048]{1,0:T(8,128)(2,1)S(1)}, u32[]{:S(2)}, u32[]{:S(2)}) collective-permute-start(bf16[256,2048]{1,0:T(8,128)(2,1)} %collective-permute-done.12), channel_id=1, source_target_pairs={{0,1},{1,0},{2,3},{3,2},{4,5},{5,4},{6,7},{7,6},{8,9},{9,8},{10,11... | collective-permute-start | bytes 3145736 | tf_op jit(solution)/shard_map/ppermute | solution.py:222
  122.3 64.2 %collective-permute-start.4 = (bf16[256,2048]{1,0:T(8,128)(2,1)}, bf16[256,2048]{1,0:T(8,128)(2,1)}, u32[]{:S(2)}, u32[]{:S(2)}) collective-permute-start(bf16[256,2048]{1,0:T(8,128)(2,1)} %collective-permute-done.3.refs_0_), channel_id=1, source_target_pairs={{0,1},{1,0},{2,3},{3,2},{4,5},{5,4},{6,7},{7,6},{8,9},{9,8},{10,11... | collective-permute-start | bytes 3145736 | tf_op jit(solution)/shard_map/ppermute | solution.py:222
  123.3 33.1 %collective-permute-start.7 = (bf16[128,2048]{1,0:T(8,128)(2,1)}, bf16[128,2048]{1,0:T(8,128)(2,1)}, u32[]{:S(2)}, u32[]{:S(2)}) collective-permute-start(bf16[128,2048]{1,0:T(8,128)(2,1)} %collective-permute-done.5.refs_0_), channel_id=1, source_target_pairs={{0,1},{1,0},{2,3},{3,2},{4,5},{5,4},{6,7},{7,6},{8,9},{9,8},{10,11... | collective-permute-start | bytes 1572872 | tf_op jit(solution)/shard_map/ppermute | solution.py:222
  133.3 23.0 %collective-permute-start.8 = (bf16[128,2048]{1,0:T(8,128)(2,1)}, bf16[128,2048]{1,0:T(8,128)(2,1)}, u32[]{:S(2)}, u32[]{:S(2)}) collective-permute-start(bf16[128,2048]{1,0:T(8,128)(2,1)} %collective-permute-done.6.refs_1_), channel_id=1, source_target_pairs={{0,1},{1,0},{2,3},{3,2},{4,5},{5,4},{6,7},{7,6},{8,9},{9,8},{10,11... | collective-permute-start | bytes 1572872 | tf_op jit(solution)/shard_map/ppermute | solution.py:222
  156.1 156.4 %all-gather.11.cloned.1.call-start = ((), (), s32[]{:S(2)}) async-start(), calls=%async_computation.18 | async-start | bytes 2621440 | tf_op jit(solution)/shard_map/all_gather | solution.py:369
  198.5 19.1 %collective-permute-start.19 = (bf16[256,2048]{1,0:T(8,128)(2,1)}, bf16[256,2048]{1,0:T(8,128)(2,1)S(1)}, u32[]{:S(2)}, u32[]{:S(2)}) collective-permute-start(bf16[256,2048]{1,0:T(8,128)(2,1)} %get-tuple-element.143), channel_id=1, source_target_pairs={{0,1},{1,0},{2,3},{3,2},{4,5},{5,4},{6,7},{7,6},{8,9},{9,8},{10,11... | collective-permute-start | bytes 3145736 | tf_op jit(solution)/shard_map/ppermute | solution.py:222
  220.7 34.4 %collective-permute-start.24 = (bf16[256,2048]{1,0:T(8,128)(2,1)S(1)}, bf16[256,2048]{1,0:T(8,128)(2,1)}, u32[]{:S(2)}, u32[]{:S(2)}) collective-permute-start(bf16[256,2048]{1,0:T(8,128)(2,1)S(1)} %add_convert_fusion.12.refs_13_), channel_id=1, source_target_pairs={{0,8},{8,0},{1,9},{9,1},{2,10},{10,2},{3,11},{11,3},{4,12},{12,4},... | collective-permute-start | bytes 3145736 | tf_op jit(solution)/shard_map/ppermute | solution.py:222
  224.0 31.1 %collective-permute-start.25 = (bf16[256,2048]{1,0:T(8,128)(2,1)}, bf16[256,2048]{1,0:T(8,128)(2,1)}, u32[]{:S(2)}, u32[]{:S(2)}) collective-permute-start(bf16[256,2048]{1,0:T(8,128)(2,1)} %add_convert_fusion.11.refs_14_), channel_id=1, source_target_pairs={{0,16},{16,0},{1,17},{17,1},{2,18},{18,2},{3,19},{19,3},{4,20},{20... | collective-permute-start | bytes 3145736 | tf_op jit(solution)/shard_map/ppermute | solution.py:222
  236.7 161.8 %reduce-scatter.6.cloned.1.call-start = ((), (), s32[]{:S(2)}) async-start(), calls=%async_computation.19 | async-start | bytes 2621440 | tf_op jit(solution)/shard_map/reduce_scatter | solution.py:452
  265.0 22.7 %collective-permute-start.31 = (bf16[128,2048]{1,0:T(8,128)(2,1)}, bf16[128,2048]{1,0:T(8,128)(2,1)S(1)}, u32[]{:S(2)}, u32[]{:S(2)}) collective-permute-start(bf16[128,2048]{1,0:T(8,128)(2,1)} %get-tuple-element.272), channel_id=1, source_target_pairs={{0,8},{8,0},{1,9},{9,1},{2,10},{10,2},{3,11},{11,3},{4,12},{12,4},... | collective-permute-start | bytes 1572872 | tf_op jit(solution)/shard_map/ppermute | solution.py:222
  265.6 23.4 %collective-permute-start.32 = (bf16[128,2048]{1,0:T(8,128)(2,1)}, bf16[128,2048]{1,0:T(8,128)(2,1)}, u32[]{:S(2)}, u32[]{:S(2)}) collective-permute-start(bf16[128,2048]{1,0:T(8,128)(2,1)} %get-tuple-element.273), channel_id=1, source_target_pairs={{0,16},{16,0},{1,17},{17,1},{2,18},{18,2},{3,19},{19,3},{4,20},{20... | collective-permute-start | bytes 1572872 | tf_op jit(solution)/shard_map/ppermute | solution.py:222
  340.4 140.8 %reduce-scatter.8.cloned.1.call-start = ((), (), s32[]{:S(2)}) async-start(), calls=%async_computation.20 | async-start | bytes 5242880 | tf_op jit(solution)/shard_map/reduce_scatter | solution.py:484
  370.5 28.0 %collective-permute-start.45 = (bf16[256,2048]{1,0:T(8,128)(2,1)S(1)}, bf16[256,2048]{1,0:T(8,128)(2,1)S(1)}, u32[]{:S(2)}, u32[]{:S(2)}) collective-permute-start(bf16[256,2048]{1,0:T(8,128)(2,1)S(1)} %add_convert_fusion.8.refs_8_), channel_id=1, source_target_pairs={{0,8},{8,0},{1,9},{9,1},{2,10},{10,2},{3,11},{11,3},{4,12},{12,4},... | collective-permute-start | bytes 3145736 | tf_op jit(solution)/shard_map/ppermute | solution.py:222
  373.1 25.3 %collective-permute-start.46 = (bf16[256,2048]{1,0:T(8,128)(2,1)S(1)}, bf16[256,2048]{1,0:T(8,128)(2,1)}, u32[]{:S(2)}, u32[]{:S(2)}) collective-permute-start(bf16[256,2048]{1,0:T(8,128)(2,1)S(1)} %add_convert_fusion.7.refs_9_), channel_id=1, source_target_pairs={{0,16},{16,0},{1,17},{17,1},{2,18},{18,2},{3,19},{19,3},{4,20},{20... | collective-permute-start | bytes 3145736 | tf_op jit(solution)/shard_map/ppermute | solution.py:222
  406.9 255.4 %reduce-scatter.10.cloned.1.call-start = ((), (), s32[]{:S(2)}) async-start(), calls=%async_computation.21 | async-start | bytes 2621440 | tf_op jit(solution)/shard_map/reduce_scatter | solution.py:484
  408.4 26.6 %collective-permute-start.48 = (bf16[128,2048]{1,0:T(8,128)(2,1)}, bf16[128,2048]{1,0:T(8,128)(2,1)}, u32[]{:S(2)}, u32[]{:S(2)}) collective-permute-start(bf16[128,2048]{1,0:T(8,128)(2,1)} %get-tuple-element.268), channel_id=1, source_target_pairs={{0,16},{16,0},{1,17},{17,1},{2,18},{18,2},{3,19},{19,3},{4,20},{20... | collective-permute-start | bytes 1572872 | tf_op jit(solution)/shard_map/ppermute | solution.py:222
  410.5 24.4 %collective-permute-start.47 = (bf16[128,2048]{1,0:T(8,128)(2,1)}, bf16[128,2048]{1,0:T(8,128)(2,1)}, u32[]{:S(2)}, u32[]{:S(2)}) collective-permute-start(bf16[128,2048]{1,0:T(8,128)(2,1)} %get-tuple-element.269), channel_id=1, source_target_pairs={{0,8},{8,0},{1,9},{9,1},{2,10},{10,2},{3,11},{11,3},{4,12},{12,4},... | collective-permute-start | bytes 1572872 | tf_op jit(solution)/shard_map/ppermute | solution.py:222
  411.4 22.9 %collective-permute-start.50 = (bf16[128,2048]{1,0:T(8,128)(2,1)}, bf16[128,2048]{1,0:T(8,128)(2,1)}, u32[]{:S(2)}, u32[]{:S(2)}) collective-permute-start(bf16[128,2048]{1,0:T(8,128)(2,1)} %get-tuple-element.269), channel_id=1, source_target_pairs={{0,16},{16,0},{1,17},{17,1},{2,18},{18,2},{3,19},{19,3},{4,20},{20... | collective-permute-start | bytes 1572872 | tf_op jit(solution)/shard_map/ppermute | solution.py:222
  491.4 186.6 %reduce-scatter.12.cloned.1.call-start = ((), (), s32[]{:S(2)}) async-start(), calls=%async_computation.22 | async-start | bytes 5242880 | tf_op jit(solution)/shard_map/reduce_scatter | solution.py:484
  509.7 123.9 %collective-permute-start.72 = (bf16[256,2048]{1,0:T(8,128)(2,1)}, bf16[256,2048]{1,0:T(8,128)(2,1)}, u32[]{:S(2)}, u32[]{:S(2)}) collective-permute-start(bf16[256,2048]{1,0:T(8,128)(2,1)} %get-tuple-element.198.refs_2_), channel_id=1, source_target_pairs={{0,1},{1,0},{2,3},{3,2},{4,5},{5,4},{6,7},{7,6},{8,9},{9,8},{10,11... | collective-permute-start | bytes 3145736 | tf_op jit(solution)/shard_map/ppermute | solution.py:222
  509.7 19.3 %collective-permute-start.55 = (bf16[256,2048]{1,0:T(8,128)(2,1)}, bf16[256,2048]{1,0:T(8,128)(2,1)}, u32[]{:S(2)}, u32[]{:S(2)}) collective-permute-start(bf16[256,2048]{1,0:T(8,128)(2,1)} %get-tuple-element.208), channel_id=1, source_target_pairs={{0,1},{1,0},{2,3},{3,2},{4,5},{5,4},{6,7},{7,6},{8,9},{9,8},{10,11... | collective-permute-start | bytes 3145736 | tf_op jit(solution)/shard_map/ppermute | solution.py:222
  510.2 22.5 %collective-permute-start.60 = (bf16[256,2048]{1,0:T(8,128)(2,1)}, bf16[256,2048]{1,0:T(8,128)(2,1)}, u32[]{:S(2)}, u32[]{:S(2)}) collective-permute-start(bf16[256,2048]{1,0:T(8,128)(2,1)} %get-tuple-element.213), channel_id=1, source_target_pairs={{0,1},{1,0},{2,3},{3,2},{4,5},{5,4},{6,7},{7,6},{8,9},{9,8},{10,11... | collective-permute-start | bytes 3145736 | tf_op jit(solution)/shard_map/ppermute | solution.py:222
  526.6 25.3 %collective-permute-start.73 = (bf16[256,2048]{1,0:T(8,128)(2,1)}, bf16[256,2048]{1,0:T(8,128)(2,1)}, u32[]{:S(2)}, u32[]{:S(2)}) collective-permute-start(bf16[256,2048]{1,0:T(8,128)(2,1)} %get-tuple-element.204.refs_8_.refs_2_), channel_id=1, source_target_pairs={{0,1},{1,0},{2,3},{3,2},{4,5},{5,4},{6,7},{7,6},{8,9},{9,8},{10,11... | collective-permute-start | bytes 3145736 | tf_op jit(solution)/shard_map/ppermute | solution.py:222
  527.7 29.3 %collective-permute-start.78 = (bf16[256,2048]{1,0:T(8,128)(2,1)}, bf16[256,2048]{1,0:T(8,128)(2,1)}, u32[]{:S(2)}, u32[]{:S(2)}) collective-permute-start(bf16[256,2048]{1,0:T(8,128)(2,1)} %get-tuple-element.237), channel_id=1, source_target_pairs={{0,1},{1,0},{2,3},{3,2},{4,5},{5,4},{6,7},{7,6},{8,9},{9,8},{10,11... | collective-permute-start | bytes 3145736 | tf_op jit(solution)/shard_map/ppermute | solution.py:222
  543.5 72.5 %collective-permute-start.54 = (bf16[256,2048]{1,0:T(8,128)(2,1)}, bf16[256,2048]{1,0:T(8,128)(2,1)}, u32[]{:S(2)}, u32[]{:S(2)}) collective-permute-start(bf16[256,2048]{1,0:T(8,128)(2,1)} %get-tuple-element.206), channel_id=1, source_target_pairs={{0,1},{1,0},{2,3},{3,2},{4,5},{5,4},{6,7},{7,6},{8,9},{9,8},{10,11... | collective-permute-start | bytes 3145736 | tf_op jit(solution)/shard_map/ppermute | solution.py:222
  546.5 60.5 %collective-permute-start.59 = (bf16[256,2048]{1,0:T(8,128)(2,1)}, bf16[256,2048]{1,0:T(8,128)(2,1)}, u32[]{:S(2)}, u32[]{:S(2)}) collective-permute-start(bf16[256,2048]{1,0:T(8,128)(2,1)} %add_convert_fusion.5), channel_id=1, source_target_pairs={{0,8},{8,0},{1,9},{9,1},{2,10},{10,2},{3,11},{11,3},{4,12},{12,4},... | collective-permute-start | bytes 3145736 | tf_op jit(solution)/shard_map/ppermute | solution.py:222
  548.0 36.9 %all-to-all-start.4 = ((bf16[8,64,1024]{2,1,0:T(8,128)(2,1)}), bf16[8,64,1024]{2,1,0:T(8,128)(2,1)S(1)}, u32[]{:S(2)}, u32[]{:S(2)}) async-start(bf16[8,64,1024]{2,1,0:T(8,128)(2,1)} %bitcast.172), calls=%async_computation.6 | async-start | bytes 2097152 | tf_op jit(solution)/shard_map/all_to_all | solution.py:335
  551.8 64.2 %collective-permute-start.61 = (bf16[256,2048]{1,0:T(8,128)(2,1)}, bf16[256,2048]{1,0:T(8,128)(2,1)}, u32[]{:S(2)}, u32[]{:S(2)}) collective-permute-start(bf16[256,2048]{1,0:T(8,128)(2,1)} %add_convert_fusion.4), channel_id=1, source_target_pairs={{0,16},{16,0},{1,17},{17,1},{2,18},{18,2},{3,19},{19,3},{4,20},{20... | collective-permute-start | bytes 3145736 | tf_op jit(solution)/shard_map/ppermute | solution.py:222
  557.0 65.5 %collective-permute-start.77 = (bf16[256,2048]{1,0:T(8,128)(2,1)}, bf16[256,2048]{1,0:T(8,128)(2,1)}, u32[]{:S(2)}, u32[]{:S(2)}) collective-permute-start(bf16[256,2048]{1,0:T(8,128)(2,1)} %add_convert_fusion.1), channel_id=1, source_target_pairs={{0,8},{8,0},{1,9},{9,1},{2,10},{10,2},{3,11},{11,3},{4,12},{12,4},... | collective-permute-start | bytes 3145736 | tf_op jit(solution)/shard_map/ppermute | solution.py:222
  606.3 83.7 %reduce-scatter.14.cloned.1.call-start = ((), (), s32[]{:S(2)}) async-start(), calls=%async_computation.23 | async-start | bytes 2621440 | tf_op jit(solution)/shard_map/reduce_scatter | solution.py:521
  607.1 26.5 %collective-permute-start.79 = (bf16[256,2048]{1,0:T(8,128)(2,1)}, bf16[256,2048]{1,0:T(8,128)(2,1)}, u32[]{:S(2)}, u32[]{:S(2)}) collective-permute-start(bf16[256,2048]{1,0:T(8,128)(2,1)} %add_convert_fusion), channel_id=1, source_target_pairs={{0,16},{16,0},{1,17},{17,1},{2,18},{18,2},{3,19},{19,3},{4,20},{20... | collective-permute-start | bytes 3145736 | tf_op jit(solution)/shard_map/ppermute | solution.py:222
  620.8 25.0 %collective-permute-start.68 = (bf16[256,2048]{1,0:T(8,128)(2,1)}, bf16[256,2048]{1,0:T(8,128)(2,1)S(1)}, u32[]{:S(2)}, u32[]{:S(2)}) collective-permute-start(bf16[256,2048]{1,0:T(8,128)(2,1)} %add_convert_fusion.3), channel_id=1, source_target_pairs={{0,8},{8,0},{1,9},{9,1},{2,10},{10,2},{3,11},{11,3},{4,12},{12,4},... | collective-permute-start | bytes 3145736 | tf_op jit(solution)/shard_map/ppermute | solution.py:222
  621.2 35.0 %collective-permute-start.69 = (bf16[256,2048]{1,0:T(8,128)(2,1)}, bf16[256,2048]{1,0:T(8,128)(2,1)S(1)}, u32[]{:S(2)}, u32[]{:S(2)}) collective-permute-start(bf16[256,2048]{1,0:T(8,128)(2,1)} %add_convert_fusion.3), channel_id=1, source_target_pairs={{0,16},{16,0},{1,17},{17,1},{2,18},{18,2},{3,19},{19,3},{4,20},{20... | collective-permute-start | bytes 3145736 | tf_op jit(solution)/shard_map/ppermute | solution.py:222
  639.4 22.9 %all-to-all-start.7 = ((f32[32,1,128]{2,1,0:T(1,128)}), f32[32,1,128]{2,1,0:T(1,128)S(1)}, u32[]{:S(2)}, u32[]{:S(2)}) async-start(f32[32,1,128]{2,1,0:T(1,128)} %reshape.722), calls=%async_computation.11 | async-start | bytes 32768 | tf_op jit(solution)/shard_map/all_to_all | solution.py:335
  646.8 35.4 %collective-permute-start.71 = (bf16[128,2048]{1,0:T(8,128)(2,1)}, bf16[128,2048]{1,0:T(8,128)(2,1)}, u32[]{:S(2)}, u32[]{:S(2)}) collective-permute-start(bf16[128,2048]{1,0:T(8,128)(2,1)} %slice.161), channel_id=1, source_target_pairs={{0,16},{16,0},{1,17},{17,1},{2,18},{18,2},{3,19},{19,3},{4,20},{20... | collective-permute-start | bytes 1572872 | tf_op jit(solution)/shard_map/ppermute | solution.py:222
  657.0 25.2 %collective-permute-start.70 = (bf16[128,2048]{1,0:T(8,128)(2,1)}, bf16[128,2048]{1,0:T(8,128)(2,1)}, u32[]{:S(2)}, u32[]{:S(2)}) collective-permute-start(bf16[128,2048]{1,0:T(8,128)(2,1)} %slice.160), channel_id=1, source_target_pairs={{0,8},{8,0},{1,9},{9,1},{2,10},{10,2},{3,11},{11,3},{4,12},{12,4},... | collective-permute-start | bytes 1572872 | tf_op jit(solution)/shard_map/ppermute | solution.py:222
  678.0 19.6 %all-to-all-start.6 = ((bf16[8,64,1024]{2,1,0:T(8,128)(2,1)}), bf16[8,64,1024]{2,1,0:T(8,128)(2,1)S(1)}, u32[]{:S(2)}, u32[]{:S(2)}) async-start(bf16[8,64,1024]{2,1,0:T(8,128)(2,1)} %bitcast.188), calls=%async_computation.10 | async-start | bytes 2097152 | tf_op jit(solution)/shard_map/all_to_all | solution.py:335
  (124 other events, 947.9 us)
Sparse Core Ops, SparseCore 0:
  9.6 48.7 all-gather.6
  59.9 114.0 all-gather.4
  176.1 78.9 all-gather.8
  256.5 44.1 all-gather.10
  340.5 41.8 reduce-scatter.5
  407.0 74.1 reduce-scatter.7
  491.5 44.1 reduce-scatter.9
  538.0 76.2 reduce-scatter.11
  616.5 44.4 reduce-scatter.13

commit v4 on v3

--- a/solution.py
+++ b/solution.py
@@ -218,6 +218,29 @@
         feed_parts[s][...] = dot(act_ref[s], down[...]).astype(BF16)
 
 
+def lay_out(received, places):
+    rows = received.shape[1]
+    widths = [sum(place[3] for place in listed) for listed in places]
+    if any(place[3] % 128 for listed in places for place in listed):
+        return [
+            jnp.concatenate(
+                [received[m, :, a : a + w] for m, a, _, w in sorted(listed, key=lambda place: place[2])], axis=1
+            ).astype(F32)
+            for listed in places
+        ]
+
+    def kernel(block, *outs):
+        for out, listed in zip(outs, places):
+            for m, a, b, w in listed:
+                out[:, b : b + w] = block[m, :, a : a + w].astype(F32)
+
+    return pl.pallas_call(
+        kernel,
+        out_shape=[jax.ShapeDtypeStruct((rows, width), F32) for width in widths],
+        name="lay_out",
+    )(received)
+
+
 def swap(field_in, axis):
     return lax.ppermute(field_in, axis, [(0, 1), (1, 0)])
 
@@ -491,7 +514,12 @@
     feed_summed = sum_layers(feed_product)
     feed_grads = to_owners(feed_summed)
 
+    feed_terms, held, leaving = GroupSum(), [], []
+
     def backward_call(n, chunk, earlier):
+        if n == 3:
+            held.extend(after([part for pair in feed_parts for part in pair], earlier[1][-1]))
+            leaving.append(feed_terms.terms(3, held[6:]))
         return chunk_call(
             mixer_backward,
             "mixer_backward",
@@ -502,7 +530,7 @@
             earlier[-1][:3] if earlier else None,
             [((length, breadth), BF16), ((length, 2 * KEY), BF16), ((length, 2 * VAL), BF16)],
             [(row_bytes, BF16)] * 2,
-            [],
+            leaving,
             2 * 10**10,
         )
 
@@ -510,27 +538,27 @@
     saved = results[-1][:3]
     out_grad, qk_grad, vg_grad = (a.reshape(GROUP * length, -1) for a in saved)
     (qk_grad,) = after([qk_grad], feed_summed)
+    leaving = [feed_terms.terms(number, held[2 * number :][:2]) for number in (1, 2)]
+    (vg_grad,) = after([vg_grad], *leaving)
+    feed_terms.terms(0, held[:2])
 
     normed_rows = mixer_normed.reshape(GROUP * length, breadth)
     qk_product = dot_rows(normed_rows, qk_grad).astype(BF16)
     vg_product = dot_rows(normed_rows, vg_grad).astype(BF16)
-    (out_grad,) = after([out_grad], feed_grads)
+    qk_grads = to_owners(sum_layers(qk_product))
+    (out_grad,) = after([out_grad], feed_grads, qk_grads)
     out_product = dot_rows(gated_all.reshape(GROUP * length, VAL), out_grad).astype(BF16)
-    qk_grads = to_owners(sum_layers(qk_product))
     vg_grads = to_owners(sum_layers(vg_product))
     output_grad = lax.psum_scatter(
         to_members(out_product, "core"), "z", scatter_dimension=0, tiled=True
     ).astype(F32)
 
-    held = after([part for pair in feed_parts for part in pair], results[1][-1])
-    summed = GroupSum()
-    for n in order:
-        summed.terms(n, held[2 * n : 2 * n + 2])
-    slot_out = (hidden_state + summed.total(out_product)).astype(BF16)
+    slot_out = (hidden_state + feed_terms.total()).astype(BF16)
     half = length // 2
     from_x, from_y = swap(slot_out, "x"), swap(slot_out, "y")
-    across = jnp.concatenate([swap(from_y[:half], "x"), swap(from_x[half:], "y")], axis=0)
-    (across,) = after([across], qk_grads)
+    across = jnp.concatenate(
+        after([swap(from_y[:half], "x"), swap(from_x[half:], "y")], vg_grads), axis=0
+    )
     reached = jnp.stack([slot_out, from_x, from_y, across])
     chosen = lax.dynamic_index_in_dim(reached, own_slot, 0, keepdims=False)
     out_tokens = (live_mask * chosen.astype(F32)).astype(BF16)
@@ -538,7 +566,7 @@
     summed = GroupSum()
     for n in order:
         summed.terms(n, results[n][3:5])
-    mixer_normed_grad = summed.total(out_product)
+    mixer_normed_grad = summed.total(out_product, vg_grads)
     mixer_hat, mixer_inverse = statistics(tokens[0].astype(F32), EPSILON)
     mixer_gain_part = jnp.sum(mixer_normed_grad * mixer_hat, axis=0)
     mixer_bias_part = jnp.sum(mixer_normed_grad, axis=0)
@@ -550,35 +578,46 @@
         split = jnp.stack(grads).reshape(len(grads), devices, -1).transpose(1, 0, 2)
         return jnp.sum(to_members(split, EVERY), axis=0)
 
-    feed_vectors = vector_grads(feed_gain_part, feed_bias_part)
-    mixer_vectors = vector_grads(mixer_gain_part, mixer_bias_part)
-
-    def head_back(grads):
-        return grads.transpose(1, 0, 2).reshape(local_model, -1)
-
-    def value_back(grads):
-        split = grads.reshape(4, 2, local_model, 2, half_layers, local_value)
-        return split.transpose(2, 0, 1, 4, 3, 5).reshape(local_model, -1)
-
-    def hidden_back(grads):
-        split = grads.reshape(4, 2, local_model, layers, local_hidden)
-        return split.transpose(2, 0, 3, 1, 4).reshape(local_model, -1)
+    vector_sums = vector_grads(mixer_gain_part, mixer_bias_part, feed_gain_part, feed_bias_part)
+
+    def head_places(at):
+        return [(member, at, member * KEY, KEY) for member in range(GROUP)]
+
+    def value_places(at):
+        return [
+            (member, at + (c * half_layers + l) * local_value, ((member * half_layers + l) * 2 + c) * local_value, local_value)
+            for member in range(GROUP)
+            for l in range(half_layers)
+            for c in range(2)
+        ]
+
+    def hidden_places(at):
+        return [
+            (f * 2 + c, at + l * local_hidden, ((f * layers + l) * 2 + c) * local_hidden, local_hidden)
+            for f in range(4)
+            for l in range(layers)
+            for c in range(2)
+        ]
+
+    query_grad, key_grad = lay_out(qk_grads, [head_places(0), head_places(KEY)])
+    value_grad, gate_grad = lay_out(vg_grads, [value_places(0), value_places(VAL)])
+    feed_gate_grad, feed_up_grad = lay_out(feed_grads, [hidden_places(0), hidden_places(hidden)])
 
     return (
         out_tokens[None],
         input_grad[None],
-        head_back(qk_grads[..., :KEY].astype(F32)),
-        head_back(qk_grads[..., KEY:].astype(F32)),
-        value_back(vg_grads[..., :VAL].astype(F32)),
-        value_back(vg_grads[..., VAL:].astype(F32)),
-        mixer_vectors[0],
-        mixer_vectors[1],
+        query_grad,
+        key_grad,
+        value_grad,
+        gate_grad,
+        vector_sums[0],
+        vector_sums[1],
         output_grad,
-        hidden_back(feed_grads[..., :hidden].astype(F32)),
-        hidden_back(feed_grads[..., hidden:].astype(F32)),
+        feed_gate_grad,
+        feed_up_grad,
         down_grad.astype(F32),
-        feed_vectors[0],
-        feed_vectors[1],
+        vector_sums[2],
+        vector_sums[3],
     )
 
 

time: 724 us -> 688 us (0.950)
  local copies, waits for them, and re-layouts: 84.6 us -> 64.4 us
  waiting for transfers between devices: 178 us -> 165 us
    reshape x14 -> x0, local copies, waits for them, and re-layouts: 20.5 us -> none  [the longest x6 9.47 us: value_back(): return split.transpose(2, 0, 1, 4, 3, 5).reshape(local_model, -1)]
    all_to_all x8 -> x7, waiting for transfers between devices: 60.8 us -> 51.2 us  [to_members(): return lax.all_to_all(packed, axes, 0, 0, tiled=True)]
    pallas_call x0 -> x3, Pallas kernels: none -> 7.26 us  [lay_out(): pl.pallas_call(kernel, out_shape=[jax.ShapeDtypeStruct((rows, width), F32...]
    all_to_all x8 -> x7, starting transfers between devices: 32.9 us -> 26.9 us  [to_members(): return lax.all_to_all(packed, axes, 0, 0, tiled=True)]
    unnamed x170 -> x154, local copies, waits for them, and re-layouts: 42.7 us -> 40.6 us
  transfers between devices with their start and end apart: 97 -> 96, of which waited for: 30 -> 27; matrix products, arithmetic and copies ran while one was open for 22% -> 21% of each run, Pallas kernels for 21% -> 24%
where the time goes in v4:
time: 688 us; the launch traced here: 679 us
  Pallas kernels  176 us (26%)
  waiting for transfers between devices  165 us (24%)
  starting transfers between devices  82.1 us (12%)
  other arithmetic  68 us (10%)
  local copies, waits for them, and re-layouts  64.4 us (9%)
  matrix products  56.4 us (8%)
  between operations  33.9 us (5%)
  blocking collectives  32.5 us (5%)
    pallas_call x16, Pallas kernels, chunk_call(): pl.pallas_call(kernel, grid=(1,), out_shape=outs, in_specs=[whole_spec(o)...  169 us
    ppermute x80, waiting for transfers between devices, swap(): return lax.ppermute(field_in, axis, [(0, 1), (1, 0)])  76.2 us
    dot_general x5, matrix products, dot_rows(): lax.dot_general(left, right, (((0,), (0,)), ((), ())), preferred_element_...  56.4 us
    ppermute x80, starting transfers between devices, swap(): return lax.ppermute(field_in, axis, [(0, 1), (1, 0)])  53.9 us
    all_to_all x7, waiting for transfers between devices, to_members(): return lax.all_to_all(packed, axes, 0, 0, tiled=True)  51.2 us
    unnamed x154, local copies, waits for them, and re-layouts  40.6 us
    all_gather x2, waiting for transfers between devices, gather_layers(): lax.all_gather(mine.reshape(4, 2 * local_model, -1), 'z', axis=1, tiled=T...  32.5 us
    all_to_all x2, blocking collectives, to_members(): return lax.all_to_all(packed, axes, 0, 0, tiled=True)  32.5 us
  transfers between devices with their start and end apart: 96, of which 27 were waited for; matrix products, arithmetic and copies ran while one was open for 21% of the time, Pallas kernels for 24%

profile of v4, /device:TPU:0, one launch (start us, length us, event | category | flops | bytes accessed | tf_op | source)
XLA Modules:
  0.0 678.9 jit_solution(6108516494011222228)
XLA Ops:
  11.4 26.2 %all_to_all.58 = bf16[8,64,1536]{2,1,0:T(8,128)(2,1)} all-to-all(bf16[8,64,1536]{2,1,0:T(8,128)(2,1)S(1)} %pad_maximum_fusion), channel_id=1, replica_groups=mesh['y'=2,'x'=2,'z'=4,'core'=2] {'y','x','core'}, dimensions={0} | all-to-all | bytes 3145728 | tf_op jit(solution)/shard_map/all_to_all | solution.py:358
  44.4 4.0 all-to-all-start
  72.5 13.1 %all-to-all-done = bf16[32,2,128]{2,1,0:T(2,128)(2,1)S(1)} async-done(((bf16[32,2,128]{2,1,0:T(2,128)(2,1)}), bf16[32,2,128]{2,1,0:T(2,128)(2,1)S(1)}, u32[]{:S(2)}, u32[]{:S(2)}) %all-to-all-start) | async-done | bytes 16416 | tf_op jit(solution)/shard_map/all_to_all | solution.py:358
  85.7 3.6 all-to-all-start.3
  93.2 11.4 %all-to-all-done.3 = bf16[8,64,1024]{2,1,0:T(8,128)(2,1)S(1)} async-done(((bf16[8,64,1024]{2,1,0:T(8,128)(2,1)}), bf16[8,64,1024]{2,1,0:T(8,128)(2,1)S(1)}, u32[]{:S(2)}, u32[]{:S(2)}) %all-to-all-start.3) | async-done | bytes 1048608 | tf_op jit(solution)/shard_map/all_to_all | solution.py:358
  123.3 10.0 %collective-permute-done.15 = bf16[128,2048]{1,0:T(8,128)(2,1)S(1)} collective-permute-done((bf16[128,2048]{1,0:T(8,128)(2,1)S(1)}, bf16[128,2048]{1,0:T(8,128)(2,1)S(1)}, u32[]{:S(2)}, u32[]{:S(2)}) %collective-permute-start.15) | collective-permute-done | bytes 524320 | tf_op jit(solution)/shard_map/ppermute | solution.py:245
  152.3 3.8 all-to-all-start.2
  158.9 15.1 %all-gather.5.cloned.1.call-done = bf16[4,512,1536]{2,1,0:T(8,128)(2,1)} async-done(((bf16[4,128,1536]{2,1,0:T(8,128)(2,1)}), bf16[4,512,1536]{2,1,0:T(8,128)(2,1)}) %all-gather.5.cloned.1.call-update) | async-done | bytes 6291472 | tf_op jit(solution)/shard_map/all_gather | solution.py:361
  174.0 12.0 %mixer_forward.4 = (bf16[8,256,2048]{2,1,0:T(8,128)(2,1)}, bf16[8,256,1024]{2,1,0:T(8,128)(2,1)}, f32[8,256,512]{2,1,0:T(8,128)}, bf16[8,256,512]{2,1,0:T(8,128)...) custom-call(bf16[128,2048]{1,0:T(8,128)(2,1)} %collective-permute-done.5.refs_0_, ...), custom_call_target="tpu_custom_call" | custom-call | tf_op jit(solution)/shard_map/mixer_forward/pallas_call | solution.py:111
  186.5 12.0 %mixer_forward.5 = (bf16[8,256,2048]{2,1,0:T(8,128)(2,1)}, bf16[8,256,1024]{2,1,0:T(8,128)(2,1)}, f32[8,256,512]{2,1,0:T(8,128)}, bf16[8,256,512]{2,1,0:T(8,128)...) custom-call(bf16[256,2048]{1,0:T(8,128)(2,1)} %collective-permute-do, ...), custom_call_target="tpu_custom_call", output_to_operand_aliasing={{0}: (7, {}), {1}: (8, {}), {2}: (9, {}), {3}: (10, {})} | custom-call | tf_op jit(solution)/shard_map/mixer_forward/pallas_call | solution.py:111
  203.0 12.4 %mixer_forward.6 = (bf16[8,256,2048]{2,1,0:T(8,128)(2,1)}, bf16[8,256,1024]{2,1,0:T(8,128)(2,1)}, f32[8,256,512]{2,1,0:T(8,128)}, bf16[8,256,512]{2,1,0:T(8,128)...) custom-call(bf16[256,2048]{1,0:T(8,128)(2,1)} %collective-permute-do, ...), custom_call_target="tpu_custom_call", output_to_operand_aliasing={{0}: (7, {}), {1}: (8, {}), {2}: (9, {}), {3}: (10, {})} | custom-call | tf_op jit(solution)/shard_map/mixer_forward/pallas_call | solution.py:111
  224.4 12.1 %mixer_forward.7 = (bf16[8,256,2048]{2,1,0:T(8,128)(2,1)}, bf16[8,256,1024]{2,1,0:T(8,128)(2,1)}, f32[8,256,512]{2,1,0:T(8,128)}, bf16[8,256,512]{2,1,0:T(8,128)...) custom-call(bf16[256,2048]{1,0:T(8,128)(2,1)} %bitcast.148, ...), custom_call_target="tpu_custom_call", output_to_operand_aliasing={{0}: (7, {}), {1}: (8, {}), {2}: (9, {}), {3}: (10, {})} | custom-call | tf_op jit(solution)/shard_map/mixer_forward/pallas_call | solution.py:111
  237.6 17.5 %all-gather.9.cloned.1.call-done = bf16[4,512,1024]{2,1,0:T(8,128)(2,1)} async-done(((bf16[4,128,1024]{2,1,0:T(8,128)(2,1)}), bf16[4,512,1024]{2,1,0:T(8,128)(2,1)}) %all-gather.9.cloned.1.call-update) | async-done | bytes 4194320 | tf_op jit(solution)/shard_map/all_gather | solution.py:361
  256.1 3.9 fusion.31
  267.2 6.9 %feed_forward.4 = (bf16[8,256,2048]{2,1,0:T(8,128)(2,1)}, bf16[8,256,512]{2,1,0:T(8,128)(2,1)}, f32[8,256,1024]{2,1,0:T(8,128)}, f32[8,128]{1,0:T(8,128)}) custom-call(bf16[256,2048]{1,0:T(8,128)(2,1)} %copy-done.10, bf16[256,2048]{1,0:T(8,128)(2,1)} %copy-done.43, bf16[2048,1024]{1,0:T(8,128)(2,1)} %bitcast.122), custom_call_target="tpu_custom_call" | custom-call | tf_op jit(solution)/shard_map/feed_forward/pallas_call | solution.py:111
  278.7 9.0 %collective-permute-done.31.refs_0_ = bf16[128,2048]{1,0:T(8,128)(2,1)S(1)} collective-permute-done((bf16[128,2048]{1,0:T(8,128)(2,1)}, bf16[128,2048]{1,0:T(8,128)(2,1)S(1)}, u32[]{:S(2)}, u32[]{:S(2)}) %collective-permute-start.31) | collective-permute-done | bytes 524320 | tf_op jit(solution)/shard_map/ppermute | solution.py:245
  293.3 6.9 %feed_forward.5 = (bf16[8,256,2048]{2,1,0:T(8,128)(2,1)}, bf16[8,256,512]{2,1,0:T(8,128)(2,1)}, f32[8,256,1024]{2,1,0:T(8,128)}, f32[8,128]{1,0:T(8,128)}) custom-call(bf16[128,2048]{1,0:T(8,128)(2,1)} %get-tuple-element.161.refs_0_, ...), custom_call_target="tpu_custom_call", output_to_operand_aliasing={{0}: (5, {}), {1}: (6, {}), {2}: (7, {})} | custom-call | tf_op jit(solution)/shard_map/feed_forward/pallas_call | solution.py:111
  305.6 6.9 %feed_forward.6 = (bf16[8,256,2048]{2,1,0:T(8,128)(2,1)}, bf16[8,256,512]{2,1,0:T(8,128)(2,1)}, f32[8,256,1024]{2,1,0:T(8,128)}, f32[8,128]{1,0:T(8,128)}) custom-call(bf16[128,2048]{1,0:T(8,128)(2,1)} %get-tuple-element.159.refs_0_, bf16[128,2048]{1,0:T(8,128)(2,1)} %get-tuple-element.168.refs_1_, ...), custom_call_target="tpu_custom_call", output_to_operand_aliasing={{0}: (5, {}), {1}: (6, {}), {2}: (7, {})} | custom-call | tf_op jit(solution)/shard_map/feed_forward/pallas_call | solution.py:111
  313.5 6.9 %feed_forward.7 = (bf16[8,256,2048]{2,1,0:T(8,128)(2,1)}, bf16[8,256,512]{2,1,0:T(8,128)(2,1)}, f32[8,256,1024]{2,1,0:T(8,128)}, f32[8,128]{1,0:T(8,128)}) custom-call(bf16[128,2048]{1,0:T(8,128)(2,1)} %get-tuple-element.166.refs_0_, bf16[128,2048]{1,0:T(8,128)(2,1)} %get-tuple-element.167.refs_1_, ...), custom_call_target="tpu_custom_call", output_to_operand_aliasing={{0}: (5, {}), {1}: (6, {}), {2}: (7, {})} | custom-call | tf_op jit(solution)/shard_map/feed_forward/pallas_call | solution.py:111
  320.4 10.2 %bitcast_convert_fusion.1.refs_5_.refs_6_ = bf16[512,2048]{1,0:T(8,128)(2,1)} fusion(bf16[8,256,512]{2,1,0:T(8,128)(2,1)} %get-tuple-element.175.refs_2_, bf16[8,256,2048]{2,1,0:T(8,128)(2,1)} %dynamic-slice_dynamic-update-slice_fusion.refs_9_.refs_11_.refs_4_), kind=kOutput, calls=%fused_computation.5 | convolution fusion | flops 4296015872 | bytes 12582912 | tf_op jit(solution)/shard_map/dot_general | solution.py:29
  330.6 9.9 %feed_backward.4 = (bf16[8,256,1024]{2,1,0:T(8,128)(2,1)}, bf16[256,2048]{1,0:T(8,128)(2,1)}, bf16[256,2048]{1,0:T(8,128)(2,1)}, bf16[256,2048]{1,0:T(8,128)(2,1)}, bf16[256,2048]{1,0:T(8,128)(2,1)}) custom-call(bf16[2048,1024]{1,0:T(8,128)(2,1)} %bitcast.126, bf16[512,2048]{1,0:T(8,128)(2,1)} %all-gather.11.cloned.1.call-done.refs_8_.refs_1_, ...), custom_call_target="tpu_custom_call" | custom-call | tf_op jit(solution)/shard_map/feed_backward/pallas_call | solution.py:111
  341.0 10.3 %feed_backward.5 = (bf16[8,256,1024]{2,1,0:T(8,128)(2,1)}, bf16[256,2048]{1,0:T(8,128)(2,1)}, bf16[256,2048]{1,0:T(8,128)(2,1)}, bf16[256,2048]{1,0:T(8,128)(2,1)}, bf16[256,2048]{1,0:T(8,128)(2,1)}) custom-call(bf16[2048,1024]{1,0:T(8,128)(2,1)} %bitcast.127, ...), custom_call_target="tpu_custom_call", output_to_operand_aliasing={{0}: (5, {})} | custom-call | tf_op jit(solution)/shard_map/feed_backward/pallas_call | solution.py:111
  354.7 10.0 %feed_backward.6 = (bf16[8,256,1024]{2,1,0:T(8,128)(2,1)}, bf16[256,2048]{1,0:T(8,128)(2,1)}, bf16[256,2048]{1,0:T(8,128)(2,1)}, bf16[256,2048]{1,0:T(8,128)(2,1)}, bf16[256,2048]{1,0:T(8,128)(2,1)}) custom-call(bf16[2048,1024]{1,0:T(8,128)(2,1)} %bitcast.128, ...), custom_call_target="tpu_custom_call", output_to_operand_aliasing={{0}: (5, {})} | custom-call | tf_op jit(solution)/shard_map/feed_backward/pallas_call | solution.py:111
  374.4 10.2 %feed_backward.7 = (bf16[8,256,1024]{2,1,0:T(8,128)(2,1)}, bf16[256,2048]{1,0:T(8,128)(2,1)}, bf16[256,2048]{1,0:T(8,128)(2,1)}, bf16[256,2048]{1,0:T(8,128)(2,1)}, bf16[256,2048]{1,0:T(8,128)(2,1)}) custom-call(bf16[2048,1024]{1,0:T(8,128)(2,1)} %bitcast.129, ...), custom_call_target="tpu_custom_call", output_to_operand_aliasing={{0}: (5, {})} | custom-call | tf_op jit(solution)/shard_map/feed_backward/pallas_call | solution.py:111
  384.5 14.0 %bitcast_convert_fusion.refs_2_ = bf16[2048,1024]{1,0:T(8,128)(2,1)} fusion(bf16[8,256,2048]{2,1,0:T(8,128)(2,1)} %get-tuple-element.198, bf16[8,256,1024]{2,1,0:T(8,128)(2,1)} %get-tuple-element.199), kind=kOutput, calls=%fused_computation | convolution fusion | flops 8592031744 | bytes 16777216 | tf_op jit(solution)/shard_map/dot_general | solution.py:29
  412.5 13.0 %mixer_backward.4 = (bf16[8,256,2048]{2,1,0:T(8,128)(2,1)}, bf16[8,256,512]{2,1,0:T(8,128)(2,1)}, bf16[8,256,1024]{2,1,0:T(8,128)(2,1)}, bf16[256,2048]{1,0:T(8,128)(2,1)}, bf16[256,2048]{1,0:T(8,128)(2,1)}) custom-call(bf16[256,2048]{1,0:T(8,128)(2,1)} %copy-done.19, bf16[256,2048]{1,0:T(8,128)(2,1)} %collective-permute-done.51.refs_1_, ...), custom_call_target="tpu_custom_call" | custom-call | flops 20000000000 | tf_op jit(solution)/shard_map/mixer_backward/pallas_call | solution.py:111
  425.5 8.8 %collective-permute-done.50.refs_1_ = bf16[128,2048]{1,0:T(8,128)(2,1)} collective-permute-done((bf16[128,2048]{1,0:T(8,128)(2,1)}, bf16[128,2048]{1,0:T(8,128)(2,1)}, u32[]{:S(2)}, u32[]{:S(2)}) %collective-permute-start.50) | collective-permute-done | bytes 524320 | tf_op jit(solution)/shard_map/ppermute | solution.py:245
  439.1 13.5 %mixer_backward.5 = (bf16[8,256,2048]{2,1,0:T(8,128)(2,1)}, bf16[8,256,512]{2,1,0:T(8,128)(2,1)}, bf16[8,256,1024]{2,1,0:T(8,128)(2,1)}, bf16[256,2048]{1,0:T(8,128)(2,1)}, bf16[256,2048]{1,0:T(8,128)(2,1)}) custom-call(bf16[128,2048]{1,0:T(8,128)(2,1)} %get-tuple-element.206.refs_0_, ...), custom_call_target="tpu_custom_call", output_to_operand_aliasing={{0}: (10, {}), {1}: (11, {}), {2}: (12, {})} | custom-call | flops 20000000000 | tf_op jit(solution)/shard_map/mixer_backward/pallas_call | solution.py:111
  453.3 13.2 %mixer_backward.6 = (bf16[8,256,2048]{2,1,0:T(8,128)(2,1)}, bf16[8,256,512]{2,1,0:T(8,128)(2,1)}, bf16[8,256,1024]{2,1,0:T(8,128)(2,1)}, bf16[256,2048]{1,0:T(8,128)(2,1)}, bf16[256,2048]{1,0:T(8,128)(2,1)}) custom-call(bf16[128,2048]{1,0:T(8,128)(2,1)} %get-tuple-element.222.refs_0_, ...), custom_call_target="tpu_custom_call", output_to_operand_aliasing={{0}: (10, {}), {1}: (11, {}), {2}: (12, {})} | custom-call | flops 20000000000 | tf_op jit(solution)/shard_map/mixer_backward/pallas_call | solution.py:111
  468.8 13.3 %mixer_backward.7 = (bf16[8,256,2048]{2,1,0:T(8,128)(2,1)}, bf16[8,256,512]{2,1,0:T(8,128)(2,1)}, bf16[8,256,1024]{2,1,0:T(8,128)(2,1)}, bf16[256,2048]{1,0:T(8,128)(2,1)}, bf16[256,2048]{1,0:T(8,128)(2,1)}) custom-call(bf16[128,2048]{1,0:T(8,128)(2,1)} %get-tuple-element.223.refs_0_, ...), custom_call_target="tpu_custom_call", output_to_operand_aliasing={{0}: (10, {}), {1}: (11, {}), {2}: (12, {})} | custom-call | flops 20000000000 | tf_op jit(solution)/shard_map/mixer_backward/pallas_call | solution.py:111
  482.1 9.9 %convolution_convert_fusion.2 = bf16[2048,512]{1,0:T(8,128)(2,1)} fusion(bf16[2048,2048]{1,0:T(8,128)(2,1)} %bitcast.138, bf16[2048,512]{1,0:T(8,128)(2,1)} %after.33), kind=kOutput, calls=%fused_computation.11 | convolution fusion | flops 4296015872 | bytes 12582912 | tf_op jit(solution)/shard_map/dot_general | solution.py:29
  495.8 12.1 %collective-permute-done.57.refs_0_ = bf16[128,2048]{1,0:T(8,128)(2,1)} collective-permute-done((bf16[128,2048]{1,0:T(8,128)(2,1)S(1)}, bf16[128,2048]{1,0:T(8,128)(2,1)}, u32[]{:S(2)}, u32[]{:S(2)}) %collective-permute-start.57) | collective-permute-done | bytes 524320 | tf_op jit(solution)/shard_map/ppermute | solution.py:245
  514.4 14.1 %convolution_convert_fusion = bf16[2048,1024]{1,0:T(8,128)(2,1)} fusion(bf16[2048,2048]{1,0:T(8,128)(2,1)} %bitcast.139, bf16[2048,1024]{1,0:T(8,128)(2,1)} %after.30), kind=kOutput, calls=%fused_computation.6 | convolution fusion | flops 8592031744 | bytes 16777216 | tf_op jit(solution)/shard_map/dot_general | solution.py:29
  530.9 3.6 all-to-all-start.5
  539.5 15.9 %collective-permute-done.61 = bf16[256,2048]{1,0:T(8,128)(2,1)} collective-permute-done((bf16[256,2048]{1,0:T(8,128)(2,1)}, bf16[256,2048]{1,0:T(8,128)(2,1)}, u32[]{:S(2)}, u32[]{:S(2)}) %collective-permute-start.61) | collective-permute-done | bytes 1048608 | tf_op jit(solution)/shard_map/ppermute | solution.py:245
  557.5 10.5 %all-to-all-done.5.refs_1_.block = bf16[8,64,1024]{2,1,0:T(8,128)(2,1)S(1)} async-done(((bf16[8,64,1024]{2,1,0:T(8,128)(2,1)}), bf16[8,64,1024]{2,1,0:T(8,128)(2,1)S(1)}, u32[]{:S(2)}, u32[]{:S(2)}) %all-to-all-start.5) | async-done | bytes 1048608 | tf_op jit(solution)/shard_map/all_to_all | solution.py:358
  568.0 4.1 all-to-all-start.6
  572.4 4.0 add_convert_fusion.3
  579.8 5.2 all-to-all-done.6.refs_2_.block
  586.6 8.2 %convolution_convert_fusion.1.refs_2_ = bf16[512,2048]{1,0:T(8,128)(2,1)S(1)} fusion(bf16[2048,512]{1,0:T(8,128)(2,1)S(1)} %bitcast.152, bf16[2048,2048]{1,0:T(8,128)(2,1)} %after.34), kind=kOutput, calls=%fused_computation.10 | convolution fusion | flops 4296015872 | bytes 12582912 | tf_op jit(solution)/shard_map/dot_general | solution.py:29
  594.8 6.3 all_to_all.59
  609.8 4.2 reduce-scatter.8.cloned.1.call-done
  613.9 3.6 all-to-all-start.4
  633.2 4.3 collective-permute-done.79.refs_1_
  637.5 8.4 %all-to-all-done.4.refs_2_.refs_3_.block = bf16[8,64,1024]{2,1,0:T(8,128)(2,1)S(1)} async-done(((bf16[8,64,1024]{2,1,0:T(8,128)(2,1)}), bf16[8,64,1024]{2,1,0:T(8,128)(2,1)S(1)}, u32[]{:S(2)}, u32[]{:S(2)}) %all-to-all-start.4) | async-done | bytes 1048608 | tf_op jit(solution)/shard_map/all_to_all | solution.py:358
  646.8 4.9 fusion.10
  652.7 4.2 all-to-all-start.7
  658.3 4.0 fusion.16
  (446 shorter events, 197.7 us)
Async XLA Ops:
  7.2 145.1 %all-gather.7.cloned.1.call-start = ((), (), s32[]{:S(2)}) async-start(), calls=%async_computation.15 | async-start | bytes 2621440 | tf_op jit(solution)/shard_map/all_gather | solution.py:376
  7.9 166.1 %all-gather.5.cloned.1.call-start = ((), (), s32[]{:S(2)}) async-start(), calls=%async_computation.14 | async-start | bytes 7864320 | tf_op jit(solution)/shard_map/all_gather | solution.py:361
  37.6 69.6 %collective-permute-start.3 = (bf16[256,2048]{1,0:T(8,128)(2,1)S(1)}, bf16[256,2048]{1,0:T(8,128)(2,1)}, u32[]{:S(2)}, u32[]{:S(2)}) collective-permute-start(bf16[256,2048]{1,0:T(8,128)(2,1)S(1)} %bitcast.149), channel_id=1, source_target_pairs={{0,8},{8,0},{1,9},{9,1},{2,10},{10,2},{3,11},{11,3},{4,12},{12,4},... | collective-permute-start | bytes 3145736 | tf_op jit(solution)/shard_map/ppermute | solution.py:245
  38.3 67.3 %collective-permute-start.1 = (bf16[256,2048]{1,0:T(8,128)(2,1)S(1)}, bf16[256,2048]{1,0:T(8,128)(2,1)}, u32[]{:S(2)}, u32[]{:S(2)}) collective-permute-start(bf16[256,2048]{1,0:T(8,128)(2,1)S(1)} %bitcast.150), channel_id=1, source_target_pairs={{0,16},{16,0},{1,17},{17,1},{2,18},{18,2},{3,19},{19,3},{4,20},{20... | collective-permute-start | bytes 3145736 | tf_op jit(solution)/shard_map/ppermute | solution.py:245
  40.7 69.4 %collective-permute-start.9 = (bf16[256,2048]{1,0:T(8,128)(2,1)}, bf16[256,2048]{1,0:T(8,128)(2,1)}, u32[]{:S(2)}, u32[]{:S(2)}) collective-permute-start(bf16[256,2048]{1,0:T(8,128)(2,1)} %fusion.14), channel_id=1, source_target_pairs={{0,1},{1,0},{2,3},{3,2},{4,5},{5,4},{6,7},{7,6},{8,9},{9,8},{10,11... | collective-permute-start | bytes 3145736 | tf_op jit(solution)/shard_map/ppermute | solution.py:245
  40.7 51.3 %collective-permute-start.10 = (bf16[256,2048]{1,0:T(8,128)(2,1)}, bf16[256,2048]{1,0:T(8,128)(2,1)}, u32[]{:S(2)}, u32[]{:S(2)}) collective-permute-start(bf16[256,2048]{1,0:T(8,128)(2,1)} %fusion.14), channel_id=1, source_target_pairs={{0,8},{8,0},{1,9},{9,1},{2,10},{10,2},{3,11},{11,3},{4,12},{12,4},... | collective-permute-start | bytes 3145736 | tf_op jit(solution)/shard_map/ppermute | solution.py:245
  42.2 69.4 %collective-permute-start.12 = (bf16[256,2048]{1,0:T(8,128)(2,1)}, bf16[256,2048]{1,0:T(8,128)(2,1)}, u32[]{:S(2)}, u32[]{:S(2)}) collective-permute-start(bf16[256,2048]{1,0:T(8,128)(2,1)} %fusion.14), channel_id=1, source_target_pairs={{0,16},{16,0},{1,17},{17,1},{2,18},{18,2},{3,19},{19,3},{4,20},{20... | collective-permute-start | bytes 3145736 | tf_op jit(solution)/shard_map/ppermute | solution.py:245
  44.4 41.3 %all-to-all-start = ((bf16[32,2,128]{2,1,0:T(2,128)(2,1)}), bf16[32,2,128]{2,1,0:T(2,128)(2,1)S(1)}, u32[]{:S(2)}, u32[]{:S(2)}) async-start(bf16[32,2,128]{2,1,0:T(2,128)(2,1)} %reshape.621), calls=%async_computation | async-start | bytes 32768 | tf_op jit(solution)/shard_map/all_to_all | solution.py:358
  85.7 18.9 %all-to-all-start.3 = ((bf16[8,64,1024]{2,1,0:T(8,128)(2,1)}), bf16[8,64,1024]{2,1,0:T(8,128)(2,1)S(1)}, u32[]{:S(2)}, u32[]{:S(2)}) async-start(bf16[8,64,1024]{2,1,0:T(8,128)(2,1)} %pad_maximum_fusion.1), calls=%async_computation.3 | async-start | bytes 2097152 | tf_op jit(solution)/shard_map/all_to_all | solution.py:358
  89.2 165.8 %all-gather.9.cloned.1.call-start = ((), (), s32[]{:S(2)}) async-start(), calls=%async_computation.16 | async-start | bytes 5242880 | tf_op jit(solution)/shard_map/all_gather | solution.py:361
  92.0 25.3 %collective-permute-start.11 = (bf16[256,2048]{1,0:T(8,128)(2,1)}, bf16[256,2048]{1,0:T(8,128)(2,1)S(1)}, u32[]{:S(2)}, u32[]{:S(2)}) collective-permute-start(bf16[256,2048]{1,0:T(8,128)(2,1)} %collective-permute-done.10), channel_id=1, source_target_pairs={{0,1},{1,0},{2,3},{3,2},{4,5},{5,4},{6,7},{7,6},{8,9},{9,8},{10,11... | collective-permute-start | bytes 3145736 | tf_op jit(solution)/shard_map/ppermute | solution.py:245
  110.1 23.2 %collective-permute-start.15 = (bf16[128,2048]{1,0:T(8,128)(2,1)S(1)}, bf16[128,2048]{1,0:T(8,128)(2,1)S(1)}, u32[]{:S(2)}, u32[]{:S(2)}) collective-permute-start(bf16[128,2048]{1,0:T(8,128)(2,1)S(1)} %slice.123), channel_id=1, source_target_pairs={{0,16},{16,0},{1,17},{17,1},{2,18},{18,2},{3,19},{19,3},{4,20},{20... | collective-permute-start | bytes 1572872 | tf_op jit(solution)/shard_map/ppermute | solution.py:245
  111.6 22.3 %collective-permute-start.13 = (bf16[256,2048]{1,0:T(8,128)(2,1)}, bf16[256,2048]{1,0:T(8,128)(2,1)S(1)}, u32[]{:S(2)}, u32[]{:S(2)}) collective-permute-start(bf16[256,2048]{1,0:T(8,128)(2,1)} %collective-permute-done.12), channel_id=1, source_target_pairs={{0,1},{1,0},{2,3},{3,2},{4,5},{5,4},{6,7},{7,6},{8,9},{9,8},{10,11... | collective-permute-start | bytes 3145736 | tf_op jit(solution)/shard_map/ppermute | solution.py:245
  122.3 64.2 %collective-permute-start.4 = (bf16[256,2048]{1,0:T(8,128)(2,1)}, bf16[256,2048]{1,0:T(8,128)(2,1)}, u32[]{:S(2)}, u32[]{:S(2)}) collective-permute-start(bf16[256,2048]{1,0:T(8,128)(2,1)} %collective-permute-done.3.refs_0_), channel_id=1, source_target_pairs={{0,1},{1,0},{2,3},{3,2},{4,5},{5,4},{6,7},{7,6},{8,9},{9,8},{10,11... | collective-permute-start | bytes 3145736 | tf_op jit(solution)/shard_map/ppermute | solution.py:245
  123.3 33.0 %collective-permute-start.7 = (bf16[128,2048]{1,0:T(8,128)(2,1)}, bf16[128,2048]{1,0:T(8,128)(2,1)}, u32[]{:S(2)}, u32[]{:S(2)}) collective-permute-start(bf16[128,2048]{1,0:T(8,128)(2,1)} %collective-permute-done.5.refs_0_), channel_id=1, source_target_pairs={{0,1},{1,0},{2,3},{3,2},{4,5},{5,4},{6,7},{7,6},{8,9},{9,8},{10,11... | collective-permute-start | bytes 1572872 | tf_op jit(solution)/shard_map/ppermute | solution.py:245
  133.3 23.0 %collective-permute-start.8 = (bf16[128,2048]{1,0:T(8,128)(2,1)}, bf16[128,2048]{1,0:T(8,128)(2,1)}, u32[]{:S(2)}, u32[]{:S(2)}) collective-permute-start(bf16[128,2048]{1,0:T(8,128)(2,1)} %collective-permute-done.6.refs_1_), channel_id=1, source_target_pairs={{0,1},{1,0},{2,3},{3,2},{4,5},{5,4},{6,7},{7,6},{8,9},{9,8},{10,11... | collective-permute-start | bytes 1572872 | tf_op jit(solution)/shard_map/ppermute | solution.py:245
  156.0 156.5 %all-gather.11.cloned.1.call-start = ((), (), s32[]{:S(2)}) async-start(), calls=%async_computation.17 | async-start | bytes 2621440 | tf_op jit(solution)/shard_map/all_gather | solution.py:392
  198.5 19.0 %collective-permute-start.19 = (bf16[256,2048]{1,0:T(8,128)(2,1)}, bf16[256,2048]{1,0:T(8,128)(2,1)S(1)}, u32[]{:S(2)}, u32[]{:S(2)}) collective-permute-start(bf16[256,2048]{1,0:T(8,128)(2,1)} %get-tuple-element.149), channel_id=1, source_target_pairs={{0,1},{1,0},{2,3},{3,2},{4,5},{5,4},{6,7},{7,6},{8,9},{9,8},{10,11... | collective-permute-start | bytes 3145736 | tf_op jit(solution)/shard_map/ppermute | solution.py:245
  220.6 34.5 %collective-permute-start.24 = (bf16[256,2048]{1,0:T(8,128)(2,1)S(1)}, bf16[256,2048]{1,0:T(8,128)(2,1)}, u32[]{:S(2)}, u32[]{:S(2)}) collective-permute-start(bf16[256,2048]{1,0:T(8,128)(2,1)S(1)} %add_convert_fusion.12.refs_13_), channel_id=1, source_target_pairs={{0,8},{8,0},{1,9},{9,1},{2,10},{10,2},{3,11},{11,3},{4,12},{12,4},... | collective-permute-start | bytes 3145736 | tf_op jit(solution)/shard_map/ppermute | solution.py:245
  223.9 31.2 %collective-permute-start.25 = (bf16[256,2048]{1,0:T(8,128)(2,1)}, bf16[256,2048]{1,0:T(8,128)(2,1)}, u32[]{:S(2)}, u32[]{:S(2)}) collective-permute-start(bf16[256,2048]{1,0:T(8,128)(2,1)} %add_convert_fusion.11.refs_14_), channel_id=1, source_target_pairs={{0,16},{16,0},{1,17},{17,1},{2,18},{18,2},{3,19},{19,3},{4,20},{20... | collective-permute-start | bytes 3145736 | tf_op jit(solution)/shard_map/ppermute | solution.py:245
  236.5 18.6 %collective-permute-start.23 = (bf16[256,2048]{1,0:T(8,128)(2,1)}, bf16[256,2048]{1,0:T(8,128)(2,1)S(1)}, u32[]{:S(2)}, u32[]{:S(2)}) collective-permute-start(bf16[256,2048]{1,0:T(8,128)(2,1)} %get-tuple-element.155), channel_id=1, source_target_pairs={{0,1},{1,0},{2,3},{3,2},{4,5},{5,4},{6,7},{7,6},{8,9},{9,8},{10,11... | collective-permute-start | bytes 3145736 | tf_op jit(solution)/shard_map/ppermute | solution.py:245
  236.5 162.1 %reduce-scatter.6.cloned.1.call-start = ((), (), s32[]{:S(2)}) async-start(), calls=%async_computation.18 | async-start | bytes 2621440 | tf_op jit(solution)/shard_map/reduce_scatter | solution.py:475
  265.1 22.7 %collective-permute-start.31 = (bf16[128,2048]{1,0:T(8,128)(2,1)}, bf16[128,2048]{1,0:T(8,128)(2,1)S(1)}, u32[]{:S(2)}, u32[]{:S(2)}) collective-permute-start(bf16[128,2048]{1,0:T(8,128)(2,1)} %get-tuple-element.280), channel_id=1, source_target_pairs={{0,8},{8,0},{1,9},{9,1},{2,10},{10,2},{3,11},{11,3},{4,12},{12,4},... | collective-permute-start | bytes 1572872 | tf_op jit(solution)/shard_map/ppermute | solution.py:245
  265.6 23.4 %collective-permute-start.32 = (bf16[128,2048]{1,0:T(8,128)(2,1)}, bf16[128,2048]{1,0:T(8,128)(2,1)}, u32[]{:S(2)}, u32[]{:S(2)}) collective-permute-start(bf16[128,2048]{1,0:T(8,128)(2,1)} %get-tuple-element.281), channel_id=1, source_target_pairs={{0,16},{16,0},{1,17},{17,1},{2,18},{18,2},{3,19},{19,3},{4,20},{20... | collective-permute-start | bytes 1572872 | tf_op jit(solution)/shard_map/ppermute | solution.py:245
  340.6 141.5 %reduce-scatter.10.cloned.1.call-start = ((), (), s32[]{:S(2)}) async-start(), calls=%async_computation.20 | async-start | bytes 5242880 | tf_op jit(solution)/shard_map/reduce_scatter | solution.py:507
  370.6 28.0 %collective-permute-start.45 = (bf16[256,2048]{1,0:T(8,128)(2,1)S(1)}, bf16[256,2048]{1,0:T(8,128)(2,1)S(1)}, u32[]{:S(2)}, u32[]{:S(2)}) collective-permute-start(bf16[256,2048]{1,0:T(8,128)(2,1)S(1)} %add_convert_fusion.8.refs_8_), channel_id=1, source_target_pairs={{0,8},{8,0},{1,9},{9,1},{2,10},{10,2},{3,11},{11,3},{4,12},{12,4},... | collective-permute-start | bytes 3145736 | tf_op jit(solution)/shard_map/ppermute | solution.py:245
  373.2 25.3 %collective-permute-start.46 = (bf16[256,2048]{1,0:T(8,128)(2,1)S(1)}, bf16[256,2048]{1,0:T(8,128)(2,1)}, u32[]{:S(2)}, u32[]{:S(2)}) collective-permute-start(bf16[256,2048]{1,0:T(8,128)(2,1)S(1)} %add_convert_fusion.7.refs_9_), channel_id=1, source_target_pairs={{0,16},{16,0},{1,17},{17,1},{2,18},{18,2},{3,19},{19,3},{4,20},{20... | collective-permute-start | bytes 3145736 | tf_op jit(solution)/shard_map/ppermute | solution.py:245
  407.0 161.0 %reduce-scatter.12.cloned.1.call-start = ((), (), s32[]{:S(2)}) async-start(), calls=%async_computation.21 | async-start | bytes 2621440 | tf_op jit(solution)/shard_map/reduce_scatter | solution.py:507
  408.5 26.6 %collective-permute-start.48 = (bf16[128,2048]{1,0:T(8,128)(2,1)}, bf16[128,2048]{1,0:T(8,128)(2,1)}, u32[]{:S(2)}, u32[]{:S(2)}) collective-permute-start(bf16[128,2048]{1,0:T(8,128)(2,1)} %get-tuple-element.276), channel_id=1, source_target_pairs={{0,16},{16,0},{1,17},{17,1},{2,18},{18,2},{3,19},{19,3},{4,20},{20... | collective-permute-start | bytes 1572872 | tf_op jit(solution)/shard_map/ppermute | solution.py:245
  410.6 24.4 %collective-permute-start.47 = (bf16[128,2048]{1,0:T(8,128)(2,1)}, bf16[128,2048]{1,0:T(8,128)(2,1)}, u32[]{:S(2)}, u32[]{:S(2)}) collective-permute-start(bf16[128,2048]{1,0:T(8,128)(2,1)} %get-tuple-element.277), channel_id=1, source_target_pairs={{0,8},{8,0},{1,9},{9,1},{2,10},{10,2},{3,11},{11,3},{4,12},{12,4},... | collective-permute-start | bytes 1572872 | tf_op jit(solution)/shard_map/ppermute | solution.py:245
  411.5 22.9 %collective-permute-start.50 = (bf16[128,2048]{1,0:T(8,128)(2,1)}, bf16[128,2048]{1,0:T(8,128)(2,1)}, u32[]{:S(2)}, u32[]{:S(2)}) collective-permute-start(bf16[128,2048]{1,0:T(8,128)(2,1)} %get-tuple-element.277), channel_id=1, source_target_pairs={{0,16},{16,0},{1,17},{17,1},{2,18},{18,2},{3,19},{19,3},{4,20},{20... | collective-permute-start | bytes 1572872 | tf_op jit(solution)/shard_map/ppermute | solution.py:245
  492.0 121.9 %reduce-scatter.8.cloned.1.call-start = ((), (), s32[]{:S(2)}) async-start(), calls=%async_computation.19 | async-start | bytes 5242880 | tf_op jit(solution)/shard_map/reduce_scatter | solution.py:507
  529.1 26.3 %collective-permute-start.61 = (bf16[256,2048]{1,0:T(8,128)(2,1)}, bf16[256,2048]{1,0:T(8,128)(2,1)}, u32[]{:S(2)}, u32[]{:S(2)}) collective-permute-start(bf16[256,2048]{1,0:T(8,128)(2,1)} %add_convert_fusion.4.refs_2_), channel_id=1, source_target_pairs={{0,16},{16,0},{1,17},{17,1},{2,18},{18,2},{3,19},{19,3},{4,20},{20... | collective-permute-start | bytes 3145736 | tf_op jit(solution)/shard_map/ppermute | solution.py:245
  530.1 42.4 %collective-permute-start.59 = (bf16[256,2048]{1,0:T(8,128)(2,1)}, bf16[256,2048]{1,0:T(8,128)(2,1)}, u32[]{:S(2)}, u32[]{:S(2)}) collective-permute-start(bf16[256,2048]{1,0:T(8,128)(2,1)} %add_convert_fusion.5.refs_1_), channel_id=1, source_target_pairs={{0,8},{8,0},{1,9},{9,1},{2,10},{10,2},{3,11},{11,3},{4,12},{12,4},... | collective-permute-start | bytes 3145736 | tf_op jit(solution)/shard_map/ppermute | solution.py:245
  530.9 70.2 %collective-permute-start.73 = (bf16[256,2048]{1,0:T(8,128)(2,1)}, bf16[256,2048]{1,0:T(8,128)(2,1)}, u32[]{:S(2)}, u32[]{:S(2)}) collective-permute-start(bf16[256,2048]{1,0:T(8,128)(2,1)} %get-tuple-element.210.refs_8_.refs_2_), channel_id=1, source_target_pairs={{0,1},{1,0},{2,3},{3,2},{4,5},{5,4},{6,7},{7,6},{8,9},{9,8},{10,11... | collective-permute-start | bytes 3145736 | tf_op jit(solution)/shard_map/ppermute | solution.py:245
  530.9 37.1 %all-to-all-start.5 = ((bf16[8,64,1024]{2,1,0:T(8,128)(2,1)}), bf16[8,64,1024]{2,1,0:T(8,128)(2,1)S(1)}, u32[]{:S(2)}, u32[]{:S(2)}) async-start(bf16[8,64,1024]{2,1,0:T(8,128)(2,1)} %bitcast.158), calls=%async_computation.8 | async-start | bytes 2097152 | tf_op jit(solution)/shard_map/all_to_all | solution.py:358
  534.5 71.0 %collective-permute-start.78 = (bf16[256,2048]{1,0:T(8,128)(2,1)}, bf16[256,2048]{1,0:T(8,128)(2,1)}, u32[]{:S(2)}, u32[]{:S(2)}) collective-permute-start(bf16[256,2048]{1,0:T(8,128)(2,1)} %get-tuple-element.241), channel_id=1, source_target_pairs={{0,1},{1,0},{2,3},{3,2},{4,5},{5,4},{6,7},{7,6},{8,9},{9,8},{10,11... | collective-permute-start | bytes 3145736 | tf_op jit(solution)/shard_map/ppermute | solution.py:245
  538.0 40.3 %collective-permute-start.75 = (bf16[128,2048]{1,0:T(8,128)(2,1)}, bf16[128,2048]{1,0:T(8,128)(2,1)}, u32[]{:S(2)}, u32[]{:S(2)}) collective-permute-start(bf16[128,2048]{1,0:T(8,128)(2,1)} %get-tuple-element.272), channel_id=1, source_target_pairs={{0,16},{16,0},{1,17},{17,1},{2,18},{18,2},{3,19},{19,3},{4,20},{20... | collective-permute-start | bytes 1572872 | tf_op jit(solution)/shard_map/ppermute | solution.py:245
  555.4 24.4 %collective-permute-start.76 = (bf16[128,2048]{1,0:T(8,128)(2,1)}, bf16[128,2048]{1,0:T(8,128)(2,1)}, u32[]{:S(2)}, u32[]{:S(2)}) collective-permute-start(bf16[128,2048]{1,0:T(8,128)(2,1)} %get-tuple-element.271), channel_id=1, source_target_pairs={{0,8},{8,0},{1,9},{9,1},{2,10},{10,2},{3,11},{11,3},{4,12},{12,4},... | collective-permute-start | bytes 1572872 | tf_op jit(solution)/shard_map/ppermute | solution.py:245
  572.2 97.8 %reduce-scatter.14.cloned.1.call-start = ((), (), s32[]{:S(2)}) async-start(), calls=%async_computation.22 | async-start | bytes 2621440 | tf_op jit(solution)/shard_map/reduce_scatter | solution.py:552
  576.4 48.7 %collective-permute-start.62 = (bf16[256,2048]{1,0:T(8,128)(2,1)}, bf16[256,2048]{1,0:T(8,128)(2,1)}, u32[]{:S(2)}, u32[]{:S(2)}) collective-permute-start(bf16[256,2048]{1,0:T(8,128)(2,1)} %add_convert_fusion.3), channel_id=1, source_target_pairs={{0,8},{8,0},{1,9},{9,1},{2,10},{10,2},{3,11},{11,3},{4,12},{12,4},... | collective-permute-start | bytes 3145736 | tf_op jit(solution)/shard_map/ppermute | solution.py:245
  578.3 42.9 %collective-permute-start.63 = (bf16[256,2048]{1,0:T(8,128)(2,1)}, bf16[256,2048]{1,0:T(8,128)(2,1)}, u32[]{:S(2)}, u32[]{:S(2)}) collective-permute-start(bf16[256,2048]{1,0:T(8,128)(2,1)} %add_convert_fusion.3), channel_id=1, source_target_pairs={{0,16},{16,0},{1,17},{17,1},{2,18},{18,2},{3,19},{19,3},{4,20},{20... | collective-permute-start | bytes 3145736 | tf_op jit(solution)/shard_map/ppermute | solution.py:245
  605.2 28.0 %collective-permute-start.77 = (bf16[256,2048]{1,0:T(8,128)(2,1)}, bf16[256,2048]{1,0:T(8,128)(2,1)S(1)}, u32[]{:S(2)}, u32[]{:S(2)}) collective-permute-start(bf16[256,2048]{1,0:T(8,128)(2,1)} %add_convert_fusion.1), channel_id=1, source_target_pairs={{0,8},{8,0},{1,9},{9,1},{2,10},{10,2},{3,11},{11,3},{4,12},{12,4},... | collective-permute-start | bytes 3145736 | tf_op jit(solution)/shard_map/ppermute | solution.py:245
  608.4 29.1 %collective-permute-start.79 = (bf16[256,2048]{1,0:T(8,128)(2,1)}, bf16[256,2048]{1,0:T(8,128)(2,1)}, u32[]{:S(2)}, u32[]{:S(2)}) collective-permute-start(bf16[256,2048]{1,0:T(8,128)(2,1)} %add_convert_fusion), channel_id=1, source_target_pairs={{0,16},{16,0},{1,17},{17,1},{2,18},{18,2},{3,19},{19,3},{4,20},{20... | collective-permute-start | bytes 3145736 | tf_op jit(solution)/shard_map/ppermute | solution.py:245
  609.8 37.1 %collective-permute-start.72 = (bf16[256,2048]{1,0:T(8,128)(2,1)}, bf16[256,2048]{1,0:T(8,128)(2,1)}, u32[]{:S(2)}, u32[]{:S(2)}) collective-permute-start(bf16[256,2048]{1,0:T(8,128)(2,1)} %get-tuple-element.204.refs_2_), channel_id=1, source_target_pairs={{0,1},{1,0},{2,3},{3,2},{4,5},{5,4},{6,7},{7,6},{8,9},{9,8},{10,11... | collective-permute-start | bytes 3145736 | tf_op jit(solution)/shard_map/ppermute | solution.py:245
  613.9 31.9 %all-to-all-start.4 = ((bf16[8,64,1024]{2,1,0:T(8,128)(2,1)}), bf16[8,64,1024]{2,1,0:T(8,128)(2,1)S(1)}, u32[]{:S(2)}, u32[]{:S(2)}) async-start(bf16[8,64,1024]{2,1,0:T(8,128)(2,1)} %bitcast.169), calls=%async_computation.6 | async-start | bytes 2097152 | tf_op jit(solution)/shard_map/all_to_all | solution.py:358
  623.1 33.8 %collective-permute-start.64 = (bf16[128,2048]{1,0:T(8,128)(2,1)}, bf16[128,2048]{1,0:T(8,128)(2,1)}, u32[]{:S(2)}, u32[]{:S(2)}) collective-permute-start(bf16[128,2048]{1,0:T(8,128)(2,1)} %slice.136), channel_id=1, source_target_pairs={{0,8},{8,0},{1,9},{9,1},{2,10},{10,2},{3,11},{11,3},{4,12},{12,4},... | collective-permute-start | bytes 1572872 | tf_op jit(solution)/shard_map/ppermute | solution.py:245
  627.0 29.9 %collective-permute-start.65 = (bf16[128,2048]{1,0:T(8,128)(2,1)}, bf16[128,2048]{1,0:T(8,128)(2,1)}, u32[]{:S(2)}, u32[]{:S(2)}) collective-permute-start(bf16[128,2048]{1,0:T(8,128)(2,1)} %slice.137), channel_id=1, source_target_pairs={{0,16},{16,0},{1,17},{17,1},{2,18},{18,2},{3,19},{19,3},{4,20},{20... | collective-permute-start | bytes 1572872 | tf_op jit(solution)/shard_map/ppermute | solution.py:245
  (116 other events, 951.6 us)
Sparse Core Ops, SparseCore 0:
  9.6 48.7 all-gather.6
  59.9 114.0 all-gather.4
  176.1 78.9 all-gather.8
  256.5 44.1 all-gather.10
  340.7 41.8 reduce-scatter.5
  407.1 74.2 reduce-scatter.9
  492.1 43.4 reduce-scatter.11
  537.9 75.9 reduce-scatter.7
  616.2 44.1 reduce-scatter.13

commit v5 on v4

--- a/solution.py
+++ b/solution.py
@@ -546,40 +546,6 @@
     qk_product = dot_rows(normed_rows, qk_grad).astype(BF16)
     vg_product = dot_rows(normed_rows, vg_grad).astype(BF16)
     qk_grads = to_owners(sum_layers(qk_product))
-    (out_grad,) = after([out_grad], feed_grads, qk_grads)
-    out_product = dot_rows(gated_all.reshape(GROUP * length, VAL), out_grad).astype(BF16)
-    vg_grads = to_owners(sum_layers(vg_product))
-    output_grad = lax.psum_scatter(
-        to_members(out_product, "core"), "z", scatter_dimension=0, tiled=True
-    ).astype(F32)
-
-    slot_out = (hidden_state + feed_terms.total()).astype(BF16)
-    half = length // 2
-    from_x, from_y = swap(slot_out, "x"), swap(slot_out, "y")
-    across = jnp.concatenate(
-        after([swap(from_y[:half], "x"), swap(from_x[half:], "y")], vg_grads), axis=0
-    )
-    reached = jnp.stack([slot_out, from_x, from_y, across])
-    chosen = lax.dynamic_index_in_dim(reached, own_slot, 0, keepdims=False)
-    out_tokens = (live_mask * chosen.astype(F32)).astype(BF16)
-
-    summed = GroupSum()
-    for n in order:
-        summed.terms(n, results[n][3:5])
-    mixer_normed_grad = summed.total(out_product, vg_grads)
-    mixer_hat, mixer_inverse = statistics(tokens[0].astype(F32), EPSILON)
-    mixer_gain_part = jnp.sum(mixer_normed_grad * mixer_hat, axis=0)
-    mixer_bias_part = jnp.sum(mixer_normed_grad, axis=0)
-    input_grad = (
-        state_grad + pull_back(mixer_hat, mixer_inverse, mixer_normed_grad * features[0])
-    ).astype(BF16)
-
-    def vector_grads(*grads):
-        split = jnp.stack(grads).reshape(len(grads), devices, -1).transpose(1, 0, 2)
-        return jnp.sum(to_members(split, EVERY), axis=0)
-
-    vector_sums = vector_grads(mixer_gain_part, mixer_bias_part, feed_gain_part, feed_bias_part)
-
     def head_places(at):
         return [(member, at, member * KEY, KEY) for member in range(GROUP)]
 
@@ -600,8 +566,42 @@
         ]
 
     query_grad, key_grad = lay_out(qk_grads, [head_places(0), head_places(KEY)])
+    feed_gate_grad, feed_up_grad = lay_out(feed_grads, [hidden_places(0), hidden_places(hidden)])
+    (out_grad,) = after([out_grad], feed_up_grad, key_grad)
+    out_product = dot_rows(gated_all.reshape(GROUP * length, VAL), out_grad).astype(BF16)
+    vg_grads = to_owners(sum_layers(vg_product))
+    output_grad = lax.psum_scatter(
+        to_members(out_product, "core"), "z", scatter_dimension=0, tiled=True
+    ).astype(F32)
+
+    slot_out = (hidden_state + feed_terms.total()).astype(BF16)
+    half = length // 2
+    from_x, from_y = swap(slot_out, "x"), swap(slot_out, "y")
+    across = jnp.concatenate(
+        after([swap(from_y[:half], "x"), swap(from_x[half:], "y")], vg_grads), axis=0
+    )
+    reached = jnp.stack([slot_out, from_x, from_y, across])
+    chosen = lax.dynamic_index_in_dim(reached, own_slot, 0, keepdims=False)
+    out_tokens = (live_mask * chosen.astype(F32)).astype(BF16)
+
+    summed = GroupSum()
+    for n in order:
+        summed.terms(n, results[n][3:5])
     value_grad, gate_grad = lay_out(vg_grads, [value_places(0), value_places(VAL)])
-    feed_gate_grad, feed_up_grad = lay_out(feed_grads, [hidden_places(0), hidden_places(hidden)])
+    mixer_normed_grad = summed.total(out_product, gate_grad)
+    mixer_hat, mixer_inverse = statistics(tokens[0].astype(F32), EPSILON)
+    mixer_gain_part = jnp.sum(mixer_normed_grad * mixer_hat, axis=0)
+    mixer_bias_part = jnp.sum(mixer_normed_grad, axis=0)
+    input_grad = (
+        state_grad + pull_back(mixer_hat, mixer_inverse, mixer_normed_grad * features[0])
+    ).astype(BF16)
+
+    def vector_grads(*grads):
+        split = jnp.stack(grads).reshape(len(grads), devices, -1).transpose(1, 0, 2)
+        return jnp.sum(to_members(split, EVERY), axis=0)
+
+    vector_sums = vector_grads(mixer_gain_part, mixer_bias_part, feed_gain_part, feed_bias_part)
+
 
     return (
         out_tokens[None],

time: 688 us -> 691 us (level)
    all_to_all x7, waiting for transfers between devices: 51.2 us -> 59 us  [to_members(): return lax.all_to_all(packed, axes, 0, 0, tiled=True)]
    unnamed x154 -> x160, local copies, waits for them, and re-layouts: 40.6 us -> 44.2 us
  transfers between devices with their start and end apart: 96 -> 96, of which waited for: 27 -> 26; matrix products, arithmetic and copies ran while one was open for 21% -> 21% of each run, Pallas kernels for 24% -> 23%
where the time goes in v5:
time: 691 us; the launch traced here: 682 us
  Pallas kernels  177 us (26%)
  waiting for transfers between devices  166 us (24%)
  starting transfers between devices  82.7 us (12%)
  local copies, waits for them, and re-layouts  68 us (10%)
  other arithmetic  66.3 us (10%)
  matrix products  56.4 us (8%)
  between operations  34.1 us (5%)
  blocking collectives  32.5 us (5%)
    pallas_call x16, Pallas kernels, chunk_call(): pl.pallas_call(kernel, grid=(1,), out_shape=outs, in_specs=[whole_spec(o)...  169 us
    ppermute x80, waiting for transfers between devices, swap(): return lax.ppermute(field_in, axis, [(0, 1), (1, 0)])  71.5 us
    all_to_all x7, waiting for transfers between devices, to_members(): return lax.all_to_all(packed, axes, 0, 0, tiled=True)  59 us
    dot_general x5, matrix products, dot_rows(): lax.dot_general(left, right, (((0,), (0,)), ((), ())), preferred_element_...  56.4 us
    ppermute x80, starting transfers between devices, swap(): return lax.ppermute(field_in, axis, [(0, 1), (1, 0)])  54 us
    unnamed x160, local copies, waits for them, and re-layouts  44.2 us
    all_to_all x2, blocking collectives, to_members(): return lax.all_to_all(packed, axes, 0, 0, tiled=True)  32.5 us
    all_gather x2, waiting for transfers between devices, gather_layers(): lax.all_gather(mine.reshape(4, 2 * local_model, -1), 'z', axis=1, tiled=T...  32.4 us
  transfers between devices with their start and end apart: 96, of which 26 were waited for; matrix products, arithmetic and copies ran while one was open for 21% of the time, Pallas kernels for 23%

profile of v5, /device:TPU:0, one launch (start us, length us, event | category | flops | bytes accessed | tf_op | source)
XLA Modules:
  0.0 682.4 jit_solution(8871005078932069609)
XLA Ops:
  11.4 26.2 %all_to_all.58 = bf16[8,64,1536]{2,1,0:T(8,128)(2,1)} all-to-all(bf16[8,64,1536]{2,1,0:T(8,128)(2,1)S(1)} %pad_maximum_fusion), channel_id=1, replica_groups=mesh['y'=2,'x'=2,'z'=4,'core'=2] {'y','x','core'}, dimensions={0} | all-to-all | bytes 3145728 | tf_op jit(solution)/shard_map/all_to_all | solution.py:358
  44.4 4.0 all-to-all-start
  72.5 13.1 %all-to-all-done = bf16[32,2,128]{2,1,0:T(2,128)(2,1)S(1)} async-done(((bf16[32,2,128]{2,1,0:T(2,128)(2,1)}), bf16[32,2,128]{2,1,0:T(2,128)(2,1)S(1)}, u32[]{:S(2)}, u32[]{:S(2)}) %all-to-all-start) | async-done | bytes 16416 | tf_op jit(solution)/shard_map/all_to_all | solution.py:358
  85.7 3.6 all-to-all-start.3
  93.3 11.3 %all-to-all-done.3 = bf16[8,64,1024]{2,1,0:T(8,128)(2,1)S(1)} async-done(((bf16[8,64,1024]{2,1,0:T(8,128)(2,1)}), bf16[8,64,1024]{2,1,0:T(8,128)(2,1)S(1)}, u32[]{:S(2)}, u32[]{:S(2)}) %all-to-all-start.3) | async-done | bytes 1048608 | tf_op jit(solution)/shard_map/all_to_all | solution.py:358
  123.3 10.0 %collective-permute-done.15 = bf16[128,2048]{1,0:T(8,128)(2,1)S(1)} collective-permute-done((bf16[128,2048]{1,0:T(8,128)(2,1)S(1)}, bf16[128,2048]{1,0:T(8,128)(2,1)S(1)}, u32[]{:S(2)}, u32[]{:S(2)}) %collective-permute-start.15) | collective-permute-done | bytes 524320 | tf_op jit(solution)/shard_map/ppermute | solution.py:245
  152.3 3.8 all-to-all-start.2
  158.9 15.1 %all-gather.5.cloned.1.call-done = bf16[4,512,1536]{2,1,0:T(8,128)(2,1)} async-done(((bf16[4,128,1536]{2,1,0:T(8,128)(2,1)}), bf16[4,512,1536]{2,1,0:T(8,128)(2,1)}) %all-gather.5.cloned.1.call-update) | async-done | bytes 6291472 | tf_op jit(solution)/shard_map/all_gather | solution.py:361
  174.0 12.0 %mixer_forward.4 = (bf16[8,256,2048]{2,1,0:T(8,128)(2,1)}, bf16[8,256,1024]{2,1,0:T(8,128)(2,1)}, f32[8,256,512]{2,1,0:T(8,128)}, bf16[8,256,512]{2,1,0:T(8,128)...) custom-call(bf16[128,2048]{1,0:T(8,128)(2,1)} %collective-permute-done.5.refs_0_, ...), custom_call_target="tpu_custom_call" | custom-call | tf_op jit(solution)/shard_map/mixer_forward/pallas_call | solution.py:111
  186.5 12.0 %mixer_forward.5 = (bf16[8,256,2048]{2,1,0:T(8,128)(2,1)}, bf16[8,256,1024]{2,1,0:T(8,128)(2,1)}, f32[8,256,512]{2,1,0:T(8,128)}, bf16[8,256,512]{2,1,0:T(8,128)...) custom-call(bf16[256,2048]{1,0:T(8,128)(2,1)} %collective-permute-do, ...), custom_call_target="tpu_custom_call", output_to_operand_aliasing={{0}: (7, {}), {1}: (8, {}), {2}: (9, {}), {3}: (10, {})} | custom-call | tf_op jit(solution)/shard_map/mixer_forward/pallas_call | solution.py:111
  203.0 12.4 %mixer_forward.6 = (bf16[8,256,2048]{2,1,0:T(8,128)(2,1)}, bf16[8,256,1024]{2,1,0:T(8,128)(2,1)}, f32[8,256,512]{2,1,0:T(8,128)}, bf16[8,256,512]{2,1,0:T(8,128)...) custom-call(bf16[256,2048]{1,0:T(8,128)(2,1)} %collective-permute-do, ...), custom_call_target="tpu_custom_call", output_to_operand_aliasing={{0}: (7, {}), {1}: (8, {}), {2}: (9, {}), {3}: (10, {})} | custom-call | tf_op jit(solution)/shard_map/mixer_forward/pallas_call | solution.py:111
  224.5 12.1 %mixer_forward.7 = (bf16[8,256,2048]{2,1,0:T(8,128)(2,1)}, bf16[8,256,1024]{2,1,0:T(8,128)(2,1)}, f32[8,256,512]{2,1,0:T(8,128)}, bf16[8,256,512]{2,1,0:T(8,128)...) custom-call(bf16[256,2048]{1,0:T(8,128)(2,1)} %bitcast.148, ...), custom_call_target="tpu_custom_call", output_to_operand_aliasing={{0}: (7, {}), {1}: (8, {}), {2}: (9, {}), {3}: (10, {})} | custom-call | tf_op jit(solution)/shard_map/mixer_forward/pallas_call | solution.py:111
  237.7 17.4 %all-gather.9.cloned.1.call-done = bf16[4,512,1024]{2,1,0:T(8,128)(2,1)} async-done(((bf16[4,128,1024]{2,1,0:T(8,128)(2,1)}), bf16[4,512,1024]{2,1,0:T(8,128)(2,1)}) %all-gather.9.cloned.1.call-update) | async-done | bytes 4194320 | tf_op jit(solution)/shard_map/all_gather | solution.py:361
  256.1 3.9 fusion.31
  267.2 6.9 %feed_forward.4 = (bf16[8,256,2048]{2,1,0:T(8,128)(2,1)}, bf16[8,256,512]{2,1,0:T(8,128)(2,1)}, f32[8,256,1024]{2,1,0:T(8,128)}, f32[8,128]{1,0:T(8,128)}) custom-call(bf16[256,2048]{1,0:T(8,128)(2,1)} %copy-done.9, bf16[256,2048]{1,0:T(8,128)(2,1)} %copy-done.46, bf16[2048,1024]{1,0:T(8,128)(2,1)} %bitcast.122), custom_call_target="tpu_custom_call" | custom-call | tf_op jit(solution)/shard_map/feed_forward/pallas_call | solution.py:111
  278.7 9.0 %collective-permute-done.31.refs_0_ = bf16[128,2048]{1,0:T(8,128)(2,1)S(1)} collective-permute-done((bf16[128,2048]{1,0:T(8,128)(2,1)}, bf16[128,2048]{1,0:T(8,128)(2,1)S(1)}, u32[]{:S(2)}, u32[]{:S(2)}) %collective-permute-start.31) | collective-permute-done | bytes 524320 | tf_op jit(solution)/shard_map/ppermute | solution.py:245
  293.3 6.9 %feed_forward.5 = (bf16[8,256,2048]{2,1,0:T(8,128)(2,1)}, bf16[8,256,512]{2,1,0:T(8,128)(2,1)}, f32[8,256,1024]{2,1,0:T(8,128)}, f32[8,128]{1,0:T(8,128)}) custom-call(bf16[128,2048]{1,0:T(8,128)(2,1)} %get-tuple-element.161.refs_0_, ...), custom_call_target="tpu_custom_call", output_to_operand_aliasing={{0}: (5, {}), {1}: (6, {}), {2}: (7, {})} | custom-call | tf_op jit(solution)/shard_map/feed_forward/pallas_call | solution.py:111
  300.2 3.4 collective-permute-done.29.refs_0_
  305.6 6.9 %feed_forward.6 = (bf16[8,256,2048]{2,1,0:T(8,128)(2,1)}, bf16[8,256,512]{2,1,0:T(8,128)(2,1)}, f32[8,256,1024]{2,1,0:T(8,128)}, f32[8,128]{1,0:T(8,128)}) custom-call(bf16[128,2048]{1,0:T(8,128)(2,1)} %get-tuple-element.159.refs_0_, bf16[128,2048]{1,0:T(8,128)(2,1)} %get-tuple-element.168.refs_1_, ...), custom_call_target="tpu_custom_call", output_to_operand_aliasing={{0}: (5, {}), {1}: (6, {}), {2}: (7, {})} | custom-call | tf_op jit(solution)/shard_map/feed_forward/pallas_call | solution.py:111
  313.5 6.9 %feed_forward.7 = (bf16[8,256,2048]{2,1,0:T(8,128)(2,1)}, bf16[8,256,512]{2,1,0:T(8,128)(2,1)}, f32[8,256,1024]{2,1,0:T(8,128)}, f32[8,128]{1,0:T(8,128)}) custom-call(bf16[128,2048]{1,0:T(8,128)(2,1)} %get-tuple-element.166.refs_0_, bf16[128,2048]{1,0:T(8,128)(2,1)} %get-tuple-element.167.refs_1_, ...), custom_call_target="tpu_custom_call", output_to_operand_aliasing={{0}: (5, {}), {1}: (6, {}), {2}: (7, {})} | custom-call | tf_op jit(solution)/shard_map/feed_forward/pallas_call | solution.py:111
  320.3 10.2 %bitcast_convert_fusion.1.refs_5_.refs_6_ = bf16[512,2048]{1,0:T(8,128)(2,1)} fusion(bf16[8,256,512]{2,1,0:T(8,128)(2,1)} %get-tuple-element.175.refs_2_, bf16[8,256,2048]{2,1,0:T(8,128)(2,1)} %dynamic-slice_dynamic-update-slice_fusion.refs_9_.refs_11_.refs_4_), kind=kOutput, calls=%fused_computation.5 | convolution fusion | flops 4296015872 | bytes 12582912 | tf_op jit(solution)/shard_map/dot_general | solution.py:29
  330.5 9.9 %feed_backward.4 = (bf16[8,256,1024]{2,1,0:T(8,128)(2,1)}, bf16[256,2048]{1,0:T(8,128)(2,1)}, bf16[256,2048]{1,0:T(8,128)(2,1)}, bf16[256,2048]{1,0:T(8,128)(2,1)}, bf16[256,2048]{1,0:T(8,128)(2,1)}) custom-call(bf16[2048,1024]{1,0:T(8,128)(2,1)} %bitcast.126, bf16[512,2048]{1,0:T(8,128)(2,1)} %all-gather.11.cloned.1.call-done.refs_8_.refs_1_, ...), custom_call_target="tpu_custom_call" | custom-call | tf_op jit(solution)/shard_map/feed_backward/pallas_call | solution.py:111
  340.9 10.3 %feed_backward.5 = (bf16[8,256,1024]{2,1,0:T(8,128)(2,1)}, bf16[256,2048]{1,0:T(8,128)(2,1)}, bf16[256,2048]{1,0:T(8,128)(2,1)}, bf16[256,2048]{1,0:T(8,128)(2,1)}, bf16[256,2048]{1,0:T(8,128)(2,1)}) custom-call(bf16[2048,1024]{1,0:T(8,128)(2,1)} %bitcast.127, ...), custom_call_target="tpu_custom_call", output_to_operand_aliasing={{0}: (5, {})} | custom-call | tf_op jit(solution)/shard_map/feed_backward/pallas_call | solution.py:111
  354.6 10.0 %feed_backward.6 = (bf16[8,256,1024]{2,1,0:T(8,128)(2,1)}, bf16[256,2048]{1,0:T(8,128)(2,1)}, bf16[256,2048]{1,0:T(8,128)(2,1)}, bf16[256,2048]{1,0:T(8,128)(2,1)}, bf16[256,2048]{1,0:T(8,128)(2,1)}) custom-call(bf16[2048,1024]{1,0:T(8,128)(2,1)} %bitcast.128, ...), custom_call_target="tpu_custom_call", output_to_operand_aliasing={{0}: (5, {})} | custom-call | tf_op jit(solution)/shard_map/feed_backward/pallas_call | solution.py:111
  374.3 10.2 %feed_backward.7 = (bf16[8,256,1024]{2,1,0:T(8,128)(2,1)}, bf16[256,2048]{1,0:T(8,128)(2,1)}, bf16[256,2048]{1,0:T(8,128)(2,1)}, bf16[256,2048]{1,0:T(8,128)(2,1)}, bf16[256,2048]{1,0:T(8,128)(2,1)}) custom-call(bf16[2048,1024]{1,0:T(8,128)(2,1)} %bitcast.129, ...), custom_call_target="tpu_custom_call", output_to_operand_aliasing={{0}: (5, {})} | custom-call | tf_op jit(solution)/shard_map/feed_backward/pallas_call | solution.py:111
  384.5 14.0 %bitcast_convert_fusion.refs_2_ = bf16[2048,1024]{1,0:T(8,128)(2,1)} fusion(bf16[8,256,2048]{2,1,0:T(8,128)(2,1)} %get-tuple-element.198, bf16[8,256,1024]{2,1,0:T(8,128)(2,1)} %get-tuple-element.199), kind=kOutput, calls=%fused_computation | convolution fusion | flops 8592031744 | bytes 16777216 | tf_op jit(solution)/shard_map/dot_general | solution.py:29
  399.5 3.5 multiply_reduce_fusion
  403.0 3.4 fusion.30
  412.5 13.0 %mixer_backward.4 = (bf16[8,256,2048]{2,1,0:T(8,128)(2,1)}, bf16[8,256,512]{2,1,0:T(8,128)(2,1)}, bf16[8,256,1024]{2,1,0:T(8,128)(2,1)}, bf16[256,2048]{1,0:T(8,128)(2,1)}, bf16[256,2048]{1,0:T(8,128)(2,1)}) custom-call(bf16[256,2048]{1,0:T(8,128)(2,1)} %copy-done.21, bf16[256,2048]{1,0:T(8,128)(2,1)} %collective-permute-done.51.refs_1_, ...), custom_call_target="tpu_custom_call" | custom-call | flops 20000000000 | tf_op jit(solution)/shard_map/mixer_backward/pallas_call | solution.py:111
  425.5 8.8 %collective-permute-done.50.refs_1_ = bf16[128,2048]{1,0:T(8,128)(2,1)} collective-permute-done((bf16[128,2048]{1,0:T(8,128)(2,1)}, bf16[128,2048]{1,0:T(8,128)(2,1)}, u32[]{:S(2)}, u32[]{:S(2)}) %collective-permute-start.50) | collective-permute-done | bytes 524320 | tf_op jit(solution)/shard_map/ppermute | solution.py:245
  439.1 13.5 %mixer_backward.5 = (bf16[8,256,2048]{2,1,0:T(8,128)(2,1)}, bf16[8,256,512]{2,1,0:T(8,128)(2,1)}, bf16[8,256,1024]{2,1,0:T(8,128)(2,1)}, bf16[256,2048]{1,0:T(8,128)(2,1)}, bf16[256,2048]{1,0:T(8,128)(2,1)}) custom-call(bf16[128,2048]{1,0:T(8,128)(2,1)} %get-tuple-element.206.refs_0_, ...), custom_call_target="tpu_custom_call", output_to_operand_aliasing={{0}: (10, {}), {1}: (11, {}), {2}: (12, {})} | custom-call | flops 20000000000 | tf_op jit(solution)/shard_map/mixer_backward/pallas_call | solution.py:111
  453.2 13.2 %mixer_backward.6 = (bf16[8,256,2048]{2,1,0:T(8,128)(2,1)}, bf16[8,256,512]{2,1,0:T(8,128)(2,1)}, bf16[8,256,1024]{2,1,0:T(8,128)(2,1)}, bf16[256,2048]{1,0:T(8,128)(2,1)}, bf16[256,2048]{1,0:T(8,128)(2,1)}) custom-call(bf16[128,2048]{1,0:T(8,128)(2,1)} %get-tuple-element.222.refs_0_, ...), custom_call_target="tpu_custom_call", output_to_operand_aliasing={{0}: (10, {}), {1}: (11, {}), {2}: (12, {})} | custom-call | flops 20000000000 | tf_op jit(solution)/shard_map/mixer_backward/pallas_call | solution.py:111
  468.7 13.3 %mixer_backward.7 = (bf16[8,256,2048]{2,1,0:T(8,128)(2,1)}, bf16[8,256,512]{2,1,0:T(8,128)(2,1)}, bf16[8,256,1024]{2,1,0:T(8,128)(2,1)}, bf16[256,2048]{1,0:T(8,128)(2,1)}, bf16[256,2048]{1,0:T(8,128)(2,1)}) custom-call(bf16[128,2048]{1,0:T(8,128)(2,1)} %get-tuple-element.223.refs_0_, ...), custom_call_target="tpu_custom_call", output_to_operand_aliasing={{0}: (10, {}), {1}: (11, {}), {2}: (12, {})} | custom-call | flops 20000000000 | tf_op jit(solution)/shard_map/mixer_backward/pallas_call | solution.py:111
  482.1 9.9 %convolution_convert_fusion.2 = bf16[2048,512]{1,0:T(8,128)(2,1)} fusion(bf16[2048,2048]{1,0:T(8,128)(2,1)} %bitcast.138, bf16[2048,512]{1,0:T(8,128)(2,1)} %after.33), kind=kOutput, calls=%fused_computation.11 | convolution fusion | flops 4296015872 | bytes 12582912 | tf_op jit(solution)/shard_map/dot_general | solution.py:29
  495.8 12.2 %collective-permute-done.57.refs_0_ = bf16[128,2048]{1,0:T(8,128)(2,1)} collective-permute-done((bf16[128,2048]{1,0:T(8,128)(2,1)S(1)}, bf16[128,2048]{1,0:T(8,128)(2,1)}, u32[]{:S(2)}, u32[]{:S(2)}) %collective-permute-start.57) | collective-permute-done | bytes 524320 | tf_op jit(solution)/shard_map/ppermute | solution.py:245
  514.4 14.1 %convolution_convert_fusion = bf16[2048,1024]{1,0:T(8,128)(2,1)} fusion(bf16[2048,2048]{1,0:T(8,128)(2,1)} %bitcast.139, bf16[2048,1024]{1,0:T(8,128)(2,1)} %after.30), kind=kOutput, calls=%fused_computation.6 | convolution fusion | flops 8592031744 | bytes 16777216 | tf_op jit(solution)/shard_map/dot_general | solution.py:29
  531.0 4.2 all-to-all-start.5
  539.9 15.5 %collective-permute-done.61 = bf16[256,2048]{1,0:T(8,128)(2,1)} collective-permute-done((bf16[256,2048]{1,0:T(8,128)(2,1)}, bf16[256,2048]{1,0:T(8,128)(2,1)}, u32[]{:S(2)}, u32[]{:S(2)}) %collective-permute-start.61) | collective-permute-done | bytes 1048608 | tf_op jit(solution)/shard_map/ppermute | solution.py:245
  557.5 10.7 %all-to-all-done.5.block = bf16[8,64,1024]{2,1,0:T(8,128)(2,1)} async-done(((bf16[8,64,1024]{2,1,0:T(8,128)(2,1)}), bf16[8,64,1024]{2,1,0:T(8,128)(2,1)}, u32[]{:S(2)}, u32[]{:S(2)}) %all-to-all-start.5) | async-done | bytes 1048608 | tf_op jit(solution)/shard_map/all_to_all | solution.py:358
  568.1 4.1 all-to-all-start.6
  572.6 3.6 add_convert_fusion.3
  588.6 8.2 %convolution_convert_fusion.1.refs_2_ = bf16[512,2048]{1,0:T(8,128)(2,1)S(1)} fusion(bf16[2048,512]{1,0:T(8,128)(2,1)S(1)} %bitcast.152, bf16[2048,2048]{1,0:T(8,128)(2,1)} %after.34), kind=kOutput, calls=%fused_computation.10 | convolution fusion | flops 4296015872 | bytes 12582912 | tf_op jit(solution)/shard_map/dot_general | solution.py:29
  596.8 6.3 all_to_all.59
  613.9 3.6 all-to-all-start.4
  629.7 18.4 %all-to-all-done.4.refs_2_.block = bf16[8,64,1024]{2,1,0:T(8,128)(2,1)S(1)} async-done(((bf16[8,64,1024]{2,1,0:T(8,128)(2,1)}), bf16[8,64,1024]{2,1,0:T(8,128)(2,1)S(1)}, u32[]{:S(2)}, u32[]{:S(2)}) %all-to-all-start.4) | async-done | bytes 1048608 | tf_op jit(solution)/shard_map/all_to_all | solution.py:358
  654.2 4.9 fusion.10
  660.0 4.0 all-to-all-start.7
  668.4 3.1 multiply_convert_fusion
  (452 shorter events, 195.3 us)
Async XLA Ops:
  7.2 145.1 %all-gather.7.cloned.1.call-start = ((), (), s32[]{:S(2)}) async-start(), calls=%async_computation.15 | async-start | bytes 2621440 | tf_op jit(solution)/shard_map/all_gather | solution.py:376
  7.9 166.1 %all-gather.5.cloned.1.call-start = ((), (), s32[]{:S(2)}) async-start(), calls=%async_computation.14 | async-start | bytes 7864320 | tf_op jit(solution)/shard_map/all_gather | solution.py:361
  37.6 69.6 %collective-permute-start.3 = (bf16[256,2048]{1,0:T(8,128)(2,1)S(1)}, bf16[256,2048]{1,0:T(8,128)(2,1)}, u32[]{:S(2)}, u32[]{:S(2)}) collective-permute-start(bf16[256,2048]{1,0:T(8,128)(2,1)S(1)} %bitcast.149), channel_id=1, source_target_pairs={{0,8},{8,0},{1,9},{9,1},{2,10},{10,2},{3,11},{11,3},{4,12},{12,4},... | collective-permute-start | bytes 3145736 | tf_op jit(solution)/shard_map/ppermute | solution.py:245
  38.3 67.3 %collective-permute-start.1 = (bf16[256,2048]{1,0:T(8,128)(2,1)S(1)}, bf16[256,2048]{1,0:T(8,128)(2,1)}, u32[]{:S(2)}, u32[]{:S(2)}) collective-permute-start(bf16[256,2048]{1,0:T(8,128)(2,1)S(1)} %bitcast.150), channel_id=1, source_target_pairs={{0,16},{16,0},{1,17},{17,1},{2,18},{18,2},{3,19},{19,3},{4,20},{20... | collective-permute-start | bytes 3145736 | tf_op jit(solution)/shard_map/ppermute | solution.py:245
  40.7 69.4 %collective-permute-start.9 = (bf16[256,2048]{1,0:T(8,128)(2,1)}, bf16[256,2048]{1,0:T(8,128)(2,1)}, u32[]{:S(2)}, u32[]{:S(2)}) collective-permute-start(bf16[256,2048]{1,0:T(8,128)(2,1)} %fusion.14), channel_id=1, source_target_pairs={{0,1},{1,0},{2,3},{3,2},{4,5},{5,4},{6,7},{7,6},{8,9},{9,8},{10,11... | collective-permute-start | bytes 3145736 | tf_op jit(solution)/shard_map/ppermute | solution.py:245
  40.7 51.4 %collective-permute-start.10 = (bf16[256,2048]{1,0:T(8,128)(2,1)}, bf16[256,2048]{1,0:T(8,128)(2,1)}, u32[]{:S(2)}, u32[]{:S(2)}) collective-permute-start(bf16[256,2048]{1,0:T(8,128)(2,1)} %fusion.14), channel_id=1, source_target_pairs={{0,8},{8,0},{1,9},{9,1},{2,10},{10,2},{3,11},{11,3},{4,12},{12,4},... | collective-permute-start | bytes 3145736 | tf_op jit(solution)/shard_map/ppermute | solution.py:245
  42.2 69.4 %collective-permute-start.12 = (bf16[256,2048]{1,0:T(8,128)(2,1)}, bf16[256,2048]{1,0:T(8,128)(2,1)}, u32[]{:S(2)}, u32[]{:S(2)}) collective-permute-start(bf16[256,2048]{1,0:T(8,128)(2,1)} %fusion.14), channel_id=1, source_target_pairs={{0,16},{16,0},{1,17},{17,1},{2,18},{18,2},{3,19},{19,3},{4,20},{20... | collective-permute-start | bytes 3145736 | tf_op jit(solution)/shard_map/ppermute | solution.py:245
  44.4 41.3 %all-to-all-start = ((bf16[32,2,128]{2,1,0:T(2,128)(2,1)}), bf16[32,2,128]{2,1,0:T(2,128)(2,1)S(1)}, u32[]{:S(2)}, u32[]{:S(2)}) async-start(bf16[32,2,128]{2,1,0:T(2,128)(2,1)} %reshape.621), calls=%async_computation | async-start | bytes 32768 | tf_op jit(solution)/shard_map/all_to_all | solution.py:358
  85.7 18.9 %all-to-all-start.3 = ((bf16[8,64,1024]{2,1,0:T(8,128)(2,1)}), bf16[8,64,1024]{2,1,0:T(8,128)(2,1)S(1)}, u32[]{:S(2)}, u32[]{:S(2)}) async-start(bf16[8,64,1024]{2,1,0:T(8,128)(2,1)} %pad_maximum_fusion.1), calls=%async_computation.3 | async-start | bytes 2097152 | tf_op jit(solution)/shard_map/all_to_all | solution.py:358
  89.2 165.8 %all-gather.9.cloned.1.call-start = ((), (), s32[]{:S(2)}) async-start(), calls=%async_computation.16 | async-start | bytes 5242880 | tf_op jit(solution)/shard_map/all_gather | solution.py:361
  92.1 25.2 %collective-permute-start.11 = (bf16[256,2048]{1,0:T(8,128)(2,1)}, bf16[256,2048]{1,0:T(8,128)(2,1)S(1)}, u32[]{:S(2)}, u32[]{:S(2)}) collective-permute-start(bf16[256,2048]{1,0:T(8,128)(2,1)} %collective-permute-done.10), channel_id=1, source_target_pairs={{0,1},{1,0},{2,3},{3,2},{4,5},{5,4},{6,7},{7,6},{8,9},{9,8},{10,11... | collective-permute-start | bytes 3145736 | tf_op jit(solution)/shard_map/ppermute | solution.py:245
  110.1 23.2 %collective-permute-start.15 = (bf16[128,2048]{1,0:T(8,128)(2,1)S(1)}, bf16[128,2048]{1,0:T(8,128)(2,1)S(1)}, u32[]{:S(2)}, u32[]{:S(2)}) collective-permute-start(bf16[128,2048]{1,0:T(8,128)(2,1)S(1)} %slice.123), channel_id=1, source_target_pairs={{0,16},{16,0},{1,17},{17,1},{2,18},{18,2},{3,19},{19,3},{4,20},{20... | collective-permute-start | bytes 1572872 | tf_op jit(solution)/shard_map/ppermute | solution.py:245
  111.6 22.3 %collective-permute-start.13 = (bf16[256,2048]{1,0:T(8,128)(2,1)}, bf16[256,2048]{1,0:T(8,128)(2,1)S(1)}, u32[]{:S(2)}, u32[]{:S(2)}) collective-permute-start(bf16[256,2048]{1,0:T(8,128)(2,1)} %collective-permute-done.12), channel_id=1, source_target_pairs={{0,1},{1,0},{2,3},{3,2},{4,5},{5,4},{6,7},{7,6},{8,9},{9,8},{10,11... | collective-permute-start | bytes 3145736 | tf_op jit(solution)/shard_map/ppermute | solution.py:245
  122.3 64.2 %collective-permute-start.4 = (bf16[256,2048]{1,0:T(8,128)(2,1)}, bf16[256,2048]{1,0:T(8,128)(2,1)}, u32[]{:S(2)}, u32[]{:S(2)}) collective-permute-start(bf16[256,2048]{1,0:T(8,128)(2,1)} %collective-permute-done.3.refs_0_), channel_id=1, source_target_pairs={{0,1},{1,0},{2,3},{3,2},{4,5},{5,4},{6,7},{7,6},{8,9},{9,8},{10,11... | collective-permute-start | bytes 3145736 | tf_op jit(solution)/shard_map/ppermute | solution.py:245
  123.3 33.0 %collective-permute-start.7 = (bf16[128,2048]{1,0:T(8,128)(2,1)}, bf16[128,2048]{1,0:T(8,128)(2,1)}, u32[]{:S(2)}, u32[]{:S(2)}) collective-permute-start(bf16[128,2048]{1,0:T(8,128)(2,1)} %collective-permute-done.5.refs_0_), channel_id=1, source_target_pairs={{0,1},{1,0},{2,3},{3,2},{4,5},{5,4},{6,7},{7,6},{8,9},{9,8},{10,11... | collective-permute-start | bytes 1572872 | tf_op jit(solution)/shard_map/ppermute | solution.py:245
  133.3 23.0 %collective-permute-start.8 = (bf16[128,2048]{1,0:T(8,128)(2,1)}, bf16[128,2048]{1,0:T(8,128)(2,1)}, u32[]{:S(2)}, u32[]{:S(2)}) collective-permute-start(bf16[128,2048]{1,0:T(8,128)(2,1)} %collective-permute-done.6.refs_1_), channel_id=1, source_target_pairs={{0,1},{1,0},{2,3},{3,2},{4,5},{5,4},{6,7},{7,6},{8,9},{9,8},{10,11... | collective-permute-start | bytes 1572872 | tf_op jit(solution)/shard_map/ppermute | solution.py:245
  156.1 156.4 %all-gather.11.cloned.1.call-start = ((), (), s32[]{:S(2)}) async-start(), calls=%async_computation.17 | async-start | bytes 2621440 | tf_op jit(solution)/shard_map/all_gather | solution.py:392
  198.5 19.0 %collective-permute-start.19 = (bf16[256,2048]{1,0:T(8,128)(2,1)}, bf16[256,2048]{1,0:T(8,128)(2,1)S(1)}, u32[]{:S(2)}, u32[]{:S(2)}) collective-permute-start(bf16[256,2048]{1,0:T(8,128)(2,1)} %get-tuple-element.149), channel_id=1, source_target_pairs={{0,1},{1,0},{2,3},{3,2},{4,5},{5,4},{6,7},{7,6},{8,9},{9,8},{10,11... | collective-permute-start | bytes 3145736 | tf_op jit(solution)/shard_map/ppermute | solution.py:245
  220.6 34.5 %collective-permute-start.24 = (bf16[256,2048]{1,0:T(8,128)(2,1)S(1)}, bf16[256,2048]{1,0:T(8,128)(2,1)}, u32[]{:S(2)}, u32[]{:S(2)}) collective-permute-start(bf16[256,2048]{1,0:T(8,128)(2,1)S(1)} %add_convert_fusion.12.refs_13_), channel_id=1, source_target_pairs={{0,8},{8,0},{1,9},{9,1},{2,10},{10,2},{3,11},{11,3},{4,12},{12,4},... | collective-permute-start | bytes 3145736 | tf_op jit(solution)/shard_map/ppermute | solution.py:245
  223.9 31.2 %collective-permute-start.25 = (bf16[256,2048]{1,0:T(8,128)(2,1)}, bf16[256,2048]{1,0:T(8,128)(2,1)}, u32[]{:S(2)}, u32[]{:S(2)}) collective-permute-start(bf16[256,2048]{1,0:T(8,128)(2,1)} %add_convert_fusion.11.refs_14_), channel_id=1, source_target_pairs={{0,16},{16,0},{1,17},{17,1},{2,18},{18,2},{3,19},{19,3},{4,20},{20... | collective-permute-start | bytes 3145736 | tf_op jit(solution)/shard_map/ppermute | solution.py:245
  236.6 18.5 %collective-permute-start.23 = (bf16[256,2048]{1,0:T(8,128)(2,1)}, bf16[256,2048]{1,0:T(8,128)(2,1)S(1)}, u32[]{:S(2)}, u32[]{:S(2)}) collective-permute-start(bf16[256,2048]{1,0:T(8,128)(2,1)} %get-tuple-element.155), channel_id=1, source_target_pairs={{0,1},{1,0},{2,3},{3,2},{4,5},{5,4},{6,7},{7,6},{8,9},{9,8},{10,11... | collective-permute-start | bytes 3145736 | tf_op jit(solution)/shard_map/ppermute | solution.py:245
  236.6 161.9 %reduce-scatter.6.cloned.1.call-start = ((), (), s32[]{:S(2)}) async-start(), calls=%async_computation.18 | async-start | bytes 2621440 | tf_op jit(solution)/shard_map/reduce_scatter | solution.py:475
  265.1 22.7 %collective-permute-start.31 = (bf16[128,2048]{1,0:T(8,128)(2,1)}, bf16[128,2048]{1,0:T(8,128)(2,1)S(1)}, u32[]{:S(2)}, u32[]{:S(2)}) collective-permute-start(bf16[128,2048]{1,0:T(8,128)(2,1)} %get-tuple-element.280), channel_id=1, source_target_pairs={{0,8},{8,0},{1,9},{9,1},{2,10},{10,2},{3,11},{11,3},{4,12},{12,4},... | collective-permute-start | bytes 1572872 | tf_op jit(solution)/shard_map/ppermute | solution.py:245
  265.6 23.4 %collective-permute-start.32 = (bf16[128,2048]{1,0:T(8,128)(2,1)}, bf16[128,2048]{1,0:T(8,128)(2,1)}, u32[]{:S(2)}, u32[]{:S(2)}) collective-permute-start(bf16[128,2048]{1,0:T(8,128)(2,1)} %get-tuple-element.281), channel_id=1, source_target_pairs={{0,16},{16,0},{1,17},{17,1},{2,18},{18,2},{3,19},{19,3},{4,20},{20... | collective-permute-start | bytes 1572872 | tf_op jit(solution)/shard_map/ppermute | solution.py:245
  340.5 141.6 %reduce-scatter.10.cloned.1.call-start = ((), (), s32[]{:S(2)}) async-start(), calls=%async_computation.20 | async-start | bytes 5242880 | tf_op jit(solution)/shard_map/reduce_scatter | solution.py:507
  370.5 28.0 %collective-permute-start.45 = (bf16[256,2048]{1,0:T(8,128)(2,1)S(1)}, bf16[256,2048]{1,0:T(8,128)(2,1)S(1)}, u32[]{:S(2)}, u32[]{:S(2)}) collective-permute-start(bf16[256,2048]{1,0:T(8,128)(2,1)S(1)} %add_convert_fusion.8.refs_8_), channel_id=1, source_target_pairs={{0,8},{8,0},{1,9},{9,1},{2,10},{10,2},{3,11},{11,3},{4,12},{12,4},... | collective-permute-start | bytes 3145736 | tf_op jit(solution)/shard_map/ppermute | solution.py:245
  373.2 25.3 %collective-permute-start.46 = (bf16[256,2048]{1,0:T(8,128)(2,1)S(1)}, bf16[256,2048]{1,0:T(8,128)(2,1)}, u32[]{:S(2)}, u32[]{:S(2)}) collective-permute-start(bf16[256,2048]{1,0:T(8,128)(2,1)S(1)} %add_convert_fusion.7.refs_9_), channel_id=1, source_target_pairs={{0,16},{16,0},{1,17},{17,1},{2,18},{18,2},{3,19},{19,3},{4,20},{20... | collective-permute-start | bytes 3145736 | tf_op jit(solution)/shard_map/ppermute | solution.py:245
  406.9 161.2 %reduce-scatter.12.cloned.1.call-start = ((), (), s32[]{:S(2)}) async-start(), calls=%async_computation.21 | async-start | bytes 2621440 | tf_op jit(solution)/shard_map/reduce_scatter | solution.py:507
  408.4 26.6 %collective-permute-start.48 = (bf16[128,2048]{1,0:T(8,128)(2,1)}, bf16[128,2048]{1,0:T(8,128)(2,1)}, u32[]{:S(2)}, u32[]{:S(2)}) collective-permute-start(bf16[128,2048]{1,0:T(8,128)(2,1)} %get-tuple-element.276), channel_id=1, source_target_pairs={{0,16},{16,0},{1,17},{17,1},{2,18},{18,2},{3,19},{19,3},{4,20},{20... | collective-permute-start | bytes 1572872 | tf_op jit(solution)/shard_map/ppermute | solution.py:245
  410.6 24.4 %collective-permute-start.47 = (bf16[128,2048]{1,0:T(8,128)(2,1)}, bf16[128,2048]{1,0:T(8,128)(2,1)}, u32[]{:S(2)}, u32[]{:S(2)}) collective-permute-start(bf16[128,2048]{1,0:T(8,128)(2,1)} %get-tuple-element.277), channel_id=1, source_target_pairs={{0,8},{8,0},{1,9},{9,1},{2,10},{10,2},{3,11},{11,3},{4,12},{12,4},... | collective-permute-start | bytes 1572872 | tf_op jit(solution)/shard_map/ppermute | solution.py:245
  411.4 22.9 %collective-permute-start.50 = (bf16[128,2048]{1,0:T(8,128)(2,1)}, bf16[128,2048]{1,0:T(8,128)(2,1)}, u32[]{:S(2)}, u32[]{:S(2)}) collective-permute-start(bf16[128,2048]{1,0:T(8,128)(2,1)} %get-tuple-element.277), channel_id=1, source_target_pairs={{0,16},{16,0},{1,17},{17,1},{2,18},{18,2},{3,19},{19,3},{4,20},{20... | collective-permute-start | bytes 1572872 | tf_op jit(solution)/shard_map/ppermute | solution.py:245
  492.0 121.9 %reduce-scatter.8.cloned.1.call-start = ((), (), s32[]{:S(2)}) async-start(), calls=%async_computation.19 | async-start | bytes 5242880 | tf_op jit(solution)/shard_map/reduce_scatter | solution.py:507
  529.1 26.3 %collective-permute-start.61 = (bf16[256,2048]{1,0:T(8,128)(2,1)}, bf16[256,2048]{1,0:T(8,128)(2,1)}, u32[]{:S(2)}, u32[]{:S(2)}) collective-permute-start(bf16[256,2048]{1,0:T(8,128)(2,1)} %add_convert_fusion.4.refs_2_), channel_id=1, source_target_pairs={{0,16},{16,0},{1,17},{17,1},{2,18},{18,2},{3,19},{19,3},{4,20},{20... | collective-permute-start | bytes 3145736 | tf_op jit(solution)/shard_map/ppermute | solution.py:245
  530.1 42.4 %collective-permute-start.59 = (bf16[256,2048]{1,0:T(8,128)(2,1)}, bf16[256,2048]{1,0:T(8,128)(2,1)}, u32[]{:S(2)}, u32[]{:S(2)}) collective-permute-start(bf16[256,2048]{1,0:T(8,128)(2,1)} %add_convert_fusion.5.refs_1_), channel_id=1, source_target_pairs={{0,8},{8,0},{1,9},{9,1},{2,10},{10,2},{3,11},{11,3},{4,12},{12,4},... | collective-permute-start | bytes 3145736 | tf_op jit(solution)/shard_map/ppermute | solution.py:245
  531.0 72.2 %collective-permute-start.73 = (bf16[256,2048]{1,0:T(8,128)(2,1)}, bf16[256,2048]{1,0:T(8,128)(2,1)}, u32[]{:S(2)}, u32[]{:S(2)}) collective-permute-start(bf16[256,2048]{1,0:T(8,128)(2,1)} %get-tuple-element.210.refs_8_.refs_2_), channel_id=1, source_target_pairs={{0,1},{1,0},{2,3},{3,2},{4,5},{5,4},{6,7},{7,6},{8,9},{9,8},{10,11... | collective-permute-start | bytes 3145736 | tf_op jit(solution)/shard_map/ppermute | solution.py:245
  531.0 37.1 %all-to-all-start.5 = ((bf16[8,64,1024]{2,1,0:T(8,128)(2,1)}), bf16[8,64,1024]{2,1,0:T(8,128)(2,1)}, u32[]{:S(2)}, u32[]{:S(2)}) async-start(bf16[8,64,1024]{2,1,0:T(8,128)(2,1)} %bitcast.48), calls=%async_computation.8 | async-start | bytes 2097152 | tf_op jit(solution)/shard_map/all_to_all | solution.py:358
  535.2 72.5 %collective-permute-start.78 = (bf16[256,2048]{1,0:T(8,128)(2,1)}, bf16[256,2048]{1,0:T(8,128)(2,1)}, u32[]{:S(2)}, u32[]{:S(2)}) collective-permute-start(bf16[256,2048]{1,0:T(8,128)(2,1)} %get-tuple-element.241), channel_id=1, source_target_pairs={{0,1},{1,0},{2,3},{3,2},{4,5},{5,4},{6,7},{7,6},{8,9},{9,8},{10,11... | collective-permute-start | bytes 3145736 | tf_op jit(solution)/shard_map/ppermute | solution.py:245
  538.4 39.6 %collective-permute-start.75 = (bf16[128,2048]{1,0:T(8,128)(2,1)}, bf16[128,2048]{1,0:T(8,128)(2,1)}, u32[]{:S(2)}, u32[]{:S(2)}) collective-permute-start(bf16[128,2048]{1,0:T(8,128)(2,1)} %get-tuple-element.272), channel_id=1, source_target_pairs={{0,16},{16,0},{1,17},{17,1},{2,18},{18,2},{3,19},{19,3},{4,20},{20... | collective-permute-start | bytes 1572872 | tf_op jit(solution)/shard_map/ppermute | solution.py:245
  555.4 24.1 %collective-permute-start.76 = (bf16[128,2048]{1,0:T(8,128)(2,1)}, bf16[128,2048]{1,0:T(8,128)(2,1)}, u32[]{:S(2)}, u32[]{:S(2)}) collective-permute-start(bf16[128,2048]{1,0:T(8,128)(2,1)} %get-tuple-element.271), channel_id=1, source_target_pairs={{0,8},{8,0},{1,9},{9,1},{2,10},{10,2},{3,11},{11,3},{4,12},{12,4},... | collective-permute-start | bytes 1572872 | tf_op jit(solution)/shard_map/ppermute | solution.py:245
  572.3 101.2 %reduce-scatter.14.cloned.1.call-start = ((), (), s32[]{:S(2)}) async-start(), calls=%async_computation.22 | async-start | bytes 2621440 | tf_op jit(solution)/shard_map/reduce_scatter | solution.py:573
  576.2 50.1 %collective-permute-start.62 = (bf16[256,2048]{1,0:T(8,128)(2,1)}, bf16[256,2048]{1,0:T(8,128)(2,1)}, u32[]{:S(2)}, u32[]{:S(2)}) collective-permute-start(bf16[256,2048]{1,0:T(8,128)(2,1)} %add_convert_fusion.3), channel_id=1, source_target_pairs={{0,8},{8,0},{1,9},{9,1},{2,10},{10,2},{3,11},{11,3},{4,12},{12,4},... | collective-permute-start | bytes 3145736 | tf_op jit(solution)/shard_map/ppermute | solution.py:245
  578.0 44.4 %collective-permute-start.63 = (bf16[256,2048]{1,0:T(8,128)(2,1)}, bf16[256,2048]{1,0:T(8,128)(2,1)}, u32[]{:S(2)}, u32[]{:S(2)}) collective-permute-start(bf16[256,2048]{1,0:T(8,128)(2,1)} %add_convert_fusion.3), channel_id=1, source_target_pairs={{0,16},{16,0},{1,17},{17,1},{2,18},{18,2},{3,19},{19,3},{4,20},{20... | collective-permute-start | bytes 3145736 | tf_op jit(solution)/shard_map/ppermute | solution.py:245
  607.2 44.4 %collective-permute-start.77 = (bf16[256,2048]{1,0:T(8,128)(2,1)}, bf16[256,2048]{1,0:T(8,128)(2,1)S(1)}, u32[]{:S(2)}, u32[]{:S(2)}) collective-permute-start(bf16[256,2048]{1,0:T(8,128)(2,1)} %add_convert_fusion.1), channel_id=1, source_target_pairs={{0,8},{8,0},{1,9},{9,1},{2,10},{10,2},{3,11},{11,3},{4,12},{12,4},... | collective-permute-start | bytes 3145736 | tf_op jit(solution)/shard_map/ppermute | solution.py:245
  610.6 41.1 %collective-permute-start.79 = (bf16[256,2048]{1,0:T(8,128)(2,1)}, bf16[256,2048]{1,0:T(8,128)(2,1)S(1)}, u32[]{:S(2)}, u32[]{:S(2)}) collective-permute-start(bf16[256,2048]{1,0:T(8,128)(2,1)} %add_convert_fusion), channel_id=1, source_target_pairs={{0,16},{16,0},{1,17},{17,1},{2,18},{18,2},{3,19},{19,3},{4,20},{20... | collective-permute-start | bytes 3145736 | tf_op jit(solution)/shard_map/ppermute | solution.py:245
  611.9 41.1 %collective-permute-start.72 = (bf16[256,2048]{1,0:T(8,128)(2,1)}, bf16[256,2048]{1,0:T(8,128)(2,1)}, u32[]{:S(2)}, u32[]{:S(2)}) collective-permute-start(bf16[256,2048]{1,0:T(8,128)(2,1)} %get-tuple-element.204.refs_2_), channel_id=1, source_target_pairs={{0,1},{1,0},{2,3},{3,2},{4,5},{5,4},{6,7},{7,6},{8,9},{9,8},{10,11... | collective-permute-start | bytes 3145736 | tf_op jit(solution)/shard_map/ppermute | solution.py:245
  613.9 34.2 %all-to-all-start.4 = ((bf16[8,64,1024]{2,1,0:T(8,128)(2,1)}), bf16[8,64,1024]{2,1,0:T(8,128)(2,1)S(1)}, u32[]{:S(2)}, u32[]{:S(2)}) async-start(bf16[8,64,1024]{2,1,0:T(8,128)(2,1)} %bitcast.168), calls=%async_computation.6 | async-start | bytes 2097152 | tf_op jit(solution)/shard_map/all_to_all | solution.py:358
  624.3 39.7 %collective-permute-start.64 = (bf16[128,2048]{1,0:T(8,128)(2,1)}, bf16[128,2048]{1,0:T(8,128)(2,1)}, u32[]{:S(2)}, u32[]{:S(2)}) collective-permute-start(bf16[128,2048]{1,0:T(8,128)(2,1)} %slice.136), channel_id=1, source_target_pairs={{0,8},{8,0},{1,9},{9,1},{2,10},{10,2},{3,11},{11,3},{4,12},{12,4},... | collective-permute-start | bytes 1572872 | tf_op jit(solution)/shard_map/ppermute | solution.py:245
  628.2 35.9 %collective-permute-start.65 = (bf16[128,2048]{1,0:T(8,128)(2,1)}, bf16[128,2048]{1,0:T(8,128)(2,1)}, u32[]{:S(2)}, u32[]{:S(2)}) collective-permute-start(bf16[128,2048]{1,0:T(8,128)(2,1)} %slice.137), channel_id=1, source_target_pairs={{0,16},{16,0},{1,17},{17,1},{2,18},{18,2},{3,19},{19,3},{4,20},{20... | collective-permute-start | bytes 1572872 | tf_op jit(solution)/shard_map/ppermute | solution.py:245
  (119 other events, 931.3 us)
Sparse Core Ops, SparseCore 0:
  9.6 48.7 all-gather.6
  59.9 114.0 all-gather.4
  176.1 78.9 all-gather.8
  256.5 44.1 all-gather.10
  340.6 41.8 reduce-scatter.5
  407.1 74.2 reduce-scatter.9
  492.1 43.3 reduce-scatter.11
  537.9 75.9 reduce-scatter.7
  616.2 44.1 reduce-scatter.13

commit v6 on v5

--- a/solution.py
+++ b/solution.py
@@ -587,8 +587,8 @@
     summed = GroupSum()
     for n in order:
         summed.terms(n, results[n][3:5])
+    mixer_normed_grad = summed.total(out_product, vg_grads)
     value_grad, gate_grad = lay_out(vg_grads, [value_places(0), value_places(VAL)])
-    mixer_normed_grad = summed.total(out_product, gate_grad)
     mixer_hat, mixer_inverse = statistics(tokens[0].astype(F32), EPSILON)
     mixer_gain_part = jnp.sum(mixer_normed_grad * mixer_hat, axis=0)
     mixer_bias_part = jnp.sum(mixer_normed_grad, axis=0)

time: 691 us -> 690 us (level)
    ppermute x80, waiting for transfers between devices: 71.5 us -> 82.7 us  [swap(): return lax.ppermute(field_in, axis, [(0, 1), (1, 0)])]
    all_to_all x7, waiting for transfers between devices: 59 us -> 48.9 us  [to_members(): return lax.all_to_all(packed, axes, 0, 0, tiled=True)]
    unnamed x160 -> x156, local copies, waits for them, and re-layouts: 44.2 us -> 40.6 us
  transfers between devices with their start and end apart: 96 -> 96, of which waited for: 26 -> 28; matrix products, arithmetic and copies ran while one was open for 21% -> 21% of each run, Pallas kernels for 23% -> 23%
where the time goes in v6:
time: 690 us; the launch traced here: 681 us
  Pallas kernels  177 us (26%)
  waiting for transfers between devices  167 us (24%)
  starting transfers between devices  82.8 us (12%)
  other arithmetic  67.3 us (10%)
  local copies, waits for them, and re-layouts  64.4 us (9%)
  matrix products  56.4 us (8%)
  between operations  34.1 us (5%)
  blocking collectives  32.5 us (5%)
    pallas_call x16, Pallas kernels, chunk_call(): pl.pallas_call(kernel, grid=(1,), out_shape=outs, in_specs=[whole_spec(o)...  169 us
    ppermute x80, waiting for transfers between devices, swap(): return lax.ppermute(field_in, axis, [(0, 1), (1, 0)])  82.7 us
    dot_general x5, matrix products, dot_rows(): lax.dot_general(left, right, (((0,), (0,)), ((), ())), preferred_element_...  56.4 us
    ppermute x80, starting transfers between devices, swap(): return lax.ppermute(field_in, axis, [(0, 1), (1, 0)])  54 us
    all_to_all x7, waiting for transfers between devices, to_members(): return lax.all_to_all(packed, axes, 0, 0, tiled=True)  48.9 us
    unnamed x156, local copies, waits for them, and re-layouts  40.6 us
    all_to_all x2, blocking collectives, to_members(): return lax.all_to_all(packed, axes, 0, 0, tiled=True)  32.5 us
    all_gather x2, waiting for transfers between devices, gather_layers(): lax.all_gather(mine.reshape(4, 2 * local_model, -1), 'z', axis=1, tiled=T...  32.5 us
  transfers between devices with their start and end apart: 96, of which 28 were waited for; matrix products, arithmetic and copies ran while one was open for 21% of the time, Pallas kernels for 23%

profile of v6, /device:TPU:0, one launch (start us, length us, event | category | flops | bytes accessed | tf_op | source)
XLA Modules:
  0.0 681.0 jit_solution(11636977930284438411)
XLA Ops:
  11.4 26.2 %all_to_all.58 = bf16[8,64,1536]{2,1,0:T(8,128)(2,1)} all-to-all(bf16[8,64,1536]{2,1,0:T(8,128)(2,1)S(1)} %pad_maximum_fusion), channel_id=1, replica_groups=mesh['y'=2,'x'=2,'z'=4,'core'=2] {'y','x','core'}, dimensions={0} | all-to-all | bytes 3145728 | tf_op jit(solution)/shard_map/all_to_all | solution.py:358
  44.4 4.0 all-to-all-start
  72.5 13.1 %all-to-all-done = bf16[32,2,128]{2,1,0:T(2,128)(2,1)S(1)} async-done(((bf16[32,2,128]{2,1,0:T(2,128)(2,1)}), bf16[32,2,128]{2,1,0:T(2,128)(2,1)S(1)}, u32[]{:S(2)}, u32[]{:S(2)}) %all-to-all-start) | async-done | bytes 16416 | tf_op jit(solution)/shard_map/all_to_all | solution.py:358
  85.7 3.6 all-to-all-start.3
  93.2 11.3 %all-to-all-done.3 = bf16[8,64,1024]{2,1,0:T(8,128)(2,1)S(1)} async-done(((bf16[8,64,1024]{2,1,0:T(8,128)(2,1)}), bf16[8,64,1024]{2,1,0:T(8,128)(2,1)S(1)}, u32[]{:S(2)}, u32[]{:S(2)}) %all-to-all-start.3) | async-done | bytes 1048608 | tf_op jit(solution)/shard_map/all_to_all | solution.py:358
  123.3 10.0 %collective-permute-done.15 = bf16[128,2048]{1,0:T(8,128)(2,1)S(1)} collective-permute-done((bf16[128,2048]{1,0:T(8,128)(2,1)S(1)}, bf16[128,2048]{1,0:T(8,128)(2,1)S(1)}, u32[]{:S(2)}, u32[]{:S(2)}) %collective-permute-start.15) | collective-permute-done | bytes 524320 | tf_op jit(solution)/shard_map/ppermute | solution.py:245
  152.3 3.8 all-to-all-start.2
  158.9 15.1 %all-gather.5.cloned.1.call-done = bf16[4,512,1536]{2,1,0:T(8,128)(2,1)} async-done(((bf16[4,128,1536]{2,1,0:T(8,128)(2,1)}), bf16[4,512,1536]{2,1,0:T(8,128)(2,1)}) %all-gather.5.cloned.1.call-update) | async-done | bytes 6291472 | tf_op jit(solution)/shard_map/all_gather | solution.py:361
  174.0 12.0 %mixer_forward.4 = (bf16[8,256,2048]{2,1,0:T(8,128)(2,1)}, bf16[8,256,1024]{2,1,0:T(8,128)(2,1)}, f32[8,256,512]{2,1,0:T(8,128)}, bf16[8,256,512]{2,1,0:T(8,128)...) custom-call(bf16[128,2048]{1,0:T(8,128)(2,1)} %collective-permute-done.5.refs_0_, ...), custom_call_target="tpu_custom_call" | custom-call | tf_op jit(solution)/shard_map/mixer_forward/pallas_call | solution.py:111
  186.5 12.0 %mixer_forward.5 = (bf16[8,256,2048]{2,1,0:T(8,128)(2,1)}, bf16[8,256,1024]{2,1,0:T(8,128)(2,1)}, f32[8,256,512]{2,1,0:T(8,128)}, bf16[8,256,512]{2,1,0:T(8,128)...) custom-call(bf16[256,2048]{1,0:T(8,128)(2,1)} %collective-permute-do, ...), custom_call_target="tpu_custom_call", output_to_operand_aliasing={{0}: (7, {}), {1}: (8, {}), {2}: (9, {}), {3}: (10, {})} | custom-call | tf_op jit(solution)/shard_map/mixer_forward/pallas_call | solution.py:111
  203.0 12.4 %mixer_forward.6 = (bf16[8,256,2048]{2,1,0:T(8,128)(2,1)}, bf16[8,256,1024]{2,1,0:T(8,128)(2,1)}, f32[8,256,512]{2,1,0:T(8,128)}, bf16[8,256,512]{2,1,0:T(8,128)...) custom-call(bf16[256,2048]{1,0:T(8,128)(2,1)} %collective-permute-do, ...), custom_call_target="tpu_custom_call", output_to_operand_aliasing={{0}: (7, {}), {1}: (8, {}), {2}: (9, {}), {3}: (10, {})} | custom-call | tf_op jit(solution)/shard_map/mixer_forward/pallas_call | solution.py:111
  224.5 12.1 %mixer_forward.7 = (bf16[8,256,2048]{2,1,0:T(8,128)(2,1)}, bf16[8,256,1024]{2,1,0:T(8,128)(2,1)}, f32[8,256,512]{2,1,0:T(8,128)}, bf16[8,256,512]{2,1,0:T(8,128)...) custom-call(bf16[256,2048]{1,0:T(8,128)(2,1)} %bitcast.148, ...), custom_call_target="tpu_custom_call", output_to_operand_aliasing={{0}: (7, {}), {1}: (8, {}), {2}: (9, {}), {3}: (10, {})} | custom-call | tf_op jit(solution)/shard_map/mixer_forward/pallas_call | solution.py:111
  237.7 17.4 %all-gather.9.cloned.1.call-done = bf16[4,512,1024]{2,1,0:T(8,128)(2,1)} async-done(((bf16[4,128,1024]{2,1,0:T(8,128)(2,1)}), bf16[4,512,1024]{2,1,0:T(8,128)(2,1)}) %all-gather.9.cloned.1.call-update) | async-done | bytes 4194320 | tf_op jit(solution)/shard_map/all_gather | solution.py:361
  256.1 3.9 fusion.31
  267.2 6.9 %feed_forward.4 = (bf16[8,256,2048]{2,1,0:T(8,128)(2,1)}, bf16[8,256,512]{2,1,0:T(8,128)(2,1)}, f32[8,256,1024]{2,1,0:T(8,128)}, f32[8,128]{1,0:T(8,128)}) custom-call(bf16[256,2048]{1,0:T(8,128)(2,1)} %copy-done.9, bf16[256,2048]{1,0:T(8,128)(2,1)} %copy-done.44, bf16[2048,1024]{1,0:T(8,128)(2,1)} %bitcast.122), custom_call_target="tpu_custom_call" | custom-call | tf_op jit(solution)/shard_map/feed_forward/pallas_call | solution.py:111
  278.7 9.0 %collective-permute-done.31.refs_0_ = bf16[128,2048]{1,0:T(8,128)(2,1)S(1)} collective-permute-done((bf16[128,2048]{1,0:T(8,128)(2,1)}, bf16[128,2048]{1,0:T(8,128)(2,1)S(1)}, u32[]{:S(2)}, u32[]{:S(2)}) %collective-permute-start.31) | collective-permute-done | bytes 524320 | tf_op jit(solution)/shard_map/ppermute | solution.py:245
  293.3 6.9 %feed_forward.5 = (bf16[8,256,2048]{2,1,0:T(8,128)(2,1)}, bf16[8,256,512]{2,1,0:T(8,128)(2,1)}, f32[8,256,1024]{2,1,0:T(8,128)}, f32[8,128]{1,0:T(8,128)}) custom-call(bf16[128,2048]{1,0:T(8,128)(2,1)} %get-tuple-element.161.refs_0_, ...), custom_call_target="tpu_custom_call", output_to_operand_aliasing={{0}: (5, {}), {1}: (6, {}), {2}: (7, {})} | custom-call | tf_op jit(solution)/shard_map/feed_forward/pallas_call | solution.py:111
  305.6 6.9 %feed_forward.6 = (bf16[8,256,2048]{2,1,0:T(8,128)(2,1)}, bf16[8,256,512]{2,1,0:T(8,128)(2,1)}, f32[8,256,1024]{2,1,0:T(8,128)}, f32[8,128]{1,0:T(8,128)}) custom-call(bf16[128,2048]{1,0:T(8,128)(2,1)} %get-tuple-element.159.refs_0_, bf16[128,2048]{1,0:T(8,128)(2,1)} %get-tuple-element.168.refs_1_, ...), custom_call_target="tpu_custom_call", output_to_operand_aliasing={{0}: (5, {}), {1}: (6, {}), {2}: (7, {})} | custom-call | tf_op jit(solution)/shard_map/feed_forward/pallas_call | solution.py:111
  313.5 6.9 %feed_forward.7 = (bf16[8,256,2048]{2,1,0:T(8,128)(2,1)}, bf16[8,256,512]{2,1,0:T(8,128)(2,1)}, f32[8,256,1024]{2,1,0:T(8,128)}, f32[8,128]{1,0:T(8,128)}) custom-call(bf16[128,2048]{1,0:T(8,128)(2,1)} %get-tuple-element.166.refs_0_, bf16[128,2048]{1,0:T(8,128)(2,1)} %get-tuple-element.167.refs_1_, ...), custom_call_target="tpu_custom_call", output_to_operand_aliasing={{0}: (5, {}), {1}: (6, {}), {2}: (7, {})} | custom-call | tf_op jit(solution)/shard_map/feed_forward/pallas_call | solution.py:111
  320.4 10.2 %bitcast_convert_fusion.1.refs_5_.refs_6_ = bf16[512,2048]{1,0:T(8,128)(2,1)} fusion(bf16[8,256,512]{2,1,0:T(8,128)(2,1)} %get-tuple-element.175.refs_2_, bf16[8,256,2048]{2,1,0:T(8,128)(2,1)} %dynamic-slice_dynamic-update-slice_fusion.refs_9_.refs_11_.refs_4_), kind=kOutput, calls=%fused_computation.5 | convolution fusion | flops 4296015872 | bytes 12582912 | tf_op jit(solution)/shard_map/dot_general | solution.py:29
  330.6 9.9 %feed_backward.4 = (bf16[8,256,1024]{2,1,0:T(8,128)(2,1)}, bf16[256,2048]{1,0:T(8,128)(2,1)}, bf16[256,2048]{1,0:T(8,128)(2,1)}, bf16[256,2048]{1,0:T(8,128)(2,1)}, bf16[256,2048]{1,0:T(8,128)(2,1)}) custom-call(bf16[2048,1024]{1,0:T(8,128)(2,1)} %bitcast.126, bf16[512,2048]{1,0:T(8,128)(2,1)} %all-gather.11.cloned.1.call-done.refs_8_.refs_1_, ...), custom_call_target="tpu_custom_call" | custom-call | tf_op jit(solution)/shard_map/feed_backward/pallas_call | solution.py:111
  341.0 10.3 %feed_backward.5 = (bf16[8,256,1024]{2,1,0:T(8,128)(2,1)}, bf16[256,2048]{1,0:T(8,128)(2,1)}, bf16[256,2048]{1,0:T(8,128)(2,1)}, bf16[256,2048]{1,0:T(8,128)(2,1)}, bf16[256,2048]{1,0:T(8,128)(2,1)}) custom-call(bf16[2048,1024]{1,0:T(8,128)(2,1)} %bitcast.127, ...), custom_call_target="tpu_custom_call", output_to_operand_aliasing={{0}: (5, {})} | custom-call | tf_op jit(solution)/shard_map/feed_backward/pallas_call | solution.py:111
  354.7 10.0 %feed_backward.6 = (bf16[8,256,1024]{2,1,0:T(8,128)(2,1)}, bf16[256,2048]{1,0:T(8,128)(2,1)}, bf16[256,2048]{1,0:T(8,128)(2,1)}, bf16[256,2048]{1,0:T(8,128)(2,1)}, bf16[256,2048]{1,0:T(8,128)(2,1)}) custom-call(bf16[2048,1024]{1,0:T(8,128)(2,1)} %bitcast.128, ...), custom_call_target="tpu_custom_call", output_to_operand_aliasing={{0}: (5, {})} | custom-call | tf_op jit(solution)/shard_map/feed_backward/pallas_call | solution.py:111
  374.4 10.2 %feed_backward.7 = (bf16[8,256,1024]{2,1,0:T(8,128)(2,1)}, bf16[256,2048]{1,0:T(8,128)(2,1)}, bf16[256,2048]{1,0:T(8,128)(2,1)}, bf16[256,2048]{1,0:T(8,128)(2,1)}, bf16[256,2048]{1,0:T(8,128)(2,1)}) custom-call(bf16[2048,1024]{1,0:T(8,128)(2,1)} %bitcast.129, ...), custom_call_target="tpu_custom_call", output_to_operand_aliasing={{0}: (5, {})} | custom-call | tf_op jit(solution)/shard_map/feed_backward/pallas_call | solution.py:111
  384.5 14.0 %bitcast_convert_fusion.refs_2_ = bf16[2048,1024]{1,0:T(8,128)(2,1)} fusion(bf16[8,256,2048]{2,1,0:T(8,128)(2,1)} %get-tuple-element.198, bf16[8,256,1024]{2,1,0:T(8,128)(2,1)} %get-tuple-element.199), kind=kOutput, calls=%fused_computation | convolution fusion | flops 8592031744 | bytes 16777216 | tf_op jit(solution)/shard_map/dot_general | solution.py:29
  399.5 3.5 multiply_reduce_fusion
  412.5 13.0 %mixer_backward.4 = (bf16[8,256,2048]{2,1,0:T(8,128)(2,1)}, bf16[8,256,512]{2,1,0:T(8,128)(2,1)}, bf16[8,256,1024]{2,1,0:T(8,128)(2,1)}, bf16[256,2048]{1,0:T(8,128)(2,1)}, bf16[256,2048]{1,0:T(8,128)(2,1)}) custom-call(bf16[256,2048]{1,0:T(8,128)(2,1)} %copy-done.19, bf16[256,2048]{1,0:T(8,128)(2,1)} %collective-permute-done.51.refs_1_, ...), custom_call_target="tpu_custom_call" | custom-call | flops 20000000000 | tf_op jit(solution)/shard_map/mixer_backward/pallas_call | solution.py:111
  425.6 8.8 %collective-permute-done.50.refs_1_ = bf16[128,2048]{1,0:T(8,128)(2,1)} collective-permute-done((bf16[128,2048]{1,0:T(8,128)(2,1)}, bf16[128,2048]{1,0:T(8,128)(2,1)}, u32[]{:S(2)}, u32[]{:S(2)}) %collective-permute-start.50) | collective-permute-done | bytes 524320 | tf_op jit(solution)/shard_map/ppermute | solution.py:245
  439.2 13.5 %mixer_backward.5 = (bf16[8,256,2048]{2,1,0:T(8,128)(2,1)}, bf16[8,256,512]{2,1,0:T(8,128)(2,1)}, bf16[8,256,1024]{2,1,0:T(8,128)(2,1)}, bf16[256,2048]{1,0:T(8,128)(2,1)}, bf16[256,2048]{1,0:T(8,128)(2,1)}) custom-call(bf16[128,2048]{1,0:T(8,128)(2,1)} %get-tuple-element.206.refs_0_, ...), custom_call_target="tpu_custom_call", output_to_operand_aliasing={{0}: (10, {}), {1}: (11, {}), {2}: (12, {})} | custom-call | flops 20000000000 | tf_op jit(solution)/shard_map/mixer_backward/pallas_call | solution.py:111
  453.3 13.2 %mixer_backward.6 = (bf16[8,256,2048]{2,1,0:T(8,128)(2,1)}, bf16[8,256,512]{2,1,0:T(8,128)(2,1)}, bf16[8,256,1024]{2,1,0:T(8,128)(2,1)}, bf16[256,2048]{1,0:T(8,128)(2,1)}, bf16[256,2048]{1,0:T(8,128)(2,1)}) custom-call(bf16[128,2048]{1,0:T(8,128)(2,1)} %get-tuple-element.222.refs_0_, ...), custom_call_target="tpu_custom_call", output_to_operand_aliasing={{0}: (10, {}), {1}: (11, {}), {2}: (12, {})} | custom-call | flops 20000000000 | tf_op jit(solution)/shard_map/mixer_backward/pallas_call | solution.py:111
  468.8 13.3 %mixer_backward.7 = (bf16[8,256,2048]{2,1,0:T(8,128)(2,1)}, bf16[8,256,512]{2,1,0:T(8,128)(2,1)}, bf16[8,256,1024]{2,1,0:T(8,128)(2,1)}, bf16[256,2048]{1,0:T(8,128)(2,1)}, bf16[256,2048]{1,0:T(8,128)(2,1)}) custom-call(bf16[128,2048]{1,0:T(8,128)(2,1)} %get-tuple-element.223.refs_0_, ...), custom_call_target="tpu_custom_call", output_to_operand_aliasing={{0}: (10, {}), {1}: (11, {}), {2}: (12, {})} | custom-call | flops 20000000000 | tf_op jit(solution)/shard_map/mixer_backward/pallas_call | solution.py:111
  482.2 9.9 %convolution_convert_fusion.2 = bf16[2048,512]{1,0:T(8,128)(2,1)} fusion(bf16[2048,2048]{1,0:T(8,128)(2,1)} %bitcast.138, bf16[2048,512]{1,0:T(8,128)(2,1)} %after.33), kind=kOutput, calls=%fused_computation.11 | convolution fusion | flops 4296015872 | bytes 12582912 | tf_op jit(solution)/shard_map/dot_general | solution.py:29
  495.9 12.2 %collective-permute-done.57.refs_0_ = bf16[128,2048]{1,0:T(8,128)(2,1)} collective-permute-done((bf16[128,2048]{1,0:T(8,128)(2,1)S(1)}, bf16[128,2048]{1,0:T(8,128)(2,1)}, u32[]{:S(2)}, u32[]{:S(2)}) %collective-permute-start.57) | collective-permute-done | bytes 524320 | tf_op jit(solution)/shard_map/ppermute | solution.py:245
  514.5 14.1 %convolution_convert_fusion = bf16[2048,1024]{1,0:T(8,128)(2,1)} fusion(bf16[2048,2048]{1,0:T(8,128)(2,1)} %bitcast.139, bf16[2048,1024]{1,0:T(8,128)(2,1)} %after.30), kind=kOutput, calls=%fused_computation.6 | convolution fusion | flops 8592031744 | bytes 16777216 | tf_op jit(solution)/shard_map/dot_general | solution.py:29
  531.0 4.3 all-to-all-start.5
  540.0 15.5 %collective-permute-done.61 = bf16[256,2048]{1,0:T(8,128)(2,1)} collective-permute-done((bf16[256,2048]{1,0:T(8,128)(2,1)}, bf16[256,2048]{1,0:T(8,128)(2,1)}, u32[]{:S(2)}, u32[]{:S(2)}) %collective-permute-start.61) | collective-permute-done | bytes 1048608 | tf_op jit(solution)/shard_map/ppermute | solution.py:245
  557.5 10.7 %all-to-all-done.5.block = bf16[8,64,1024]{2,1,0:T(8,128)(2,1)} async-done(((bf16[8,64,1024]{2,1,0:T(8,128)(2,1)}), bf16[8,64,1024]{2,1,0:T(8,128)(2,1)}, u32[]{:S(2)}, u32[]{:S(2)}) %all-to-all-start.5) | async-done | bytes 1048608 | tf_op jit(solution)/shard_map/all_to_all | solution.py:358
  568.2 4.1 all-to-all-start.6
  572.7 3.6 add_convert_fusion.3
  588.7 8.2 %convolution_convert_fusion.1.refs_2_ = bf16[512,2048]{1,0:T(8,128)(2,1)S(1)} fusion(bf16[2048,512]{1,0:T(8,128)(2,1)S(1)} %bitcast.152, bf16[2048,2048]{1,0:T(8,128)(2,1)} %after.34), kind=kOutput, calls=%fused_computation.10 | convolution fusion | flops 4296015872 | bytes 12582912 | tf_op jit(solution)/shard_map/dot_general | solution.py:29
  596.9 6.3 all_to_all.59
  613.9 3.7 all-to-all-start.4
  628.7 4.8 collective-permute-done.77.refs_0_
  633.5 6.3 collective-permute-done.79.refs_1_
  639.9 8.3 %all-to-all-done.4.refs_2_.refs_3_.block = bf16[8,64,1024]{2,1,0:T(8,128)(2,1)S(1)} async-done(((bf16[8,64,1024]{2,1,0:T(8,128)(2,1)}), bf16[8,64,1024]{2,1,0:T(8,128)(2,1)S(1)}, u32[]{:S(2)}, u32[]{:S(2)}) %all-to-all-start.4) | async-done | bytes 1048608 | tf_op jit(solution)/shard_map/all_to_all | solution.py:358
  649.2 4.9 fusion.10
  655.0 4.1 all-to-all-start.7
  660.4 4.0 fusion.16
  (448 shorter events, 198.6 us)
Async XLA Ops:
  7.2 145.1 %all-gather.7.cloned.1.call-start = ((), (), s32[]{:S(2)}) async-start(), calls=%async_computation.15 | async-start | bytes 2621440 | tf_op jit(solution)/shard_map/all_gather | solution.py:376
  7.9 166.1 %all-gather.5.cloned.1.call-start = ((), (), s32[]{:S(2)}) async-start(), calls=%async_computation.14 | async-start | bytes 7864320 | tf_op jit(solution)/shard_map/all_gather | solution.py:361
  37.6 69.6 %collective-permute-start.3 = (bf16[256,2048]{1,0:T(8,128)(2,1)S(1)}, bf16[256,2048]{1,0:T(8,128)(2,1)}, u32[]{:S(2)}, u32[]{:S(2)}) collective-permute-start(bf16[256,2048]{1,0:T(8,128)(2,1)S(1)} %bitcast.149), channel_id=1, source_target_pairs={{0,8},{8,0},{1,9},{9,1},{2,10},{10,2},{3,11},{11,3},{4,12},{12,4},... | collective-permute-start | bytes 3145736 | tf_op jit(solution)/shard_map/ppermute | solution.py:245
  38.3 67.3 %collective-permute-start.1 = (bf16[256,2048]{1,0:T(8,128)(2,1)S(1)}, bf16[256,2048]{1,0:T(8,128)(2,1)}, u32[]{:S(2)}, u32[]{:S(2)}) collective-permute-start(bf16[256,2048]{1,0:T(8,128)(2,1)S(1)} %bitcast.150), channel_id=1, source_target_pairs={{0,16},{16,0},{1,17},{17,1},{2,18},{18,2},{3,19},{19,3},{4,20},{20... | collective-permute-start | bytes 3145736 | tf_op jit(solution)/shard_map/ppermute | solution.py:245
  40.7 69.4 %collective-permute-start.9 = (bf16[256,2048]{1,0:T(8,128)(2,1)}, bf16[256,2048]{1,0:T(8,128)(2,1)}, u32[]{:S(2)}, u32[]{:S(2)}) collective-permute-start(bf16[256,2048]{1,0:T(8,128)(2,1)} %fusion.14), channel_id=1, source_target_pairs={{0,1},{1,0},{2,3},{3,2},{4,5},{5,4},{6,7},{7,6},{8,9},{9,8},{10,11... | collective-permute-start | bytes 3145736 | tf_op jit(solution)/shard_map/ppermute | solution.py:245
  40.7 51.3 %collective-permute-start.10 = (bf16[256,2048]{1,0:T(8,128)(2,1)}, bf16[256,2048]{1,0:T(8,128)(2,1)}, u32[]{:S(2)}, u32[]{:S(2)}) collective-permute-start(bf16[256,2048]{1,0:T(8,128)(2,1)} %fusion.14), channel_id=1, source_target_pairs={{0,8},{8,0},{1,9},{9,1},{2,10},{10,2},{3,11},{11,3},{4,12},{12,4},... | collective-permute-start | bytes 3145736 | tf_op jit(solution)/shard_map/ppermute | solution.py:245
  42.2 69.4 %collective-permute-start.12 = (bf16[256,2048]{1,0:T(8,128)(2,1)}, bf16[256,2048]{1,0:T(8,128)(2,1)}, u32[]{:S(2)}, u32[]{:S(2)}) collective-permute-start(bf16[256,2048]{1,0:T(8,128)(2,1)} %fusion.14), channel_id=1, source_target_pairs={{0,16},{16,0},{1,17},{17,1},{2,18},{18,2},{3,19},{19,3},{4,20},{20... | collective-permute-start | bytes 3145736 | tf_op jit(solution)/shard_map/ppermute | solution.py:245
  44.4 41.3 %all-to-all-start = ((bf16[32,2,128]{2,1,0:T(2,128)(2,1)}), bf16[32,2,128]{2,1,0:T(2,128)(2,1)S(1)}, u32[]{:S(2)}, u32[]{:S(2)}) async-start(bf16[32,2,128]{2,1,0:T(2,128)(2,1)} %reshape.621), calls=%async_computation | async-start | bytes 32768 | tf_op jit(solution)/shard_map/all_to_all | solution.py:358
  85.7 18.9 %all-to-all-start.3 = ((bf16[8,64,1024]{2,1,0:T(8,128)(2,1)}), bf16[8,64,1024]{2,1,0:T(8,128)(2,1)S(1)}, u32[]{:S(2)}, u32[]{:S(2)}) async-start(bf16[8,64,1024]{2,1,0:T(8,128)(2,1)} %pad_maximum_fusion.1), calls=%async_computation.3 | async-start | bytes 2097152 | tf_op jit(solution)/shard_map/all_to_all | solution.py:358
  89.2 165.8 %all-gather.9.cloned.1.call-start = ((), (), s32[]{:S(2)}) async-start(), calls=%async_computation.16 | async-start | bytes 5242880 | tf_op jit(solution)/shard_map/all_gather | solution.py:361
  92.1 25.2 %collective-permute-start.11 = (bf16[256,2048]{1,0:T(8,128)(2,1)}, bf16[256,2048]{1,0:T(8,128)(2,1)S(1)}, u32[]{:S(2)}, u32[]{:S(2)}) collective-permute-start(bf16[256,2048]{1,0:T(8,128)(2,1)} %collective-permute-done.10), channel_id=1, source_target_pairs={{0,1},{1,0},{2,3},{3,2},{4,5},{5,4},{6,7},{7,6},{8,9},{9,8},{10,11... | collective-permute-start | bytes 3145736 | tf_op jit(solution)/shard_map/ppermute | solution.py:245
  110.1 23.2 %collective-permute-start.15 = (bf16[128,2048]{1,0:T(8,128)(2,1)S(1)}, bf16[128,2048]{1,0:T(8,128)(2,1)S(1)}, u32[]{:S(2)}, u32[]{:S(2)}) collective-permute-start(bf16[128,2048]{1,0:T(8,128)(2,1)S(1)} %slice.123), channel_id=1, source_target_pairs={{0,16},{16,0},{1,17},{17,1},{2,18},{18,2},{3,19},{19,3},{4,20},{20... | collective-permute-start | bytes 1572872 | tf_op jit(solution)/shard_map/ppermute | solution.py:245
  111.6 22.3 %collective-permute-start.13 = (bf16[256,2048]{1,0:T(8,128)(2,1)}, bf16[256,2048]{1,0:T(8,128)(2,1)S(1)}, u32[]{:S(2)}, u32[]{:S(2)}) collective-permute-start(bf16[256,2048]{1,0:T(8,128)(2,1)} %collective-permute-done.12), channel_id=1, source_target_pairs={{0,1},{1,0},{2,3},{3,2},{4,5},{5,4},{6,7},{7,6},{8,9},{9,8},{10,11... | collective-permute-start | bytes 3145736 | tf_op jit(solution)/shard_map/ppermute | solution.py:245
  122.3 64.2 %collective-permute-start.4 = (bf16[256,2048]{1,0:T(8,128)(2,1)}, bf16[256,2048]{1,0:T(8,128)(2,1)}, u32[]{:S(2)}, u32[]{:S(2)}) collective-permute-start(bf16[256,2048]{1,0:T(8,128)(2,1)} %collective-permute-done.3.refs_0_), channel_id=1, source_target_pairs={{0,1},{1,0},{2,3},{3,2},{4,5},{5,4},{6,7},{7,6},{8,9},{9,8},{10,11... | collective-permute-start | bytes 3145736 | tf_op jit(solution)/shard_map/ppermute | solution.py:245
  123.3 33.0 %collective-permute-start.7 = (bf16[128,2048]{1,0:T(8,128)(2,1)}, bf16[128,2048]{1,0:T(8,128)(2,1)}, u32[]{:S(2)}, u32[]{:S(2)}) collective-permute-start(bf16[128,2048]{1,0:T(8,128)(2,1)} %collective-permute-done.5.refs_0_), channel_id=1, source_target_pairs={{0,1},{1,0},{2,3},{3,2},{4,5},{5,4},{6,7},{7,6},{8,9},{9,8},{10,11... | collective-permute-start | bytes 1572872 | tf_op jit(solution)/shard_map/ppermute | solution.py:245
  133.3 23.0 %collective-permute-start.8 = (bf16[128,2048]{1,0:T(8,128)(2,1)}, bf16[128,2048]{1,0:T(8,128)(2,1)}, u32[]{:S(2)}, u32[]{:S(2)}) collective-permute-start(bf16[128,2048]{1,0:T(8,128)(2,1)} %collective-permute-done.6.refs_1_), channel_id=1, source_target_pairs={{0,1},{1,0},{2,3},{3,2},{4,5},{5,4},{6,7},{7,6},{8,9},{9,8},{10,11... | collective-permute-start | bytes 1572872 | tf_op jit(solution)/shard_map/ppermute | solution.py:245
  156.1 156.5 %all-gather.11.cloned.1.call-start = ((), (), s32[]{:S(2)}) async-start(), calls=%async_computation.17 | async-start | bytes 2621440 | tf_op jit(solution)/shard_map/all_gather | solution.py:392
  198.5 19.0 %collective-permute-start.19 = (bf16[256,2048]{1,0:T(8,128)(2,1)}, bf16[256,2048]{1,0:T(8,128)(2,1)S(1)}, u32[]{:S(2)}, u32[]{:S(2)}) collective-permute-start(bf16[256,2048]{1,0:T(8,128)(2,1)} %get-tuple-element.149), channel_id=1, source_target_pairs={{0,1},{1,0},{2,3},{3,2},{4,5},{5,4},{6,7},{7,6},{8,9},{9,8},{10,11... | collective-permute-start | bytes 3145736 | tf_op jit(solution)/shard_map/ppermute | solution.py:245
  220.6 34.5 %collective-permute-start.24 = (bf16[256,2048]{1,0:T(8,128)(2,1)S(1)}, bf16[256,2048]{1,0:T(8,128)(2,1)}, u32[]{:S(2)}, u32[]{:S(2)}) collective-permute-start(bf16[256,2048]{1,0:T(8,128)(2,1)S(1)} %add_convert_fusion.12.refs_13_), channel_id=1, source_target_pairs={{0,8},{8,0},{1,9},{9,1},{2,10},{10,2},{3,11},{11,3},{4,12},{12,4},... | collective-permute-start | bytes 3145736 | tf_op jit(solution)/shard_map/ppermute | solution.py:245
  223.9 31.2 %collective-permute-start.25 = (bf16[256,2048]{1,0:T(8,128)(2,1)}, bf16[256,2048]{1,0:T(8,128)(2,1)}, u32[]{:S(2)}, u32[]{:S(2)}) collective-permute-start(bf16[256,2048]{1,0:T(8,128)(2,1)} %add_convert_fusion.11.refs_14_), channel_id=1, source_target_pairs={{0,16},{16,0},{1,17},{17,1},{2,18},{18,2},{3,19},{19,3},{4,20},{20... | collective-permute-start | bytes 3145736 | tf_op jit(solution)/shard_map/ppermute | solution.py:245
  236.6 18.5 %collective-permute-start.23 = (bf16[256,2048]{1,0:T(8,128)(2,1)}, bf16[256,2048]{1,0:T(8,128)(2,1)S(1)}, u32[]{:S(2)}, u32[]{:S(2)}) collective-permute-start(bf16[256,2048]{1,0:T(8,128)(2,1)} %get-tuple-element.155), channel_id=1, source_target_pairs={{0,1},{1,0},{2,3},{3,2},{4,5},{5,4},{6,7},{7,6},{8,9},{9,8},{10,11... | collective-permute-start | bytes 3145736 | tf_op jit(solution)/shard_map/ppermute | solution.py:245
  236.6 162.0 %reduce-scatter.6.cloned.1.call-start = ((), (), s32[]{:S(2)}) async-start(), calls=%async_computation.18 | async-start | bytes 2621440 | tf_op jit(solution)/shard_map/reduce_scatter | solution.py:475
  265.1 22.7 %collective-permute-start.31 = (bf16[128,2048]{1,0:T(8,128)(2,1)}, bf16[128,2048]{1,0:T(8,128)(2,1)S(1)}, u32[]{:S(2)}, u32[]{:S(2)}) collective-permute-start(bf16[128,2048]{1,0:T(8,128)(2,1)} %get-tuple-element.280), channel_id=1, source_target_pairs={{0,8},{8,0},{1,9},{9,1},{2,10},{10,2},{3,11},{11,3},{4,12},{12,4},... | collective-permute-start | bytes 1572872 | tf_op jit(solution)/shard_map/ppermute | solution.py:245
  265.7 23.4 %collective-permute-start.32 = (bf16[128,2048]{1,0:T(8,128)(2,1)}, bf16[128,2048]{1,0:T(8,128)(2,1)}, u32[]{:S(2)}, u32[]{:S(2)}) collective-permute-start(bf16[128,2048]{1,0:T(8,128)(2,1)} %get-tuple-element.281), channel_id=1, source_target_pairs={{0,16},{16,0},{1,17},{17,1},{2,18},{18,2},{3,19},{19,3},{4,20},{20... | collective-permute-start | bytes 1572872 | tf_op jit(solution)/shard_map/ppermute | solution.py:245
  340.5 141.6 %reduce-scatter.10.cloned.1.call-start = ((), (), s32[]{:S(2)}) async-start(), calls=%async_computation.20 | async-start | bytes 5242880 | tf_op jit(solution)/shard_map/reduce_scatter | solution.py:507
  370.6 28.0 %collective-permute-start.45 = (bf16[256,2048]{1,0:T(8,128)(2,1)S(1)}, bf16[256,2048]{1,0:T(8,128)(2,1)S(1)}, u32[]{:S(2)}, u32[]{:S(2)}) collective-permute-start(bf16[256,2048]{1,0:T(8,128)(2,1)S(1)} %add_convert_fusion.8.refs_8_), channel_id=1, source_target_pairs={{0,8},{8,0},{1,9},{9,1},{2,10},{10,2},{3,11},{11,3},{4,12},{12,4},... | collective-permute-start | bytes 3145736 | tf_op jit(solution)/shard_map/ppermute | solution.py:245
  373.2 25.3 %collective-permute-start.46 = (bf16[256,2048]{1,0:T(8,128)(2,1)S(1)}, bf16[256,2048]{1,0:T(8,128)(2,1)}, u32[]{:S(2)}, u32[]{:S(2)}) collective-permute-start(bf16[256,2048]{1,0:T(8,128)(2,1)S(1)} %add_convert_fusion.7.refs_9_), channel_id=1, source_target_pairs={{0,16},{16,0},{1,17},{17,1},{2,18},{18,2},{3,19},{19,3},{4,20},{20... | collective-permute-start | bytes 3145736 | tf_op jit(solution)/shard_map/ppermute | solution.py:245
  407.0 161.2 %reduce-scatter.12.cloned.1.call-start = ((), (), s32[]{:S(2)}) async-start(), calls=%async_computation.21 | async-start | bytes 2621440 | tf_op jit(solution)/shard_map/reduce_scatter | solution.py:507
  408.5 26.6 %collective-permute-start.48 = (bf16[128,2048]{1,0:T(8,128)(2,1)}, bf16[128,2048]{1,0:T(8,128)(2,1)}, u32[]{:S(2)}, u32[]{:S(2)}) collective-permute-start(bf16[128,2048]{1,0:T(8,128)(2,1)} %get-tuple-element.276), channel_id=1, source_target_pairs={{0,16},{16,0},{1,17},{17,1},{2,18},{18,2},{3,19},{19,3},{4,20},{20... | collective-permute-start | bytes 1572872 | tf_op jit(solution)/shard_map/ppermute | solution.py:245
  410.6 24.4 %collective-permute-start.47 = (bf16[128,2048]{1,0:T(8,128)(2,1)}, bf16[128,2048]{1,0:T(8,128)(2,1)}, u32[]{:S(2)}, u32[]{:S(2)}) collective-permute-start(bf16[128,2048]{1,0:T(8,128)(2,1)} %get-tuple-element.277), channel_id=1, source_target_pairs={{0,8},{8,0},{1,9},{9,1},{2,10},{10,2},{3,11},{11,3},{4,12},{12,4},... | collective-permute-start | bytes 1572872 | tf_op jit(solution)/shard_map/ppermute | solution.py:245
  411.5 22.9 %collective-permute-start.50 = (bf16[128,2048]{1,0:T(8,128)(2,1)}, bf16[128,2048]{1,0:T(8,128)(2,1)}, u32[]{:S(2)}, u32[]{:S(2)}) collective-permute-start(bf16[128,2048]{1,0:T(8,128)(2,1)} %get-tuple-element.277), channel_id=1, source_target_pairs={{0,16},{16,0},{1,17},{17,1},{2,18},{18,2},{3,19},{19,3},{4,20},{20... | collective-permute-start | bytes 1572872 | tf_op jit(solution)/shard_map/ppermute | solution.py:245
  492.1 121.8 %reduce-scatter.8.cloned.1.call-start = ((), (), s32[]{:S(2)}) async-start(), calls=%async_computation.19 | async-start | bytes 5242880 | tf_op jit(solution)/shard_map/reduce_scatter | solution.py:507
  529.2 26.3 %collective-permute-start.61 = (bf16[256,2048]{1,0:T(8,128)(2,1)}, bf16[256,2048]{1,0:T(8,128)(2,1)}, u32[]{:S(2)}, u32[]{:S(2)}) collective-permute-start(bf16[256,2048]{1,0:T(8,128)(2,1)} %add_convert_fusion.4.refs_2_), channel_id=1, source_target_pairs={{0,16},{16,0},{1,17},{17,1},{2,18},{18,2},{3,19},{19,3},{4,20},{20... | collective-permute-start | bytes 3145736 | tf_op jit(solution)/shard_map/ppermute | solution.py:245
  530.2 42.4 %collective-permute-start.59 = (bf16[256,2048]{1,0:T(8,128)(2,1)}, bf16[256,2048]{1,0:T(8,128)(2,1)}, u32[]{:S(2)}, u32[]{:S(2)}) collective-permute-start(bf16[256,2048]{1,0:T(8,128)(2,1)} %add_convert_fusion.5.refs_1_), channel_id=1, source_target_pairs={{0,8},{8,0},{1,9},{9,1},{2,10},{10,2},{3,11},{11,3},{4,12},{12,4},... | collective-permute-start | bytes 3145736 | tf_op jit(solution)/shard_map/ppermute | solution.py:245
  531.0 72.2 %collective-permute-start.73 = (bf16[256,2048]{1,0:T(8,128)(2,1)}, bf16[256,2048]{1,0:T(8,128)(2,1)}, u32[]{:S(2)}, u32[]{:S(2)}) collective-permute-start(bf16[256,2048]{1,0:T(8,128)(2,1)} %get-tuple-element.210.refs_8_.refs_2_), channel_id=1, source_target_pairs={{0,1},{1,0},{2,3},{3,2},{4,5},{5,4},{6,7},{7,6},{8,9},{9,8},{10,11... | collective-permute-start | bytes 3145736 | tf_op jit(solution)/shard_map/ppermute | solution.py:245
  531.0 37.2 %all-to-all-start.5 = ((bf16[8,64,1024]{2,1,0:T(8,128)(2,1)}), bf16[8,64,1024]{2,1,0:T(8,128)(2,1)}, u32[]{:S(2)}, u32[]{:S(2)}) async-start(bf16[8,64,1024]{2,1,0:T(8,128)(2,1)} %bitcast.48), calls=%async_computation.8 | async-start | bytes 2097152 | tf_op jit(solution)/shard_map/all_to_all | solution.py:358
  535.3 72.4 %collective-permute-start.78 = (bf16[256,2048]{1,0:T(8,128)(2,1)}, bf16[256,2048]{1,0:T(8,128)(2,1)}, u32[]{:S(2)}, u32[]{:S(2)}) collective-permute-start(bf16[256,2048]{1,0:T(8,128)(2,1)} %get-tuple-element.241), channel_id=1, source_target_pairs={{0,1},{1,0},{2,3},{3,2},{4,5},{5,4},{6,7},{7,6},{8,9},{9,8},{10,11... | collective-permute-start | bytes 3145736 | tf_op jit(solution)/shard_map/ppermute | solution.py:245
  538.5 39.6 %collective-permute-start.75 = (bf16[128,2048]{1,0:T(8,128)(2,1)}, bf16[128,2048]{1,0:T(8,128)(2,1)}, u32[]{:S(2)}, u32[]{:S(2)}) collective-permute-start(bf16[128,2048]{1,0:T(8,128)(2,1)} %get-tuple-element.272), channel_id=1, source_target_pairs={{0,16},{16,0},{1,17},{17,1},{2,18},{18,2},{3,19},{19,3},{4,20},{20... | collective-permute-start | bytes 1572872 | tf_op jit(solution)/shard_map/ppermute | solution.py:245
  555.5 24.1 %collective-permute-start.76 = (bf16[128,2048]{1,0:T(8,128)(2,1)}, bf16[128,2048]{1,0:T(8,128)(2,1)}, u32[]{:S(2)}, u32[]{:S(2)}) collective-permute-start(bf16[128,2048]{1,0:T(8,128)(2,1)} %get-tuple-element.271), channel_id=1, source_target_pairs={{0,8},{8,0},{1,9},{9,1},{2,10},{10,2},{3,11},{11,3},{4,12},{12,4},... | collective-permute-start | bytes 1572872 | tf_op jit(solution)/shard_map/ppermute | solution.py:245
  572.4 99.7 %reduce-scatter.14.cloned.1.call-start = ((), (), s32[]{:S(2)}) async-start(), calls=%async_computation.22 | async-start | bytes 2621440 | tf_op jit(solution)/shard_map/reduce_scatter | solution.py:573
  576.3 49.1 %collective-permute-start.62 = (bf16[256,2048]{1,0:T(8,128)(2,1)}, bf16[256,2048]{1,0:T(8,128)(2,1)}, u32[]{:S(2)}, u32[]{:S(2)}) collective-permute-start(bf16[256,2048]{1,0:T(8,128)(2,1)} %add_convert_fusion.3), channel_id=1, source_target_pairs={{0,8},{8,0},{1,9},{9,1},{2,10},{10,2},{3,11},{11,3},{4,12},{12,4},... | collective-permute-start | bytes 3145736 | tf_op jit(solution)/shard_map/ppermute | solution.py:245
  578.1 43.3 %collective-permute-start.63 = (bf16[256,2048]{1,0:T(8,128)(2,1)}, bf16[256,2048]{1,0:T(8,128)(2,1)}, u32[]{:S(2)}, u32[]{:S(2)}) collective-permute-start(bf16[256,2048]{1,0:T(8,128)(2,1)} %add_convert_fusion.3), channel_id=1, source_target_pairs={{0,16},{16,0},{1,17},{17,1},{2,18},{18,2},{3,19},{19,3},{4,20},{20... | collective-permute-start | bytes 3145736 | tf_op jit(solution)/shard_map/ppermute | solution.py:245
  607.3 26.2 %collective-permute-start.77 = (bf16[256,2048]{1,0:T(8,128)(2,1)}, bf16[256,2048]{1,0:T(8,128)(2,1)S(1)}, u32[]{:S(2)}, u32[]{:S(2)}) collective-permute-start(bf16[256,2048]{1,0:T(8,128)(2,1)} %add_convert_fusion.1), channel_id=1, source_target_pairs={{0,8},{8,0},{1,9},{9,1},{2,10},{10,2},{3,11},{11,3},{4,12},{12,4},... | collective-permute-start | bytes 3145736 | tf_op jit(solution)/shard_map/ppermute | solution.py:245
  610.7 29.2 %collective-permute-start.79 = (bf16[256,2048]{1,0:T(8,128)(2,1)}, bf16[256,2048]{1,0:T(8,128)(2,1)}, u32[]{:S(2)}, u32[]{:S(2)}) collective-permute-start(bf16[256,2048]{1,0:T(8,128)(2,1)} %add_convert_fusion), channel_id=1, source_target_pairs={{0,16},{16,0},{1,17},{17,1},{2,18},{18,2},{3,19},{19,3},{4,20},{20... | collective-permute-start | bytes 3145736 | tf_op jit(solution)/shard_map/ppermute | solution.py:245
  612.0 37.2 %collective-permute-start.72 = (bf16[256,2048]{1,0:T(8,128)(2,1)}, bf16[256,2048]{1,0:T(8,128)(2,1)}, u32[]{:S(2)}, u32[]{:S(2)}) collective-permute-start(bf16[256,2048]{1,0:T(8,128)(2,1)} %get-tuple-element.204.refs_2_), channel_id=1, source_target_pairs={{0,1},{1,0},{2,3},{3,2},{4,5},{5,4},{6,7},{7,6},{8,9},{9,8},{10,11... | collective-permute-start | bytes 3145736 | tf_op jit(solution)/shard_map/ppermute | solution.py:245
  613.9 34.2 %all-to-all-start.4 = ((bf16[8,64,1024]{2,1,0:T(8,128)(2,1)}), bf16[8,64,1024]{2,1,0:T(8,128)(2,1)S(1)}, u32[]{:S(2)}, u32[]{:S(2)}) async-start(bf16[8,64,1024]{2,1,0:T(8,128)(2,1)} %bitcast.168), calls=%async_computation.6 | async-start | bytes 2097152 | tf_op jit(solution)/shard_map/all_to_all | solution.py:358
  623.3 35.8 %collective-permute-start.64 = (bf16[128,2048]{1,0:T(8,128)(2,1)}, bf16[128,2048]{1,0:T(8,128)(2,1)}, u32[]{:S(2)}, u32[]{:S(2)}) collective-permute-start(bf16[128,2048]{1,0:T(8,128)(2,1)} %slice.136), channel_id=1, source_target_pairs={{0,8},{8,0},{1,9},{9,1},{2,10},{10,2},{3,11},{11,3},{4,12},{12,4},... | collective-permute-start | bytes 1572872 | tf_op jit(solution)/shard_map/ppermute | solution.py:245
  627.2 31.8 %collective-permute-start.65 = (bf16[128,2048]{1,0:T(8,128)(2,1)}, bf16[128,2048]{1,0:T(8,128)(2,1)}, u32[]{:S(2)}, u32[]{:S(2)}) collective-permute-start(bf16[128,2048]{1,0:T(8,128)(2,1)} %slice.137), channel_id=1, source_target_pairs={{0,16},{16,0},{1,17},{17,1},{2,18},{18,2},{3,19},{19,3},{4,20},{20... | collective-permute-start | bytes 1572872 | tf_op jit(solution)/shard_map/ppermute | solution.py:245
  (117 other events, 999.0 us)
Sparse Core Ops, SparseCore 0:
  9.6 48.7 all-gather.6
  59.9 114.0 all-gather.4
  176.1 78.9 all-gather.8
  256.5 44.1 all-gather.10
  340.7 41.8 reduce-scatter.5
  407.1 74.2 reduce-scatter.9
  492.2 43.3 reduce-scatter.11
  537.9 75.9 reduce-scatter.7
  616.2 44.1 reduce-scatter.13
